TPU v7x, 512 devices: a whole 4x4x16 slice. The times are simulated.
512 devices in a mesh: row: 16 (over z_lo, core), col: 32 (over x, y, z_hi).
Axes of the slice: x: 4, y: 4, z: 16 (z_hi: 2, z_lo: 8; z = z_hi * 8 + z_lo), core: 2. Of those that a mesh axis runs over, the one named last changes fastest.
Arguments:
- features: bfloat16 [65536, 256], P(('row', 'col')), may hold values from -6 to 6
- blocks: bfloat16 [512, 128, 128, 128], P('row', 'col'), may hold values from -0.046875 to 0.046875
- block_col: int32 [512, 128], P('row', 'col'), may hold values from 0 to 15
- row_count: int32 [512, 32], P('row', 'col'), may hold values from 0 to 4, as said below
- weight: bfloat16 [256, 256], replicated, may hold values from -0.375 to 0.375
- out_bias: float32 [256], replicated, may hold values from -4 to 4
Outputs:
- layer_out: bfloat16 [65536, 256], P(('row', 'col'))
Inputs may be any that keep to these rules, and one draw needn't show every extreme that they name: row_count[i, j] is how many of the 4 slots of block row i in column group j are in use; the others are ignored.
All inputs are finite; a program needn't handle non-finite values.
Results may differ from a plain program's by a relative error of at most 0.018.
Values may be sent and summed in bfloat16 or wider, within the bound.
No kernel may reach another device: no remote copies, remote signals or barrier semaphores. Data moves between devices by JAX's collectives and lax.ppermute only.
A program may use at most 64 MiB of HBM per device.

v0:
```python
import jax
import jax.numpy as jnp
from jax import lax
from jax.sharding import PartitionSpec as P


def local_terms(blocks, block_col, counts, stripe):
    slot_ids = jnp.arange(block_col.shape[1], dtype=jnp.int32)[None, :]
    live_slots = (slot_ids < counts).astype(stripe.dtype)
    picked = stripe[block_col] * live_slots[:, :, None, None]
    term_rows = jnp.einsum("ikab,ikbf->iaf", blocks, picked, preferred_element_type=jnp.float32)
    return term_rows.reshape(-1, stripe.shape[2])


def local(features, blocks, block_col, row_count, weight, out_bias):
    feat_width = features.shape[1]
    block_size = blocks.shape[2]
    gathered = lax.all_gather(features, "row", axis=0, tiled=True)
    stripe = gathered.reshape(-1, block_size, feat_width)
    partial_value = local_terms(blocks, block_col, row_count, stripe)
    summed = lax.psum_scatter(
        partial_value.astype(jnp.bfloat16), "col", scatter_dimension=0, tiled=True
    )
    hidden = jnp.dot(summed, weight, preferred_element_type=jnp.float32) + out_bias
    return jnp.maximum(hidden, 0.0).astype(jnp.bfloat16)


def solution(mesh):
    return jax.shard_map(
        local,
        mesh=mesh,
        in_specs=(
            P(("row", "col"), None),
            P("row", "col", None, None),
            P("row", "col"),
            P("row", "col"),
            P(),
            P(),
        ),
        out_specs=P(("row", "col"), None),
        check_vma=False,
    )
```

profile of v0, /device:TPU:96, one launch (start us, length us, event | category | flops | bytes accessed | tf_op | source)
XLA Modules:
  0.0 514.1 jit_solution(12059601364966467931)
XLA Ops:
  6.5 0.0 copy-start
  6.5 0.0 all-gather.2.cloned.1.call-start
  6.5 0.7 all-gather.2.cloned.1.call-update
  7.3 0.0 reduce-scatter.2.cloned.1.call-start
  7.3 0.7 compare_select_fusion
  8.0 0.1 copy.8
  8.1 0.1 reshape.32
  8.2 0.7 fusion.7
  8.9 78.4 %all-gather.2.cloned.1.call-done = bf16[2048,256]{1,0:T(8,128)(2,1)} async-done(((bf16[128,256]{1,0:T(8,128)(2,1)}), bf16[2048,256]{1,0:T(8,128)(2,1)}) %all-gather.2.cloned.1.call-update) | async-done | bytes 1048592 | tf_op jit(solution)/shard_map/all_gather | solution.py:18
  87.4 7.8 %gather_fusion = bf16[128,128,256]{2,1,0:T(8,128)(2,1)} fusion(bf16[16,128,256]{2,1,0:T(8,128)(2,1)} %bitcast.12, s32[1024]{0:T(1024)S(1)} %pad_clamp_fusion), kind=kCustom, calls=%fused_computation | custom fusion | bytes 16777728 | tf_op jit(solution)/shard_map/gather | solution.py:10
  95.2 0.0 copy-start.1
  95.2 7.9 %bitcast_convert_fusion = bf16[32,256,128]{1,2,0:T(8,128)(2,1)} fusion(bf16[32,4,128,128]{3,2,1,0:T(8,128)(2,1)} %param.7, bf16[32,4,128,256]{3,2,1,0:T(8,128)(2,1)} %bitcast.13, bf16[32,4]{1,0:T(8,128)(2,1)S(1)} %fusion.7), kind=kOutput, calls=%fused_computation.3 | convolution fusion | flops 1091567616 | bytes 14680320 | tf_op jit(solution)/shard_map/ikab,ikbf->iaf/dot_general | solution.py:11
  103.1 0.0 reduce-scatter.2.cloned.1.call-update
  103.1 402.6 %reduce-scatter.2.cloned.1.call-done = bf16[128,256]{1,0:T(8,128)(2,1)} async-done(((bf16[4096,256]{1,0:T(8,128)(2,1)}), bf16[128,256]{1,0:T(8,128)(2,1)}) %reduce-scatter.2.cloned.1.call-update) | async-done | bytes 65552 | tf_op jit(solution)/shard_map/reduce_scatter | solution.py:21
  505.7 0.0 copy-done
  505.7 0.0 copy-done.1
  505.7 1.6 fusion.6
  (1 shorter events, 0.0 us)
Async XLA Ops:
  6.5 499.1 %copy-start = (bf16[256,256]{1,0:T(8,128)(2,1)S(1)}, bf16[256,256]{1,0:T(8,128)(2,1)}, u32[]{:S(2)}) copy-start(bf16[256,256]{1,0:T(8,128)(2,1)} %param.10) | copy-start | bytes 393220
  6.5 80.8 %all-gather.2.cloned.1.call-start = ((), (), s32[]{:S(2)}) async-start(), calls=%async_computation.1 | async-start | bytes 1114112 | tf_op jit(solution)/shard_map/all_gather | solution.py:18
  7.3 498.4 %reduce-scatter.2.cloned.1.call-start = ((), (), s32[]{:S(2)}) async-start(), calls=%async_computation.2 | async-start | bytes 2162688 | tf_op jit(solution)/shard_map/reduce_scatter | solution.py:21
  95.2 410.5 %copy-start.1 = (f32[256]{0:T(256)S(1)}, f32[256]{0:T(256)}, u32[]{:S(2)}) copy-start(f32[256]{0:T(256)} %param.11) | copy-start | bytes 3076
Sparse Core Ops, SparseCore 0:
  9.4 77.8 all-gather.1
  103.2 402.3 reduce-scatter.1
where the time goes:
time: 515 us; the launch traced here: 514 us
  waiting for transfers between devices  482 us (94%)
  between operations  13.4 us (3%)
  matrix products  9.55 us (2%)
  local copies, waits for them, and re-layouts  7.99 us (2%)
    reduce_scatter x1, waiting for transfers between devices, local(): lax.psum_scatter(partial_value.astype(jnp.bfloat16), 'col', scatter_dimen...  403 us
    all_gather x1, waiting for transfers between devices, local(): gathered = lax.all_gather(features, 'row', axis=0, tiled=True)  78.4 us
  transfers between devices with their start and end apart: 2, of which 2 were waited for; matrix products, arithmetic and copies ran while one was open for 0% of the time, Pallas kernels for 0%

commit v1 on v0

v1 whole, which is shorter than its diff:
```python
import jax
import jax.numpy as jnp
from jax import lax
from jax.experimental import pallas as pl
from jax.experimental.pallas import tpu as pltpu
from jax.sharding import Mesh, PartitionSpec as P

ZL, CORE, X, Y, ZH = 8, 2, 4, 4, 2
SLOTS, BS, F = 4, 128, 256


def swap(value, axis, size, bit):
    return lax.ppermute(value, axis, [(i, i ^ bit) for i in range(size)])


def terms_kernel(me_ref, cols_ref, counts_ref, blocks_ref, stripe_ref, out_ref):
    rows = blocks_ref.shape[0]
    base = pl.program_id(0) * rows
    me = me_ref[0]
    for i in range(rows):
        count = counts_ref[base + i]
        lhs, rhs = [], []
        for k in range(SLOTS):
            offset = cols_ref[(base + i) * SLOTS + k] ^ me
            spot = (
                ((offset & 1) << 3)
                | ((offset & 2) << 1)
                | ((offset & 4) >> 1)
                | ((offset & 8) >> 3)
            )
            block = blocks_ref[i, k]
            lhs.append(jnp.where(k < count, block, jnp.zeros_like(block)))
            rhs.append(stripe_ref[spot])
        term = jnp.dot(
            jnp.concatenate(lhs, axis=1),
            jnp.concatenate(rhs, axis=0),
            preferred_element_type=jnp.float32,
        )
        out_ref[i] = term.astype(jnp.bfloat16)


def terms(me, cols, counts, blocks, stripe):
    rows = blocks.shape[0]
    step = 8
    return pl.pallas_call(
        terms_kernel,
        grid_spec=pltpu.PrefetchScalarGridSpec(
            num_scalar_prefetch=3,
            grid=(rows // step,),
            in_specs=[
                pl.BlockSpec((step, SLOTS, BS, BS), lambda i, *_: (i, 0, 0, 0)),
                pl.BlockSpec((16, BS, F), lambda i, *_: (0, 0, 0)),
            ],
            out_specs=pl.BlockSpec((step, BS, F), lambda i, *_: (i, 0, 0)),
        ),
        out_shape=jax.ShapeDtypeStruct((rows, BS, F), jnp.bfloat16),
        compiler_params=pltpu.CompilerParams(vmem_limit_bytes=12 << 20),
        cost_estimate=pl.CostEstimate(
            flops=2 * rows * SLOTS * BS * BS * F, bytes_accessed=8 << 20, transcendentals=0
        ),
        name="terms",
    )(me, cols, counts, blocks, stripe)


def sum_kernel(zh_ref, parts_ref, own_ref, send_ref):
    zh = zh_ref[0]

    def total(which):
        acc = parts_ref[0, which].astype(jnp.float32)
        for i in range(1, parts_ref.shape[0]):
            acc = acc + parts_ref[i, which].astype(jnp.float32)
        return acc

    own_ref[...] = total(zh)
    send_ref[...] = total(1 - zh).astype(jnp.bfloat16)


def partial_sums(zh, parts):
    return pl.pallas_call(
        sum_kernel,
        in_specs=[
            pl.BlockSpec(memory_space=pltpu.SMEM),
            pl.BlockSpec(memory_space=pltpu.VMEM),
        ],
        out_specs=[pl.BlockSpec(memory_space=pltpu.VMEM)] * 2,
        out_shape=[
            jax.ShapeDtypeStruct((BS, F), jnp.float32),
            jax.ShapeDtypeStruct((BS, F), jnp.bfloat16),
        ],
        compiler_params=pltpu.CompilerParams(vmem_limit_bytes=8 << 20),
        name="partial_sums",
    )(zh, parts)


def finish_kernel(own_ref, other_ref, weight_ref, bias_ref, out_ref):
    summed = own_ref[...] + other_ref[...].astype(jnp.float32)
    hidden = jnp.dot(
        summed.astype(jnp.bfloat16),
        weight_ref[...],
        preferred_element_type=jnp.float32,
    )
    out_ref[...] = jnp.maximum(hidden + bias_ref[...], 0.0).astype(jnp.bfloat16)


def finish(own, other, weight, bias):
    return pl.pallas_call(
        finish_kernel,
        in_specs=[pl.BlockSpec(memory_space=pltpu.VMEM)] * 4,
        out_specs=pl.BlockSpec(memory_space=pltpu.VMEM),
        out_shape=jax.ShapeDtypeStruct((BS, F), jnp.bfloat16),
        compiler_params=pltpu.CompilerParams(vmem_limit_bytes=4 << 20),
        name="finish",
    )(own, other, weight, bias)


def local(features, blocks, block_col, row_count, weight, out_bias):
    me = (lax.axis_index("zl") * CORE + lax.axis_index("core")).astype(jnp.int32)
    zh = lax.axis_index("zh").astype(jnp.int32)
    held = features[None]
    for axis, size, bit in (("zl", ZL, 4), ("zl", ZL, 2), ("zl", ZL, 1), ("core", CORE, 1)):
        held = jnp.concatenate([held, swap(held, axis, size, bit)], axis=0)
    value = terms(
        me[None], block_col.reshape(-1), row_count.reshape(-1), blocks, held
    )
    parts = lax.all_to_all(
        value.reshape(X * Y, ZH, BS, F), ("x", "y"), 0, 0
    )
    own, send = partial_sums(zh[None], parts)
    other = swap(send, "zh", ZH, 1)
    return finish(own, other, weight, out_bias[None])


def solution(mesh):
    fine = Mesh(
        mesh.devices.reshape(ZL, CORE, X, Y, ZH), ("zl", "core", "x", "y", "zh")
    )
    row, col = ("zl", "core"), ("x", "y", "zh")
    return jax.shard_map(
        local,
        mesh=fine,
        in_specs=(
            P(row + col, None),
            P(row, col, None, None),
            P(row, col),
            P(row, col),
            P(),
            P(),
        ),
        out_specs=P(row + col, None),
        check_vma=False,
    )
```

time: 515 us -> 104 us (0.20)
  the two profiles are of different devices: /device:TPU:96 before, /device:TPU:1 now
where the time goes in v1:
time: 104 us; the launch traced here: 103 us
  starting transfers between devices  50.2 us (48%)
  waiting for transfers between devices  41.6 us (40%)
  local copies, waits for them, and re-layouts  5.31 us (5%)
  Pallas kernels  3.56 us (3%)
  other arithmetic  2.61 us (3%)
    ppermute x5, starting transfers between devices, swap(): return lax.ppermute(value, axis, [(i, i ^ bit) for i in range(size)])  43.4 us
    all_to_all x1, waiting for transfers between devices, local(): parts = lax.all_to_all(value.reshape(X * Y, ZH, BS, F), ('x', 'y'), 0, 0)  29.2 us
    ppermute x5, waiting for transfers between devices, swap(): return lax.ppermute(value, axis, [(i, i ^ bit) for i in range(size)])  12.4 us
    all_to_all x1, starting transfers between devices, local(): parts = lax.all_to_all(value.reshape(X * Y, ZH, BS, F), ('x', 'y'), 0, 0)  6.75 us
    unnamed x15, local copies, waits for them, and re-layouts  5.17 us
    concatenate x3, other arithmetic, local(): held = jnp.concatenate([held, swap(held, axis, size, bit)], axis=0)  2.61 us
    pallas_call x1, Pallas kernels, terms(): pl.pallas_call(terms_kernel, grid_spec=pltpu.PrefetchScalarGridSpec(num_s...  2.49 us
  transfers between devices with their start and end apart: 6, of which 6 were waited for; matrix products, arithmetic and copies ran while one was open for 2% of the time, Pallas kernels for 0%

profile of v1, /device:TPU:1, one launch (start us, length us, event | category | flops | bytes accessed | tf_op | source)
XLA Modules:
  0.0 103.4 jit_solution(3632502225909756152)
XLA Ops:
  0.0 9.8 %collective-permute-start = (bf16[1,128,256]{2,1,0:T(8,128)(2,1)}, bf16[1,128,256]{2,1,0:T(8,128)(2,1)S(1)}, u32[]{:S(2)}, u32[]{:S(2)}) collective-permute-start(bf16[1,128,256]{2,1,0:T(8,128)(2,1)} %bitcast.10), channel_id=1, source_target_pairs={{0,256},{64,320},{128,384},{192,448},{256,0},{320,64},{384,128},{4... | collective-permute-start | bytes 196616 | tf_op jit(solution)/shard_map/ppermute | solution.py:13
  9.8 1.9 %collective-permute-done = bf16[1,128,256]{2,1,0:T(8,128)(2,1)S(1)} collective-permute-done((bf16[1,128,256]{2,1,0:T(8,128)(2,1)}, bf16[1,128,256]{2,1,0:T(8,128)(2,1)S(1)}, u32[]{:S(2)}, u32[]{:S(2)}) %collective-permute-start) | collective-permute-done | bytes 65568 | tf_op jit(solution)/shard_map/ppermute | solution.py:13
  11.6 0.9 pad_maximum_fusion.2
  12.5 7.1 %collective-permute-start.1 = (bf16[2,128,256]{2,1,0:T(8,128)(2,1)S(1)}, bf16[2,128,256]{2,1,0:T(8,128)(2,1)S(1)}, u32[]{:S(2)}, u32[]{:S(2)}) collective-permute-start(bf16[2,128,256]{2,1,0:T(8,128)(2,1)S(1)} %pad_maximum_fusion.2), channel_id=1, source_target_pairs={{0,128},{64,192},{128,0},{192,64},{256,384},{320,448},{384,256},{4... | collective-permute-start | bytes 393224 | tf_op jit(solution)/shard_map/ppermute | solution.py:13
  19.6 2.3 %collective-permute-done.1 = bf16[2,128,256]{2,1,0:T(8,128)(2,1)S(1)} collective-permute-done((bf16[2,128,256]{2,1,0:T(8,128)(2,1)S(1)}, bf16[2,128,256]{2,1,0:T(8,128)(2,1)S(1)}, u32[]{:S(2)}, u32[]{:S(2)}) %collective-permute-start.1) | collective-permute-done | bytes 131104 | tf_op jit(solution)/shard_map/ppermute | solution.py:13
  21.9 0.9 pad_maximum_fusion.1
  22.8 6.8 %collective-permute-start.2 = (bf16[4,128,256]{2,1,0:T(8,128)(2,1)S(1)}, bf16[4,128,256]{2,1,0:T(8,128)(2,1)S(1)}, u32[]{:S(2)}, u32[]{:S(2)}) collective-permute-start(bf16[4,128,256]{2,1,0:T(8,128)(2,1)S(1)} %pad_maximum_fusion.1), channel_id=1, source_target_pairs={{0,64},{64,0},{128,192},{192,128},{256,320},{320,256},{384,448},{4... | collective-permute-start | bytes 786440 | tf_op jit(solution)/shard_map/ppermute | solution.py:13
  29.6 0.8 copy.8
  30.3 0.1 reshape.9.cols_ref
  30.5 4.3 %collective-permute-done.2 = bf16[4,128,256]{2,1,0:T(8,128)(2,1)S(1)} collective-permute-done((bf16[4,128,256]{2,1,0:T(8,128)(2,1)S(1)}, bf16[4,128,256]{2,1,0:T(8,128)(2,1)S(1)}, u32[]{:S(2)}, u32[]{:S(2)}) %collective-permute-start.2) | collective-permute-done | bytes 262176 | tf_op jit(solution)/shard_map/ppermute | solution.py:13
  34.7 0.9 pad_maximum_fusion
  35.6 4.0 %collective-permute-start.3 = (bf16[8,128,256]{2,1,0:T(8,128)(2,1)S(1)}, bf16[8,128,256]{2,1,0:T(8,128)(2,1)S(1)}, u32[]{:S(2)}, u32[]{:S(2)}) collective-permute-start(bf16[8,128,256]{2,1,0:T(8,128)(2,1)S(1)} %pad_maximum_fusion), channel_id=1, source_target_pairs={{0,32},{32,0},{1,33},{33,1},{2,34},{34,2},{3,35},{35,3},{4,36},{36... | collective-permute-start | bytes 1572872 | tf_op jit(solution)/shard_map/ppermute | solution.py:13
  39.6 0.8 constant_dynamic-update-slice_fusion.4
  40.5 0.6 collective-permute-done.3
  41.2 0.0 copy-start.1
  41.2 2.2 %copy-done.1 = bf16[32,4,128,128]{3,2,1,0:T(8,128)(2,1)S(1)} copy-done((bf16[32,4,128,128]{3,2,1,0:T(8,128)(2,1)S(1)}, bf16[32,4,128,128]{3,2,1,0:T(8,128)(2,1)}, u32[]{:S(2)}) %copy-start.1) | copy-done | bytes 4194328
  43.4 2.5 %terms.1 = bf16[32,128,256]{2,1,0:T(8,128)(2,1)S(1)} custom-call(s32[1]{0:T(128)} %bitcast.1.me_ref, s32[128]{0:T(128)S(1)} %reshape.9.cols_ref, s32[32]{0:T(128)S(1)} %bitcast.9, bf16[32,4,128,128]{3,2,1,0:T(8,128)(2,1)S(1)} %copy-done.1, bf16[16,128,256]{2,1,0:T(8,128)(2,1)S(1)} %constant_dynamic-update-slice_fusion.stripe_ref), custom_call_target="tpu_custom_call" | custom-call | flops 1073741824 | bytes 8388608 | tf_op jit(solution)/shard_map/terms/pallas_call | solution.py:45
  45.9 1.3 %copy-done = bf16[32,128,256]{2,1,0:T(8,128)(2,1)} copy-done((bf16[32,128,256]{2,1,0:T(8,128)(2,1)}, bf16[32,128,256]{2,1,0:T(8,128)(2,1)S(1)}, u32[]{:S(2)}) %copy-start) | copy-done | bytes 2097176
  47.2 6.8 %all-to-all-start = ((bf16[16,2,128,256]{3,2,1,0:T(8,128)(2,1)}), bf16[16,2,128,256]{3,2,1,0:T(8,128)(2,1)S(1)}, u32[]{:S(2)}, u32[]{:S(2)}) async-start(bf16[16,2,128,256]{3,2,1,0:T(8,128)(2,1)} %bitcast.7), calls=%async_computation | async-start | bytes 4194304 | tf_op jit(solution)/shard_map/all_to_all | solution.py:125
  54.0 29.2 %all-to-all-done.parts_ref = bf16[16,2,128,256]{3,2,1,0:T(8,128)(2,1)S(1)} async-done(((bf16[16,2,128,256]{3,2,1,0:T(8,128)(2,1)}), bf16[16,2,128,256]{3,2,1,0:T(8,128)(2,1)S(1)}, u32[]{:S(2)}, u32[]{:S(2)}) %all-to-all-start) | async-done | bytes 2097184 | tf_op jit(solution)/shard_map/all_to_all | solution.py:125
  83.2 0.3 partial_sums.1
  83.5 15.8 %collective-permute-start.4 = (bf16[128,256]{1,0:T(8,128)(2,1)S(1)}, bf16[128,256]{1,0:T(8,128)(2,1)S(1)}, u32[]{:S(2)}, u32[]{:S(2)}) collective-permute-start(bf16[128,256]{1,0:T(8,128)(2,1)S(1)} %get-tuple-element.8), channel_id=1, source_target_pairs={{0,1},{1,0},{2,3},{3,2},{4,5},{5,4},{6,7},{7,6},{8,9},{9,8},{10,11... | collective-permute-start | bytes 196616 | tf_op jit(solution)/shard_map/ppermute | solution.py:13
  99.3 3.3 %collective-permute-done.4.other_ref = bf16[128,256]{1,0:T(8,128)(2,1)S(1)} collective-permute-done((bf16[128,256]{1,0:T(8,128)(2,1)S(1)}, bf16[128,256]{1,0:T(8,128)(2,1)S(1)}, u32[]{:S(2)}, u32[]{:S(2)}) %collective-permute-start.4) | collective-permute-done | bytes 65568 | tf_op jit(solution)/shard_map/ppermute | solution.py:13
  102.6 0.8 finish.1
  (11 shorter events, 0.1 us)
Async XLA Ops:
  0.0 41.2 %copy-start.4 = (s32[32,1]{0,1:T(1,128)S(1)}, s32[32,1]{0,1:T(1,128)}, u32[]{:S(2)}) copy-start(s32[32,1]{0,1:T(1,128)} %param.9) | copy-start | bytes 388
  0.0 11.6 %collective-permute-start = (bf16[1,128,256]{2,1,0:T(8,128)(2,1)}, bf16[1,128,256]{2,1,0:T(8,128)(2,1)S(1)}, u32[]{:S(2)}, u32[]{:S(2)}) collective-permute-start(bf16[1,128,256]{2,1,0:T(8,128)(2,1)} %bitcast.10), channel_id=1, source_target_pairs={{0,256},{64,320},{128,384},{192,448},{256,0},{320,64},{384,128},{4... | collective-permute-start | bytes 196616 | tf_op jit(solution)/shard_map/ppermute | solution.py:13
  12.5 9.4 %collective-permute-start.1 = (bf16[2,128,256]{2,1,0:T(8,128)(2,1)S(1)}, bf16[2,128,256]{2,1,0:T(8,128)(2,1)S(1)}, u32[]{:S(2)}, u32[]{:S(2)}) collective-permute-start(bf16[2,128,256]{2,1,0:T(8,128)(2,1)S(1)} %pad_maximum_fusion.2), channel_id=1, source_target_pairs={{0,128},{64,192},{128,0},{192,64},{256,384},{320,448},{384,256},{4... | collective-permute-start | bytes 393224 | tf_op jit(solution)/shard_map/ppermute | solution.py:13
  22.8 11.9 %collective-permute-start.2 = (bf16[4,128,256]{2,1,0:T(8,128)(2,1)S(1)}, bf16[4,128,256]{2,1,0:T(8,128)(2,1)S(1)}, u32[]{:S(2)}, u32[]{:S(2)}) collective-permute-start(bf16[4,128,256]{2,1,0:T(8,128)(2,1)S(1)} %pad_maximum_fusion.1), channel_id=1, source_target_pairs={{0,64},{64,0},{128,192},{192,128},{256,320},{320,256},{384,448},{4... | collective-permute-start | bytes 786440 | tf_op jit(solution)/shard_map/ppermute | solution.py:13
  35.6 5.5 %collective-permute-start.3 = (bf16[8,128,256]{2,1,0:T(8,128)(2,1)S(1)}, bf16[8,128,256]{2,1,0:T(8,128)(2,1)S(1)}, u32[]{:S(2)}, u32[]{:S(2)}) collective-permute-start(bf16[8,128,256]{2,1,0:T(8,128)(2,1)S(1)} %pad_maximum_fusion), channel_id=1, source_target_pairs={{0,32},{32,0},{1,33},{33,1},{2,34},{34,2},{3,35},{35,3},{4,36},{36... | collective-permute-start | bytes 1572872 | tf_op jit(solution)/shard_map/ppermute | solution.py:13
  41.2 2.2 %copy-start.1 = (bf16[32,4,128,128]{3,2,1,0:T(8,128)(2,1)S(1)}, bf16[32,4,128,128]{3,2,1,0:T(8,128)(2,1)}, u32[]{:S(2)}) copy-start(bf16[32,4,128,128]{3,2,1,0:T(8,128)(2,1)} %blocks_ref.1) | copy-start | bytes 12582916
  45.9 1.3 %copy-start = (bf16[32,128,256]{2,1,0:T(8,128)(2,1)}, bf16[32,128,256]{2,1,0:T(8,128)(2,1)S(1)}, u32[]{:S(2)}) copy-start(bf16[32,128,256]{2,1,0:T(8,128)(2,1)S(1)} %terms.1) | copy-start | bytes 6291460
  47.2 36.0 %all-to-all-start = ((bf16[16,2,128,256]{3,2,1,0:T(8,128)(2,1)}), bf16[16,2,128,256]{3,2,1,0:T(8,128)(2,1)S(1)}, u32[]{:S(2)}, u32[]{:S(2)}) async-start(bf16[16,2,128,256]{3,2,1,0:T(8,128)(2,1)} %bitcast.7), calls=%async_computation | async-start | bytes 4194304 | tf_op jit(solution)/shard_map/all_to_all | solution.py:125
  54.0 48.6 %copy-start.2 = (bf16[256,256]{1,0:T(8,128)(2,1)S(1)}, bf16[256,256]{1,0:T(8,128)(2,1)}, u32[]{:S(2)}) copy-start(bf16[256,256]{1,0:T(8,128)(2,1)} %weight_ref.1) | copy-start | bytes 393220
  54.0 48.6 %copy-start.3 = (f32[256]{0:T(256)S(1)}, f32[256]{0:T(256)}, u32[]{:S(2)}) copy-start(f32[256]{0:T(256)} %param.11) | copy-start | bytes 3076
  83.5 19.1 %collective-permute-start.4 = (bf16[128,256]{1,0:T(8,128)(2,1)S(1)}, bf16[128,256]{1,0:T(8,128)(2,1)S(1)}, u32[]{:S(2)}, u32[]{:S(2)}) collective-permute-start(bf16[128,256]{1,0:T(8,128)(2,1)S(1)} %get-tuple-element.8), channel_id=1, source_target_pairs={{0,1},{1,0},{2,3},{3,2},{4,5},{5,4},{6,7},{7,6},{8,9},{9,8},{10,11... | collective-permute-start | bytes 196616 | tf_op jit(solution)/shard_map/ppermute | solution.py:13

commit v2 on v0

v2 whole, which is shorter than its diff:
```python
import jax
import jax.numpy as jnp
from jax import lax
from jax.experimental import pallas as pl
from jax.experimental.pallas import tpu as pltpu
from jax.sharding import Mesh, PartitionSpec as P

ZL, CORE, X, Y, ZH = 8, 2, 4, 4, 2
SLOTS, BS, F = 4, 128, 256
VMEM = pl.BlockSpec(memory_space=pltpu.VMEM)
SMEM = pl.BlockSpec(memory_space=pltpu.SMEM)


def swap(value, axis, size, bit):
    return lax.ppermute(value, axis, [(i, i ^ bit) for i in range(size)])


def whole(kernel, ins, out_shape, name, cost, limit=4 << 20):
    return pl.pallas_call(
        kernel,
        in_specs=[SMEM if a.dtype == jnp.int32 else VMEM for a in ins],
        out_specs=jax.tree.map(lambda _: VMEM, out_shape),
        out_shape=out_shape,
        compiler_params=pltpu.CompilerParams(vmem_limit_bytes=limit),
        cost_estimate=pl.CostEstimate(
            flops=cost[0], bytes_accessed=cost[1], transcendentals=0
        ),
        name=name,
    )(*ins)


def side_by_side(counts_ref, row, block_of):
    count = counts_ref[0, row]
    lhs = []
    for k in range(SLOTS):
        block = block_of(k)
        lhs.append(jnp.where(k < count, block, jnp.zeros_like(block)))
    return jnp.concatenate(lhs, axis=1)


def product(place_ref, cols_ref, row, lhs, stripe_ref):
    rhs = [stripe_ref[cols_ref[k, row] ^ place_ref[0]] for k in range(SLOTS)]
    term = jnp.dot(
        lhs, jnp.concatenate(rhs, axis=0), preferred_element_type=jnp.float32
    )
    return term.astype(jnp.bfloat16)


def lhs_kernel(place_ref, counts_ref, blocks_ref, out_ref):
    step = blocks_ref.shape[0]
    base = pl.program_id(0) * step
    half = 1 - place_ref[1]
    for i in range(step):
        out_ref[i] = side_by_side(
            counts_ref, 2 * (base + i) + half, lambda k: blocks_ref[i, 0, k]
        )


def near_kernel(place_ref, counts_ref, cols_ref, blocks_ref, stripe_ref, out_ref):
    step = blocks_ref.shape[0]
    base = pl.program_id(0) * step
    for i in range(step):
        row = 2 * (base + i) + place_ref[1]
        lhs = side_by_side(counts_ref, row, lambda k: blocks_ref[i, 0, k])
        out_ref[i] = product(place_ref, cols_ref, row, lhs, stripe_ref)


def on_blocks(kernel, scalars, blocks, more, width, far, name, cost):
    step = 4

    def pick(i, place_ref, *_):
        return (i, 1 - place_ref[1] if far else place_ref[1], 0, 0, 0)

    return pl.pallas_call(
        kernel,
        grid_spec=pltpu.PrefetchScalarGridSpec(
            num_scalar_prefetch=len(scalars),
            grid=(X * Y // step,),
            in_specs=[pl.BlockSpec((step, 1, SLOTS, BS, BS), pick)]
            + [VMEM for _ in more],
            out_specs=pl.BlockSpec((step, BS, width), lambda i, *_: (i, 0, 0)),
        ),
        out_shape=jax.ShapeDtypeStruct((X * Y, BS, width), jnp.bfloat16),
        compiler_params=pltpu.CompilerParams(vmem_limit_bytes=8 << 20),
        cost_estimate=pl.CostEstimate(
            flops=cost[0], bytes_accessed=cost[1], transcendentals=0
        ),
        name=name,
    )(*scalars, pltpu.with_memory_space_constraint(blocks, pltpu.HBM), *more)


def far_kernel(place_ref, cols_ref, lhs_ref, *refs):
    p0, p1, p2, p4, p53, p6, p7, far0, far1, stripe_ref, out_ref = refs
    near = (p0, p1, p2, p53.at[1], p4, p53.at[0], p6, p7)
    across = [far0.at[i] for i in range(4)] + [far1.at[i] for i in range(4)]
    for offset in range(ZL):
        stripe_ref[2 * offset] = near[offset][...]
        stripe_ref[2 * offset + 1] = across[(0, 1, 2, 4, 5, 3, 6, 7).index(offset)][...]
    for j in range(out_ref.shape[0]):
        row = 2 * j + 1 - place_ref[1]
        out_ref[j] = product(place_ref, cols_ref, row, lhs_ref[j], stripe_ref)


def total(parts_ref):
    acc = parts_ref[0].astype(jnp.float32)
    for i in range(1, parts_ref.shape[0]):
        acc = acc + parts_ref[i].astype(jnp.float32)
    return acc


def send_kernel(parts_ref, out_ref):
    out_ref[...] = total(parts_ref).astype(jnp.bfloat16)


def finish_kernel(parts_ref, other_ref, weight_ref, bias_ref, out_ref):
    summed = total(parts_ref) + other_ref[...].astype(jnp.float32)
    hidden = jnp.dot(
        summed.astype(jnp.bfloat16),
        weight_ref[...],
        preferred_element_type=jnp.float32,
    )
    out_ref[...] = jnp.maximum(hidden + bias_ref[...], 0.0).astype(jnp.bfloat16)


def local(features, blocks, block_col, row_count, weight, out_bias):
    bf16 = jnp.bfloat16
    place = jnp.stack(
        [lax.axis_index("zl") * CORE + lax.axis_index("core"), lax.axis_index("zh")]
    ).astype(jnp.int32)
    cols, counts = block_col.T, row_count.T
    blocks = blocks.reshape(X * Y, ZH, SLOTS, BS, BS)
    far_lhs = on_blocks(
        lhs_kernel, [place, counts], blocks, [], SLOTS * BS, True, "far_lhs", (0, 4 << 20)
    )
    p = {0: features}
    p[4] = swap(p[0], "zl", ZL, 4)
    p[2] = swap(p[0], "zl", ZL, 2)
    p[1] = swap(p[0], "zl", ZL, 1)
    p[6] = swap(p[4], "zl", ZL, 2)
    p53 = swap(jnp.stack([p[4], p[2]]), "zl", ZL, 1)
    p[6], far_lhs = lax.optimization_barrier((p[6], far_lhs))
    p[7] = swap(p[6], "zl", ZL, 1)
    far0 = swap(jnp.stack([p[0], p[1], p[2], p[4]]), "core", CORE, 1)
    far1 = swap(
        jnp.concatenate([p53, p[6][None], p[7][None]], axis=0), "core", CORE, 1
    )
    half = jax.ShapeDtypeStruct((X * Y, BS, F), bf16)
    work = (2 * X * Y * SLOTS * BS * BS * F, 4 << 20)
    stripe, far_terms = whole(
        far_kernel,
        [place, cols, far_lhs, p[0], p[1], p[2], p[4], p53, p[6], p[7], far0, far1],
        [half, half],
        "far_terms",
        work,
    )
    near_terms = on_blocks(
        near_kernel, [place, counts, cols], blocks, [stripe], F, False, "near_terms", work
    )
    far_parts = lax.all_to_all(far_terms, ("x", "y"), 0, 0)
    near_parts = lax.all_to_all(near_terms, ("x", "y"), 0, 0)
    out = jax.ShapeDtypeStruct((BS, F), bf16)
    send = whole(send_kernel, [far_parts], out, "send", (0, 1 << 20))
    other = swap(send, "zh", ZH, 1)
    return whole(
        finish_kernel,
        [near_parts, other, weight, out_bias[None]],
        out,
        "finish",
        (2 * BS * F * F, 2 << 20),
    )


def solution(mesh):
    fine = Mesh(
        mesh.devices.reshape(ZL, CORE, X, Y, ZH), ("zl", "core", "x", "y", "zh")
    )
    row, col = ("zl", "core"), ("x", "y", "zh")
    return jax.shard_map(
        local,
        mesh=fine,
        in_specs=(
            P(row + col, None),
            P(row, col, None, None),
            P(row, col),
            P(row, col),
            P(),
            P(),
        ),
        out_specs=P(row + col, None),
        check_vma=False,
    )
```

time: 515 us -> 89.6 us (0.17)
  the two profiles are of different devices: /device:TPU:96 before, /device:TPU:62 now
where the time goes in v2:
time: 89.6 us; the launch traced here: 88.9 us
  starting transfers between devices  55.6 us (62%)
  waiting for transfers between devices  21 us (23%)
  Pallas kernels  11.2 us (12%)
    ppermute x9, starting transfers between devices, swap(): return lax.ppermute(value, axis, [(i, i ^ bit) for i in range(size)])  40.2 us
    ppermute x9, waiting for transfers between devices, swap(): return lax.ppermute(value, axis, [(i, i ^ bit) for i in range(size)])  12.4 us
    all_to_all x1, waiting for transfers between devices, local(): far_parts = lax.all_to_all(far_terms, ('x', 'y'), 0, 0)  8.62 us
    all_to_all x1, starting transfers between devices, local(): near_parts = lax.all_to_all(near_terms, ('x', 'y'), 0, 0)  8.3 us
    pallas_call x2, Pallas kernels, on_blocks(): pl.pallas_call(kernel, grid_spec=pltpu.PrefetchScalarGridSpec(num_scalar_...  7.83 us
    all_to_all x1, starting transfers between devices, local(): far_parts = lax.all_to_all(far_terms, ('x', 'y'), 0, 0)  7.09 us
    pallas_call x3, Pallas kernels, whole(): pl.pallas_call(kernel, in_specs=[SMEM if a.dtype == jnp.int32 else VMEM f...  3.39 us
  transfers between devices with their start and end apart: 11, of which 6 were waited for; matrix products, arithmetic and copies ran while one was open for 0% of the time, Pallas kernels for 9%

profile of v2, /device:TPU:62, one launch (start us, length us, event | category | flops | bytes accessed | tf_op | source)
XLA Modules:
  0.0 88.9 jit_solution(8507942241872233464)
XLA Ops:
  0.0 5.3 %collective-permute-start.3 = (bf16[128,256]{1,0:T(8,128)(2,1)}, bf16[128,256]{1,0:T(8,128)(2,1)S(1)}, u32[]{:S(2)}, u32[]{:S(2)}) collective-permute-start(bf16[128,256]{1,0:T(8,128)(2,1)} %refs_0_.1), channel_id=1, source_target_pairs={{0,128},{64,192},{128,0},{192,64},{256,384},{320,448},{384,256},{4... | collective-permute-start | bytes 196616 | tf_op jit(solution)/shard_map/ppermute | solution.py:15
  5.3 9.1 %collective-permute-start = (bf16[128,256]{1,0:T(8,128)(2,1)}, bf16[128,256]{1,0:T(8,128)(2,1)S(1)}, u32[]{:S(2)}, u32[]{:S(2)}) collective-permute-start(bf16[128,256]{1,0:T(8,128)(2,1)} %refs_0_.1), channel_id=1, source_target_pairs={{0,256},{64,320},{128,384},{192,448},{256,0},{320,64},{384,128},{4... | collective-permute-start | bytes 196616 | tf_op jit(solution)/shard_map/ppermute | solution.py:15
  14.4 2.0 %collective-permute-start.2 = (bf16[128,256]{1,0:T(8,128)(2,1)}, bf16[128,256]{1,0:T(8,128)(2,1)S(1)}, u32[]{:S(2)}, u32[]{:S(2)}) collective-permute-start(bf16[128,256]{1,0:T(8,128)(2,1)} %refs_0_.1), channel_id=1, source_target_pairs={{0,64},{64,0},{128,192},{192,128},{256,320},{320,256},{384,448},{4... | collective-permute-start | bytes 196616 | tf_op jit(solution)/shard_map/ppermute | solution.py:15
  16.5 2.4 %collective-permute-done.refs_3_ = bf16[128,256]{1,0:T(8,128)(2,1)S(1)} collective-permute-done((bf16[128,256]{1,0:T(8,128)(2,1)}, bf16[128,256]{1,0:T(8,128)(2,1)S(1)}, u32[]{:S(2)}, u32[]{:S(2)}) %collective-permute-start) | collective-permute-done | bytes 65568 | tf_op jit(solution)/shard_map/ppermute | solution.py:15
  18.9 4.0 %collective-permute-start.4 = (bf16[2,128,256]{2,1,0:T(8,128)(2,1)S(1)}, bf16[2,128,256]{2,1,0:T(8,128)(2,1)S(1)}, u32[]{:S(2)}, u32[]{:S(2)}) collective-permute-start(bf16[2,128,256]{2,1,0:T(8,128)(2,1)S(1)} %pad_maximum_fusion.2), channel_id=1, source_target_pairs={{0,64},{64,0},{128,192},{192,128},{256,320},{320,256},{384,448},{4... | collective-permute-start | bytes 393224 | tf_op jit(solution)/shard_map/ppermute | solution.py:15
  22.9 1.9 %collective-permute-start.1 = (bf16[128,256]{1,0:T(8,128)(2,1)S(1)}, bf16[128,256]{1,0:T(8,128)(2,1)S(1)}, u32[]{:S(2)}, u32[]{:S(2)}) collective-permute-start(bf16[128,256]{1,0:T(8,128)(2,1)S(1)} %collective-permute-done.refs_3_), channel_id=1, source_target_pairs={{0,128},{64,192},{128,0},{192,64},{256,384},{320,448},{384,256},{4... | collective-permute-start | bytes 196616 | tf_op jit(solution)/shard_map/ppermute | solution.py:15
  24.9 0.1 pad_add_fusion.place_ref
  25.0 0.7 copy-done.3
  25.6 3.1 %far_lhs.1.lhs_ref = bf16[16,128,512]{2,1,0:T(8,128)(2,1)S(1)} custom-call(s32[2]{0:T(128)S(1)} %pad_add_fusion.place_ref, s32[1,32]{1,0:T(1,128)S(1)} %bitcast.22, bf16[16,2,4,128,128]{4,3,2,1,0:T(8,128)(2,1)} %bitcast.25), custom_call_target="tpu_custom_call" | custom-call | bytes 4194304 | tf_op jit(solution)/shard_map/far_lhs/pallas_call | solution.py:74
  28.7 1.3 %collective-permute-done.1.refs_5_ = bf16[128,256]{1,0:T(8,128)(2,1)S(1)} collective-permute-done((bf16[128,256]{1,0:T(8,128)(2,1)S(1)}, bf16[128,256]{1,0:T(8,128)(2,1)S(1)}, u32[]{:S(2)}, u32[]{:S(2)}) %collective-permute-start.1) | collective-permute-done | bytes 65568 | tf_op jit(solution)/shard_map/ppermute | solution.py:15
  30.0 1.9 %collective-permute-start.5 = (bf16[128,256]{1,0:T(8,128)(2,1)S(1)}, bf16[128,256]{1,0:T(8,128)(2,1)S(1)}, u32[]{:S(2)}, u32[]{:S(2)}) collective-permute-start(bf16[128,256]{1,0:T(8,128)(2,1)S(1)} %collective-permute-done.1.refs_5_), channel_id=1, source_target_pairs={{0,64},{64,0},{128,192},{192,128},{256,320},{320,256},{384,448},{4... | collective-permute-start | bytes 196616 | tf_op jit(solution)/shard_map/ppermute | solution.py:15
  32.0 1.9 %collective-permute-start.6 = (bf16[4,128,256]{2,1,0:T(8,128)(2,1)S(1)}, bf16[4,128,256]{2,1,0:T(8,128)(2,1)S(1)}, u32[]{:S(2)}, u32[]{:S(2)}) collective-permute-start(bf16[4,128,256]{2,1,0:T(8,128)(2,1)S(1)} %pad_maximum_fusion), channel_id=1, source_target_pairs={{0,32},{32,0},{1,33},{33,1},{2,34},{34,2},{3,35},{35,3},{4,36},{36... | collective-permute-start | bytes 786440 | tf_op jit(solution)/shard_map/ppermute | solution.py:15
  33.9 2.2 %collective-permute-done.5.refs_6_ = bf16[128,256]{1,0:T(8,128)(2,1)S(1)} collective-permute-done((bf16[128,256]{1,0:T(8,128)(2,1)S(1)}, bf16[128,256]{1,0:T(8,128)(2,1)S(1)}, u32[]{:S(2)}, u32[]{:S(2)}) %collective-permute-start.5) | collective-permute-done | bytes 65568 | tf_op jit(solution)/shard_map/ppermute | solution.py:15
  36.2 1.9 %collective-permute-start.7 = (bf16[4,128,256]{2,1,0:T(8,128)(2,1)S(1)}, bf16[4,128,256]{2,1,0:T(8,128)(2,1)S(1)}, u32[]{:S(2)}, u32[]{:S(2)}) collective-permute-start(bf16[4,128,256]{2,1,0:T(8,128)(2,1)S(1)} %pad_maximum_fusion.1), channel_id=1, source_target_pairs={{0,32},{32,0},{1,33},{33,1},{2,34},{34,2},{3,35},{35,3},{4,36},{36... | collective-permute-start | bytes 786440 | tf_op jit(solution)/shard_map/ppermute | solution.py:15
  38.1 1.5 %collective-permute-done.7.refs_8_ = bf16[4,128,256]{2,1,0:T(8,128)(2,1)S(1)} collective-permute-done((bf16[4,128,256]{2,1,0:T(8,128)(2,1)S(1)}, bf16[4,128,256]{2,1,0:T(8,128)(2,1)S(1)}, u32[]{:S(2)}, u32[]{:S(2)}) %collective-permute-start.7) | collective-permute-done | bytes 262176 | tf_op jit(solution)/shard_map/ppermute | solution.py:15
  39.6 2.3 %far_terms.1 = (bf16[16,128,256]{2,1,0:T(8,128)(2,1)S(1)}, bf16[16,128,256]{2,1,0:T(8,128)(2,1)}) custom-call(s32[2]{0:T(128)S(1)} %pad_add_fusion.place_ref, s32[4,32]{1,0:T(4,128)S(1)} %bitcast.20, bf16[16,128,512]{2,1,0:T(8,128)(2,1)S(1)} %far_lhs.1.lhs_ref, bf16[128,256]{1,0:T(8,128)(2,1)S(1)} %copy-done, ...), custom_call_target="tpu_custom_call" | custom-call | flops 536870912 | bytes 4194304 | tf_op jit(solution)/shard_map/far_terms/pallas_call | solution.py:19
  42.0 7.1 %all-to-all-start.1 = ((bf16[16,128,256]{2,1,0:T(8,128)(2,1)}), bf16[16,128,256]{2,1,0:T(8,128)(2,1)S(1)}, u32[]{:S(2)}, u32[]{:S(2)}) async-start(bf16[16,128,256]{2,1,0:T(8,128)(2,1)} %get-tuple-element.12), calls=%async_computation.1 | async-start | bytes 2097152 | tf_op jit(solution)/shard_map/all_to_all | solution.py:159
  49.1 4.8 %near_terms.1 = bf16[16,128,256]{2,1,0:T(8,128)(2,1)} custom-call(s32[2]{0:T(128)S(1)} %pad_add_fusion.place_ref, s32[1,32]{1,0:T(1,128)S(1)} %bitcast.23, s32[4,32]{1,0:T(4,128)S(1)} %bitcast.21, bf16[16,2,4,128,128]{4,3,2,1,0:T(8,128)(2,1)} %bitcast.26, bf16[16,128,256]{2,1,0:T(8,128)(2,1)S(1)} %get-tuple-element.11.stripe_ref), custom_call_target="tpu_custom_call" | custom-call | flops 536870912 | bytes 4194304 | tf_op jit(solution)/shard_map/near_terms/pallas_call | solution.py:74
  53.9 8.6 %all-to-all-done.1.parts_ref = bf16[16,128,256]{2,1,0:T(8,128)(2,1)S(1)} async-done(((bf16[16,128,256]{2,1,0:T(8,128)(2,1)}), bf16[16,128,256]{2,1,0:T(8,128)(2,1)S(1)}, u32[]{:S(2)}, u32[]{:S(2)}) %all-to-all-start.1) | async-done | bytes 1048608 | tf_op jit(solution)/shard_map/all_to_all | solution.py:159
  62.5 8.3 %all-to-all-start = ((bf16[16,128,256]{2,1,0:T(8,128)(2,1)}), bf16[16,128,256]{2,1,0:T(8,128)(2,1)S(1)}, u32[]{:S(2)}, u32[]{:S(2)}) async-start(bf16[16,128,256]{2,1,0:T(8,128)(2,1)} %near_terms.1), calls=%async_computation | async-start | bytes 2097152 | tf_op jit(solution)/shard_map/all_to_all | solution.py:160
  70.8 0.1 send.1
  70.9 12.1 %collective-permute-start.8 = (bf16[128,256]{1,0:T(8,128)(2,1)S(1)}, bf16[128,256]{1,0:T(8,128)(2,1)S(1)}, u32[]{:S(2)}, u32[]{:S(2)}) collective-permute-start(bf16[128,256]{1,0:T(8,128)(2,1)S(1)} %send.1), channel_id=1, source_target_pairs={{0,1},{1,0},{2,3},{3,2},{4,5},{5,4},{6,7},{7,6},{8,9},{9,8},{10,11... | collective-permute-start | bytes 196616 | tf_op jit(solution)/shard_map/ppermute | solution.py:15
  83.1 5.0 %collective-permute-done.8.other_ref = bf16[128,256]{1,0:T(8,128)(2,1)S(1)} collective-permute-done((bf16[128,256]{1,0:T(8,128)(2,1)S(1)}, bf16[128,256]{1,0:T(8,128)(2,1)S(1)}, u32[]{:S(2)}, u32[]{:S(2)}) %collective-permute-start.8) | collective-permute-done | bytes 65568 | tf_op jit(solution)/shard_map/ppermute | solution.py:15
  88.0 0.9 %finish.1 = bf16[128,256]{1,0:T(8,128)(2,1)} custom-call(bf16[16,128,256]{2,1,0:T(8,128)(2,1)S(1)} %all-to-all-done.parts_ref, bf16[128,256]{1,0:T(8,128)(2,1)S(1)} %collective-permute-done.8.other_ref, bf16[256,256]{1,0:T(8,128)(2,1)S(1)} %copy-done.1, f32[1,256]{1,0:T(1,128)S(1)} %bitcast.24), custom_call_target="tpu_custom_call" | custom-call | flops 16777216 | bytes 2097152 | tf_op jit(solution)/shard_map/finish/pallas_call | solution.py:19
  (19 shorter events, 0.1 us)
Async XLA Ops:
  0.0 31.9 %copy-start = (bf16[128,256]{1,0:T(8,128)(2,1)S(1)}, bf16[128,256]{1,0:T(8,128)(2,1)}, u32[]{:S(2)}) copy-start(bf16[128,256]{1,0:T(8,128)(2,1)} %refs_0_.1) | copy-start | bytes 196612
  0.0 39.6 %copy-start.2 = (s32[32,4]{0,1:T(4,128)S(1)}, s32[32,4]{0,1:T(4,128)}, u32[]{:S(2)}) copy-start(s32[32,4]{0,1:T(4,128)} %param.8) | copy-start | bytes 1540
  0.0 16.4 %collective-permute-start.3 = (bf16[128,256]{1,0:T(8,128)(2,1)}, bf16[128,256]{1,0:T(8,128)(2,1)S(1)}, u32[]{:S(2)}, u32[]{:S(2)}) collective-permute-start(bf16[128,256]{1,0:T(8,128)(2,1)} %refs_0_.1), channel_id=1, source_target_pairs={{0,128},{64,192},{128,0},{192,64},{256,384},{320,448},{384,256},{4... | collective-permute-start | bytes 196616 | tf_op jit(solution)/shard_map/ppermute | solution.py:15
  5.3 13.6 %collective-permute-start = (bf16[128,256]{1,0:T(8,128)(2,1)}, bf16[128,256]{1,0:T(8,128)(2,1)S(1)}, u32[]{:S(2)}, u32[]{:S(2)}) collective-permute-start(bf16[128,256]{1,0:T(8,128)(2,1)} %refs_0_.1), channel_id=1, source_target_pairs={{0,256},{64,320},{128,384},{192,448},{256,0},{320,64},{384,128},{4... | collective-permute-start | bytes 196616 | tf_op jit(solution)/shard_map/ppermute | solution.py:15
  14.4 17.5 %collective-permute-start.2 = (bf16[128,256]{1,0:T(8,128)(2,1)}, bf16[128,256]{1,0:T(8,128)(2,1)S(1)}, u32[]{:S(2)}, u32[]{:S(2)}) collective-permute-start(bf16[128,256]{1,0:T(8,128)(2,1)} %refs_0_.1), channel_id=1, source_target_pairs={{0,64},{64,0},{128,192},{192,128},{256,320},{320,256},{384,448},{4... | collective-permute-start | bytes 196616 | tf_op jit(solution)/shard_map/ppermute | solution.py:15
  18.9 15.0 %collective-permute-start.4 = (bf16[2,128,256]{2,1,0:T(8,128)(2,1)S(1)}, bf16[2,128,256]{2,1,0:T(8,128)(2,1)S(1)}, u32[]{:S(2)}, u32[]{:S(2)}) collective-permute-start(bf16[2,128,256]{2,1,0:T(8,128)(2,1)S(1)} %pad_maximum_fusion.2), channel_id=1, source_target_pairs={{0,64},{64,0},{128,192},{192,128},{256,320},{320,256},{384,448},{4... | collective-permute-start | bytes 393224 | tf_op jit(solution)/shard_map/ppermute | solution.py:15
  22.9 7.1 %collective-permute-start.1 = (bf16[128,256]{1,0:T(8,128)(2,1)S(1)}, bf16[128,256]{1,0:T(8,128)(2,1)S(1)}, u32[]{:S(2)}, u32[]{:S(2)}) collective-permute-start(bf16[128,256]{1,0:T(8,128)(2,1)S(1)} %collective-permute-done.refs_3_), channel_id=1, source_target_pairs={{0,128},{64,192},{128,0},{192,64},{256,384},{320,448},{384,256},{4... | collective-permute-start | bytes 196616 | tf_op jit(solution)/shard_map/ppermute | solution.py:15
  24.9 0.7 copy-start.3
  28.7 20.4 %copy-start.4 = (s32[32,1]{0,1:T(1,128)S(1)}, s32[32,1]{0,1:T(1,128)}, u32[]{:S(2)}) copy-start(s32[32,1]{0,1:T(1,128)} %param.9) | copy-start | bytes 388
  30.0 6.1 %collective-permute-start.5 = (bf16[128,256]{1,0:T(8,128)(2,1)S(1)}, bf16[128,256]{1,0:T(8,128)(2,1)S(1)}, u32[]{:S(2)}, u32[]{:S(2)}) collective-permute-start(bf16[128,256]{1,0:T(8,128)(2,1)S(1)} %collective-permute-done.1.refs_5_), channel_id=1, source_target_pairs={{0,64},{64,0},{128,192},{192,128},{256,320},{320,256},{384,448},{4... | collective-permute-start | bytes 196616 | tf_op jit(solution)/shard_map/ppermute | solution.py:15
  32.0 6.1 %collective-permute-start.6 = (bf16[4,128,256]{2,1,0:T(8,128)(2,1)S(1)}, bf16[4,128,256]{2,1,0:T(8,128)(2,1)S(1)}, u32[]{:S(2)}, u32[]{:S(2)}) collective-permute-start(bf16[4,128,256]{2,1,0:T(8,128)(2,1)S(1)} %pad_maximum_fusion), channel_id=1, source_target_pairs={{0,32},{32,0},{1,33},{33,1},{2,34},{34,2},{3,35},{35,3},{4,36},{36... | collective-permute-start | bytes 786440 | tf_op jit(solution)/shard_map/ppermute | solution.py:15
  36.2 3.4 %collective-permute-start.7 = (bf16[4,128,256]{2,1,0:T(8,128)(2,1)S(1)}, bf16[4,128,256]{2,1,0:T(8,128)(2,1)S(1)}, u32[]{:S(2)}, u32[]{:S(2)}) collective-permute-start(bf16[4,128,256]{2,1,0:T(8,128)(2,1)S(1)} %pad_maximum_fusion.1), channel_id=1, source_target_pairs={{0,32},{32,0},{1,33},{33,1},{2,34},{34,2},{3,35},{35,3},{4,36},{36... | collective-permute-start | bytes 786440 | tf_op jit(solution)/shard_map/ppermute | solution.py:15
  42.0 20.5 %all-to-all-start.1 = ((bf16[16,128,256]{2,1,0:T(8,128)(2,1)}), bf16[16,128,256]{2,1,0:T(8,128)(2,1)S(1)}, u32[]{:S(2)}, u32[]{:S(2)}) async-start(bf16[16,128,256]{2,1,0:T(8,128)(2,1)} %get-tuple-element.12), calls=%async_computation.1 | async-start | bytes 2097152 | tf_op jit(solution)/shard_map/all_to_all | solution.py:159
  49.1 39.0 %copy-start.1 = (bf16[256,256]{1,0:T(8,128)(2,1)S(1)}, bf16[256,256]{1,0:T(8,128)(2,1)}, u32[]{:S(2)}) copy-start(bf16[256,256]{1,0:T(8,128)(2,1)} %weight_ref.1) | copy-start | bytes 393220
  49.1 38.9 %copy-start.5 = (f32[256]{0:T(256)S(1)}, f32[256]{0:T(256)}, u32[]{:S(2)}) copy-start(f32[256]{0:T(256)} %param.11) | copy-start | bytes 3076
  62.5 20.6 %all-to-all-start = ((bf16[16,128,256]{2,1,0:T(8,128)(2,1)}), bf16[16,128,256]{2,1,0:T(8,128)(2,1)S(1)}, u32[]{:S(2)}, u32[]{:S(2)}) async-start(bf16[16,128,256]{2,1,0:T(8,128)(2,1)} %near_terms.1), calls=%async_computation | async-start | bytes 2097152 | tf_op jit(solution)/shard_map/all_to_all | solution.py:160
  70.9 17.1 %collective-permute-start.8 = (bf16[128,256]{1,0:T(8,128)(2,1)S(1)}, bf16[128,256]{1,0:T(8,128)(2,1)S(1)}, u32[]{:S(2)}, u32[]{:S(2)}) collective-permute-start(bf16[128,256]{1,0:T(8,128)(2,1)S(1)} %send.1), channel_id=1, source_target_pairs={{0,1},{1,0},{2,3},{3,2},{4,5},{5,4},{6,7},{7,6},{8,9},{9,8},{10,11... | collective-permute-start | bytes 196616 | tf_op jit(solution)/shard_map/ppermute | solution.py:15

commit v3 on v2

v3 whole, which is shorter than its diff:
```python
import jax
import jax.numpy as jnp
from jax import lax
from jax.experimental import pallas as pl
from jax.experimental.pallas import tpu as pltpu
from jax.sharding import Mesh, PartitionSpec as P

ZL, CORE, X, Y, ZH = 8, 2, 4, 4, 2
SLOTS, BS, F = 4, 128, 256
VMEM = pl.BlockSpec(memory_space=pltpu.VMEM)
SMEM = pl.BlockSpec(memory_space=pltpu.SMEM)


def swap(value, axis, size, bit):
    return lax.ppermute(value, axis, [(i, i ^ bit) for i in range(size)])


def whole(kernel, ins, out_shape, name, cost, limit=4 << 20):
    return pl.pallas_call(
        kernel,
        in_specs=[SMEM if a.dtype == jnp.int32 else VMEM for a in ins],
        out_specs=jax.tree.map(lambda _: VMEM, out_shape),
        out_shape=out_shape,
        compiler_params=pltpu.CompilerParams(vmem_limit_bytes=limit),
        cost_estimate=pl.CostEstimate(
            flops=cost[0], bytes_accessed=cost[1], transcendentals=0
        ),
        name=name,
    )(*ins)


def side_by_side(table_ref, row, block_of):
    count = table_ref[SLOTS, row]
    lhs = []
    for k in range(SLOTS):
        block = block_of(k)
        lhs.append(jnp.where(k < count, block, jnp.zeros_like(block)))
    return jnp.concatenate(lhs, axis=1)


def product(table_ref, row, lhs, stripe_ref):
    rhs = [stripe_ref[table_ref[k, row]] for k in range(SLOTS)]
    term = jnp.dot(
        lhs, jnp.concatenate(rhs, axis=0), preferred_element_type=jnp.float32
    )
    return term.astype(jnp.bfloat16)


def near_kernel(table_ref, blocks_ref, stripe_ref, out_ref):
    step = blocks_ref.shape[0]
    base = pl.program_id(0) * step
    for i in range(step):
        row = 2 * (base + i) + table_ref[SLOTS + 1, 0]
        lhs = side_by_side(table_ref, row, lambda k: blocks_ref[i, 0, k])
        out_ref[i] = product(table_ref, row, lhs, stripe_ref)


def near_half(table, blocks, stripe, cost):
    step = 4

    def pick(i, table_ref):
        return (i, table_ref[SLOTS + 1, 0], 0, 0, 0)

    return pl.pallas_call(
        near_kernel,
        grid_spec=pltpu.PrefetchScalarGridSpec(
            num_scalar_prefetch=1,
            grid=(X * Y // step,),
            in_specs=[pl.BlockSpec((step, 1, SLOTS, BS, BS), pick), VMEM],
            out_specs=pl.BlockSpec((step, BS, F), lambda i, *_: (i, 0, 0)),
        ),
        out_shape=jax.ShapeDtypeStruct((X * Y, BS, F), jnp.bfloat16),
        compiler_params=pltpu.CompilerParams(vmem_limit_bytes=8 << 20),
        cost_estimate=pl.CostEstimate(
            flops=cost[0], bytes_accessed=cost[1], transcendentals=0
        ),
        name="near_terms",
    )(table, pltpu.with_memory_space_constraint(blocks, pltpu.HBM), stripe)


def far_kernel(table_ref, blocks_ref, *refs):
    trio, p6, ones, p7, core0, core1 = refs[:6]
    stripe_ref, out_ref, held, made, in_sem, out_sem = refs[6:]
    half = 1 - table_ref[SLOTS + 1, 0]
    rows = X * Y
    loads = [
        pltpu.make_async_copy(blocks_ref.at[j, half], held.at[j], in_sem.at[j])
        for j in range(rows)
    ]
    stores = [
        pltpu.make_async_copy(made.at[j], out_ref.at[j], out_sem.at[j])
        for j in range(rows)
    ]
    for load in loads:
        load.start()
    near = (
        trio.at[0],
        ones.at[0],
        trio.at[2],
        ones.at[2],
        trio.at[1],
        ones.at[1],
        p6,
        p7,
    )
    across = [core0.at[i] for i in range(4)] + [core1.at[i] for i in range(4)]
    order = (0, 4, 2, 6, 1, 5, 3, 7)
    for offset in range(ZL):
        stripe_ref[2 * offset] = near[offset][...]
        stripe_ref[2 * offset + 1] = across[order.index(offset)][...]
    for j in range(rows):
        row = 2 * j + half
        loads[j].wait()
        lhs = side_by_side(table_ref, row, lambda k: held[j, k])
        made[j] = product(table_ref, row, lhs, stripe_ref)
        stores[j].start()
    for store in stores:
        store.wait()


def far_half(table, blocks, pieces, cost):
    half = (X * Y, BS, F)
    return pl.pallas_call(
        far_kernel,
        in_specs=[SMEM, pl.BlockSpec(memory_space=pl.ANY)] + [VMEM] * len(pieces),
        out_specs=[VMEM, pl.BlockSpec(memory_space=pl.ANY)],
        out_shape=[jax.ShapeDtypeStruct(half, jnp.bfloat16)] * 2,
        scratch_shapes=[
            pltpu.VMEM((X * Y, SLOTS, BS, BS), jnp.bfloat16),
            pltpu.VMEM(half, jnp.bfloat16),
            pltpu.SemaphoreType.DMA((X * Y,)),
            pltpu.SemaphoreType.DMA((X * Y,)),
        ],
        compiler_params=pltpu.CompilerParams(vmem_limit_bytes=10 << 20),
        cost_estimate=pl.CostEstimate(
            flops=cost[0], bytes_accessed=cost[1], transcendentals=0
        ),
        name="far_terms",
    )(table, pltpu.with_memory_space_constraint(blocks, pltpu.HBM), *pieces)


def total(parts_ref):
    acc = parts_ref[0].astype(jnp.float32)
    for i in range(1, parts_ref.shape[0]):
        acc = acc + parts_ref[i].astype(jnp.float32)
    return acc


def send_kernel(parts_ref, out_ref):
    out_ref[...] = total(parts_ref).astype(jnp.bfloat16)


def finish_kernel(parts_ref, other_ref, weight_ref, bias_ref, out_ref):
    summed = total(parts_ref) + other_ref[...].astype(jnp.float32)
    hidden = jnp.dot(
        summed.astype(jnp.bfloat16),
        weight_ref[...],
        preferred_element_type=jnp.float32,
    )
    out_ref[...] = jnp.maximum(hidden + bias_ref[...], 0.0).astype(jnp.bfloat16)


def local(features, blocks, block_col, row_count, weight, out_bias):
    bf16 = jnp.bfloat16
    me = (lax.axis_index("zl") * CORE + lax.axis_index("core")).astype(jnp.int32)
    zh = lax.axis_index("zh").astype(jnp.int32)
    table = jnp.concatenate(
        [block_col.T ^ me, row_count.T, jnp.full_like(row_count.T, zh)], axis=0
    )
    blocks = blocks.reshape(X * Y, ZH, SLOTS, BS, BS)
    p = {0: features}
    p[4] = swap(p[0], "zl", ZL, 4)
    p[2] = swap(p[0], "zl", ZL, 2)
    p[4], table = lax.optimization_barrier((p[4], table))
    p[6] = swap(p[4], "zl", ZL, 2)
    trio = jnp.stack([p[0], p[4], p[2]])
    ones = swap(trio, "zl", ZL, 1)
    p[7] = swap(p[6], "zl", ZL, 1)
    core0 = swap(jnp.concatenate([trio, p[6][None]], axis=0), "core", CORE, 1)
    core1 = swap(jnp.concatenate([ones, p[7][None]], axis=0), "core", CORE, 1)
    work = (2 * X * Y * SLOTS * BS * BS * F, 4 << 20)
    stripe, far_terms = far_half(
        table,
        blocks,
        [trio, p[6], ones, p[7], core0, core1],
        work,
    )
    near_terms = near_half(table, blocks, stripe, work)
    far_parts = lax.all_to_all(far_terms, ("x", "y"), 0, 0)
    near_parts = lax.all_to_all(near_terms, ("x", "y"), 0, 0)
    out = jax.ShapeDtypeStruct((BS, F), bf16)
    send = whole(send_kernel, [far_parts], out, "send", (0, 1 << 20))
    other = swap(send, "zh", ZH, 1)
    return whole(
        finish_kernel,
        [near_parts, other, weight, out_bias[None]],
        out,
        "finish",
        (2 * BS * F * F, 2 << 20),
    )


def solution(mesh):
    fine = Mesh(
        mesh.devices.reshape(ZL, CORE, X, Y, ZH), ("zl", "core", "x", "y", "zh")
    )
    row, col = ("zl", "core"), ("x", "y", "zh")
    return jax.shard_map(
        local,
        mesh=fine,
        in_specs=(
            P(row + col, None),
            P(row, col, None, None),
            P(row, col),
            P(row, col),
            P(),
            P(),
        ),
        out_specs=P(row + col, None),
        check_vma=False,
    )
```

time: 89.6 us -> 90.4 us (level)
  the two profiles are of different devices: /device:TPU:62 before, /device:TPU:4 now
where the time goes in v3:
time: 90.4 us; the launch traced here: 89.7 us
  starting transfers between devices  54.5 us (60%)
  waiting for transfers between devices  20 us (22%)
  Pallas kernels  11.9 us (13%)
  other arithmetic  3.17 us (4%)
    ppermute x8, starting transfers between devices, swap(): return lax.ppermute(value, axis, [(i, i ^ bit) for i in range(size)])  40.8 us
    all_to_all x1, waiting for transfers between devices, local(): far_parts = lax.all_to_all(far_terms, ('x', 'y'), 0, 0)  10.9 us
    all_to_all x1, starting transfers between devices, local(): far_parts = lax.all_to_all(far_terms, ('x', 'y'), 0, 0)  7.46 us
    ppermute x8, waiting for transfers between devices, swap(): return lax.ppermute(value, axis, [(i, i ^ bit) for i in range(size)])  7.09 us
    all_to_all x1, starting transfers between devices, local(): near_parts = lax.all_to_all(near_terms, ('x', 'y'), 0, 0)  6.16 us
    pallas_call x1, Pallas kernels, far_half(): pl.pallas_call(far_kernel, in_specs=[SMEM, pl.BlockSpec(memory_space=pl.A...  5.98 us
    pallas_call x1, Pallas kernels, near_half(): pl.pallas_call(near_kernel, grid_spec=pltpu.PrefetchScalarGridSpec(num_sc...  4.82 us
    all_to_all x1, waiting for transfers between devices, local(): near_parts = lax.all_to_all(near_terms, ('x', 'y'), 0, 0)  1.97 us
  transfers between devices with their start and end apart: 10, of which 7 were waited for; matrix products, arithmetic and copies ran while one was open for 3% of the time, Pallas kernels for 5%

profile of v3, /device:TPU:4, one launch (start us, length us, event | category | flops | bytes accessed | tf_op | source)
XLA Modules:
  0.0 89.7 jit_solution(17168180846818554591)
XLA Ops:
  0.0 9.1 %collective-permute-start = (bf16[128,256]{1,0:T(8,128)(2,1)}, bf16[128,256]{1,0:T(8,128)(2,1)S(1)}, u32[]{:S(2)}, u32[]{:S(2)}) collective-permute-start(bf16[128,256]{1,0:T(8,128)(2,1)} %param.6), channel_id=1, source_target_pairs={{0,256},{64,320},{128,384},{192,448},{256,0},{320,64},{384,128},{4... | collective-permute-start | bytes 196616 | tf_op jit(solution)/shard_map/ppermute | solution.py:15
  9.1 5.2 %collective-permute-start.1 = (bf16[128,256]{1,0:T(8,128)(2,1)}, bf16[128,256]{1,0:T(8,128)(2,1)S(1)}, u32[]{:S(2)}, u32[]{:S(2)}) collective-permute-start(bf16[128,256]{1,0:T(8,128)(2,1)} %param.6), channel_id=1, source_target_pairs={{0,128},{64,192},{128,0},{192,64},{256,384},{320,448},{384,256},{4... | collective-permute-start | bytes 196616 | tf_op jit(solution)/shard_map/ppermute | solution.py:15
  14.4 0.7 xor_bitcast_fusion
  15.1 0.7 add_add_fusion.table_ref
  15.8 2.3 %collective-permute-done.1 = bf16[128,256]{1,0:T(8,128)(2,1)S(1)} collective-permute-done((bf16[128,256]{1,0:T(8,128)(2,1)}, bf16[128,256]{1,0:T(8,128)(2,1)S(1)}, u32[]{:S(2)}, u32[]{:S(2)}) %collective-permute-start.1) | collective-permute-done | bytes 65568 | tf_op jit(solution)/shard_map/ppermute | solution.py:15
  18.1 0.9 pad_maximum_fusion.2.refs_0_
  19.0 2.4 %collective-permute-start.3 = (bf16[3,128,256]{2,1,0:T(8,128)(2,1)S(1)}, bf16[3,128,256]{2,1,0:T(8,128)(2,1)S(1)}, u32[]{:S(2)}, u32[]{:S(2)}) collective-permute-start(bf16[3,128,256]{2,1,0:T(8,128)(2,1)S(1)} %pad_maximum_fusion.2.refs_0_), channel_id=1, source_target_pairs={{0,64},{64,0},{128,192},{192,128},{256,320},{320,256},{384,448},{4... | collective-permute-start | bytes 589832 | tf_op jit(solution)/shard_map/ppermute | solution.py:15
  21.4 5.1 %collective-permute-start.2 = (bf16[128,256]{1,0:T(8,128)(2,1)S(1)}, bf16[128,256]{1,0:T(8,128)(2,1)S(1)}, u32[]{:S(2)}, u32[]{:S(2)}) collective-permute-start(bf16[128,256]{1,0:T(8,128)(2,1)S(1)} %collective-permute-done), channel_id=1, source_target_pairs={{0,128},{64,192},{128,0},{192,64},{256,384},{320,448},{384,256},{4... | collective-permute-start | bytes 196616 | tf_op jit(solution)/shard_map/ppermute | solution.py:15
  26.5 2.2 %collective-permute-done.2.refs_1_ = bf16[128,256]{1,0:T(8,128)(2,1)S(1)} collective-permute-done((bf16[128,256]{1,0:T(8,128)(2,1)S(1)}, bf16[128,256]{1,0:T(8,128)(2,1)S(1)}, u32[]{:S(2)}, u32[]{:S(2)}) %collective-permute-start.2) | collective-permute-done | bytes 65568 | tf_op jit(solution)/shard_map/ppermute | solution.py:15
  28.7 3.2 %collective-permute-start.4 = (bf16[128,256]{1,0:T(8,128)(2,1)S(1)}, bf16[128,256]{1,0:T(8,128)(2,1)S(1)}, u32[]{:S(2)}, u32[]{:S(2)}) collective-permute-start(bf16[128,256]{1,0:T(8,128)(2,1)S(1)} %collective-permute-done.2.refs_1_), channel_id=1, source_target_pairs={{0,64},{64,0},{128,192},{192,128},{256,320},{320,256},{384,448},{4... | collective-permute-start | bytes 196616 | tf_op jit(solution)/shard_map/ppermute | solution.py:15
  31.9 0.9 pad_maximum_fusion
  32.8 1.9 %collective-permute-start.5 = (bf16[4,128,256]{2,1,0:T(8,128)(2,1)S(1)}, bf16[4,128,256]{2,1,0:T(8,128)(2,1)S(1)}, u32[]{:S(2)}, u32[]{:S(2)}) collective-permute-start(bf16[4,128,256]{2,1,0:T(8,128)(2,1)S(1)} %pad_maximum_fusion), channel_id=1, source_target_pairs={{0,32},{32,0},{1,33},{33,1},{2,34},{34,2},{3,35},{35,3},{4,36},{36... | collective-permute-start | bytes 786440 | tf_op jit(solution)/shard_map/ppermute | solution.py:15
  34.7 0.2 collective-permute-done.4.refs_3_
  34.9 2.3 %collective-permute-start.6 = (bf16[4,128,256]{2,1,0:T(8,128)(2,1)S(1)}, bf16[4,128,256]{2,1,0:T(8,128)(2,1)S(1)}, u32[]{:S(2)}, u32[]{:S(2)}) collective-permute-start(bf16[4,128,256]{2,1,0:T(8,128)(2,1)S(1)} %pad_maximum_fusion.1), channel_id=1, source_target_pairs={{0,32},{32,0},{1,33},{33,1},{2,34},{34,2},{3,35},{35,3},{4,36},{36... | collective-permute-start | bytes 786440 | tf_op jit(solution)/shard_map/ppermute | solution.py:15
  37.2 1.2 %collective-permute-done.6.refs_5_ = bf16[4,128,256]{2,1,0:T(8,128)(2,1)S(1)} collective-permute-done((bf16[4,128,256]{2,1,0:T(8,128)(2,1)S(1)}, bf16[4,128,256]{2,1,0:T(8,128)(2,1)S(1)}, u32[]{:S(2)}, u32[]{:S(2)}) %collective-permute-start.6) | collective-permute-done | bytes 262176 | tf_op jit(solution)/shard_map/ppermute | solution.py:15
  38.3 6.0 %far_terms.1 = (bf16[16,128,256]{2,1,0:T(8,128)(2,1)S(1)}, bf16[16,128,256]{2,1,0:T(8,128)(2,1)}) custom-call(s32[6,32]{1,0:T(8,128)S(1)} %add_add_fusion.table_ref, bf16[16,2,4,128,128]{4,3,2,1,0:T(8,128)(2,1)} %bitcast.14, bf16[3,128,256]{2,1,0:T(8,128)(2,1)S(1)} %pad_maximum_fusion.2.refs_0_, bf16[128,256]{1,0:T(8,128)(2,1)S(1)} %collective-permute-done.2.refs_1_, ...), custom_call_target="tpu_custom_call" | custom-call | flops 536870912 | bytes 4194304 | tf_op jit(solution)/shard_map/far_terms/pallas_call | solution.py:123
  44.3 7.5 %all-to-all-start.1 = ((bf16[16,128,256]{2,1,0:T(8,128)(2,1)}), bf16[16,128,256]{2,1,0:T(8,128)(2,1)S(1)}, u32[]{:S(2)}, u32[]{:S(2)}) async-start(bf16[16,128,256]{2,1,0:T(8,128)(2,1)} %get-tuple-element.12), calls=%async_computation.1 | async-start | bytes 2097152 | tf_op jit(solution)/shard_map/all_to_all | solution.py:189
  51.8 4.8 %near_terms.1 = bf16[16,128,256]{2,1,0:T(8,128)(2,1)} custom-call(s32[6,32]{1,0:T(8,128)S(1)} %add_add_fusion.table_ref, bf16[16,2,4,128,128]{4,3,2,1,0:T(8,128)(2,1)} %bitcast.15, bf16[16,128,256]{2,1,0:T(8,128)(2,1)S(1)} %get-tuple-element.11.stripe_ref), custom_call_target="tpu_custom_call" | custom-call | flops 536870912 | bytes 4194304 | tf_op jit(solution)/shard_map/near_terms/pallas_call | solution.py:64
  56.6 10.9 %all-to-all-done.1.parts_ref = bf16[16,128,256]{2,1,0:T(8,128)(2,1)S(1)} async-done(((bf16[16,128,256]{2,1,0:T(8,128)(2,1)}), bf16[16,128,256]{2,1,0:T(8,128)(2,1)S(1)}, u32[]{:S(2)}, u32[]{:S(2)}) %all-to-all-start.1) | async-done | bytes 1048608 | tf_op jit(solution)/shard_map/all_to_all | solution.py:189
  67.5 6.2 %all-to-all-start = ((bf16[16,128,256]{2,1,0:T(8,128)(2,1)}), bf16[16,128,256]{2,1,0:T(8,128)(2,1)S(1)}, u32[]{:S(2)}, u32[]{:S(2)}) async-start(bf16[16,128,256]{2,1,0:T(8,128)(2,1)} %near_terms.1), calls=%async_computation | async-start | bytes 2097152 | tf_op jit(solution)/shard_map/all_to_all | solution.py:190
  73.8 11.7 %collective-permute-start.7 = (bf16[128,256]{1,0:T(8,128)(2,1)S(1)}, bf16[128,256]{1,0:T(8,128)(2,1)S(1)}, u32[]{:S(2)}, u32[]{:S(2)}) collective-permute-start(bf16[128,256]{1,0:T(8,128)(2,1)S(1)} %send.1), channel_id=1, source_target_pairs={{0,1},{1,0},{2,3},{3,2},{4,5},{5,4},{6,7},{7,6},{8,9},{9,8},{10,11... | collective-permute-start | bytes 196616 | tf_op jit(solution)/shard_map/ppermute | solution.py:15
  85.6 2.0 %all-to-all-done.parts_ref = bf16[16,128,256]{2,1,0:T(8,128)(2,1)S(1)} async-done(((bf16[16,128,256]{2,1,0:T(8,128)(2,1)}), bf16[16,128,256]{2,1,0:T(8,128)(2,1)S(1)}, u32[]{:S(2)}, u32[]{:S(2)}) %all-to-all-start) | async-done | bytes 1048608 | tf_op jit(solution)/shard_map/all_to_all | solution.py:190
  87.6 1.2 %collective-permute-done.7.other_ref = bf16[128,256]{1,0:T(8,128)(2,1)S(1)} collective-permute-done((bf16[128,256]{1,0:T(8,128)(2,1)S(1)}, bf16[128,256]{1,0:T(8,128)(2,1)S(1)}, u32[]{:S(2)}, u32[]{:S(2)}) %collective-permute-start.7) | collective-permute-done | bytes 65568 | tf_op jit(solution)/shard_map/ppermute | solution.py:15
  88.8 0.9 %finish.1 = bf16[128,256]{1,0:T(8,128)(2,1)} custom-call(bf16[16,128,256]{2,1,0:T(8,128)(2,1)S(1)} %all-to-all-done.parts_ref, bf16[128,256]{1,0:T(8,128)(2,1)S(1)} %collective-permute-done.7.other_ref, bf16[256,256]{1,0:T(8,128)(2,1)S(1)} %copy-done, f32[1,256]{1,0:T(1,128)S(1)} %bitcast.13), custom_call_target="tpu_custom_call" | custom-call | flops 16777216 | bytes 2097152 | tf_op jit(solution)/shard_map/finish/pallas_call | solution.py:19
  (10 shorter events, 0.3 us)
Async XLA Ops:
  0.0 15.8 %collective-permute-start = (bf16[128,256]{1,0:T(8,128)(2,1)}, bf16[128,256]{1,0:T(8,128)(2,1)S(1)}, u32[]{:S(2)}, u32[]{:S(2)}) collective-permute-start(bf16[128,256]{1,0:T(8,128)(2,1)} %param.6), channel_id=1, source_target_pairs={{0,256},{64,320},{128,384},{192,448},{256,0},{320,64},{384,128},{4... | collective-permute-start | bytes 196616 | tf_op jit(solution)/shard_map/ppermute | solution.py:15
  9.1 9.0 %collective-permute-start.1 = (bf16[128,256]{1,0:T(8,128)(2,1)}, bf16[128,256]{1,0:T(8,128)(2,1)S(1)}, u32[]{:S(2)}, u32[]{:S(2)}) collective-permute-start(bf16[128,256]{1,0:T(8,128)(2,1)} %param.6), channel_id=1, source_target_pairs={{0,128},{64,192},{128,0},{192,64},{256,384},{320,448},{384,256},{4... | collective-permute-start | bytes 196616 | tf_op jit(solution)/shard_map/ppermute | solution.py:15
  19.0 15.9 %collective-permute-start.3 = (bf16[3,128,256]{2,1,0:T(8,128)(2,1)S(1)}, bf16[3,128,256]{2,1,0:T(8,128)(2,1)S(1)}, u32[]{:S(2)}, u32[]{:S(2)}) collective-permute-start(bf16[3,128,256]{2,1,0:T(8,128)(2,1)S(1)} %pad_maximum_fusion.2.refs_0_), channel_id=1, source_target_pairs={{0,64},{64,0},{128,192},{192,128},{256,320},{320,256},{384,448},{4... | collective-permute-start | bytes 589832 | tf_op jit(solution)/shard_map/ppermute | solution.py:15
  21.4 7.3 %collective-permute-start.2 = (bf16[128,256]{1,0:T(8,128)(2,1)S(1)}, bf16[128,256]{1,0:T(8,128)(2,1)S(1)}, u32[]{:S(2)}, u32[]{:S(2)}) collective-permute-start(bf16[128,256]{1,0:T(8,128)(2,1)S(1)} %collective-permute-done), channel_id=1, source_target_pairs={{0,128},{64,192},{128,0},{192,64},{256,384},{320,448},{384,256},{4... | collective-permute-start | bytes 196616 | tf_op jit(solution)/shard_map/ppermute | solution.py:15
  28.7 6.1 %collective-permute-start.4 = (bf16[128,256]{1,0:T(8,128)(2,1)S(1)}, bf16[128,256]{1,0:T(8,128)(2,1)S(1)}, u32[]{:S(2)}, u32[]{:S(2)}) collective-permute-start(bf16[128,256]{1,0:T(8,128)(2,1)S(1)} %collective-permute-done.2.refs_1_), channel_id=1, source_target_pairs={{0,64},{64,0},{128,192},{192,128},{256,320},{320,256},{384,448},{4... | collective-permute-start | bytes 196616 | tf_op jit(solution)/shard_map/ppermute | solution.py:15
  32.8 4.4 %collective-permute-start.5 = (bf16[4,128,256]{2,1,0:T(8,128)(2,1)S(1)}, bf16[4,128,256]{2,1,0:T(8,128)(2,1)S(1)}, u32[]{:S(2)}, u32[]{:S(2)}) collective-permute-start(bf16[4,128,256]{2,1,0:T(8,128)(2,1)S(1)} %pad_maximum_fusion), channel_id=1, source_target_pairs={{0,32},{32,0},{1,33},{33,1},{2,34},{34,2},{3,35},{35,3},{4,36},{36... | collective-permute-start | bytes 786440 | tf_op jit(solution)/shard_map/ppermute | solution.py:15
  34.9 3.4 %collective-permute-start.6 = (bf16[4,128,256]{2,1,0:T(8,128)(2,1)S(1)}, bf16[4,128,256]{2,1,0:T(8,128)(2,1)S(1)}, u32[]{:S(2)}, u32[]{:S(2)}) collective-permute-start(bf16[4,128,256]{2,1,0:T(8,128)(2,1)S(1)} %pad_maximum_fusion.1), channel_id=1, source_target_pairs={{0,32},{32,0},{1,33},{33,1},{2,34},{34,2},{3,35},{35,3},{4,36},{36... | collective-permute-start | bytes 786440 | tf_op jit(solution)/shard_map/ppermute | solution.py:15
  44.3 23.2 %all-to-all-start.1 = ((bf16[16,128,256]{2,1,0:T(8,128)(2,1)}), bf16[16,128,256]{2,1,0:T(8,128)(2,1)S(1)}, u32[]{:S(2)}, u32[]{:S(2)}) async-start(bf16[16,128,256]{2,1,0:T(8,128)(2,1)} %get-tuple-element.12), calls=%async_computation.1 | async-start | bytes 2097152 | tf_op jit(solution)/shard_map/all_to_all | solution.py:189
  51.8 37.0 %copy-start = (bf16[256,256]{1,0:T(8,128)(2,1)S(1)}, bf16[256,256]{1,0:T(8,128)(2,1)}, u32[]{:S(2)}) copy-start(bf16[256,256]{1,0:T(8,128)(2,1)} %weight_ref.1) | copy-start | bytes 393220
  51.8 37.0 %copy-start.1 = (f32[256]{0:T(256)S(1)}, f32[256]{0:T(256)}, u32[]{:S(2)}) copy-start(f32[256]{0:T(256)} %param.11) | copy-start | bytes 3076
  67.5 20.0 %all-to-all-start = ((bf16[16,128,256]{2,1,0:T(8,128)(2,1)}), bf16[16,128,256]{2,1,0:T(8,128)(2,1)S(1)}, u32[]{:S(2)}, u32[]{:S(2)}) async-start(bf16[16,128,256]{2,1,0:T(8,128)(2,1)} %near_terms.1), calls=%async_computation | async-start | bytes 2097152 | tf_op jit(solution)/shard_map/all_to_all | solution.py:190
  73.8 14.9 %collective-permute-start.7 = (bf16[128,256]{1,0:T(8,128)(2,1)S(1)}, bf16[128,256]{1,0:T(8,128)(2,1)S(1)}, u32[]{:S(2)}, u32[]{:S(2)}) collective-permute-start(bf16[128,256]{1,0:T(8,128)(2,1)S(1)} %send.1), channel_id=1, source_target_pairs={{0,1},{1,0},{2,3},{3,2},{4,5},{5,4},{6,7},{7,6},{8,9},{9,8},{10,11... | collective-permute-start | bytes 196616 | tf_op jit(solution)/shard_map/ppermute | solution.py:15

commit v4 on v0

v4 whole, which is shorter than its diff:
```python
import jax
import jax.numpy as jnp
from jax import lax
from jax.experimental import pallas as pl
from jax.experimental.pallas import tpu as pltpu
from jax.sharding import Mesh, PartitionSpec as P

ZL, CORE, X, Y, ZH = 8, 2, 4, 4, 2
SLOTS, BS, F = 4, 128, 256
COUNT, HALF, SIDE = SLOTS, SLOTS + 1, SLOTS + 2
VMEM = pl.BlockSpec(memory_space=pltpu.VMEM)
SMEM = pl.BlockSpec(memory_space=pltpu.SMEM)
ANY = pl.BlockSpec(memory_space=pl.ANY)
STEPS = ((4, 2, 1), (2, 4, 1))


def whole(kernel, ins, out_shape, name, cost, limit=4 << 20, specs=None, scratch=()):
    return pl.pallas_call(
        kernel,
        in_specs=specs or [VMEM] * len(ins),
        out_specs=jax.tree.map(lambda _: VMEM, out_shape),
        out_shape=out_shape,
        scratch_shapes=scratch,
        compiler_params=pltpu.CompilerParams(vmem_limit_bytes=limit),
        cost_estimate=pl.CostEstimate(
            flops=cost[0], bytes_accessed=cost[1], transcendentals=0
        ),
        name=name,
    )(*ins)


def copy_kernel(in_ref, out_ref):
    out_ref[...] = in_ref[...]


def side_by_side(table_ref, row, block_of):
    count = table_ref[COUNT, row]
    lhs = []
    for k in range(SLOTS):
        block = block_of(k)
        lhs.append(jnp.where(k < count, block, jnp.zeros_like(block)))
    return jnp.concatenate(lhs, axis=1)


def product(table_ref, row, lhs, stripe_ref):
    rhs = [stripe_ref[table_ref[k, row]] for k in range(SLOTS)]
    term = jnp.dot(
        lhs, jnp.concatenate(rhs, axis=0), preferred_element_type=jnp.float32
    )
    return term.astype(jnp.bfloat16)


def far_lhs_kernel(table_ref, blocks_ref, out_ref):
    step = blocks_ref.shape[0]
    base = pl.program_id(0) * step
    for i in range(step):
        row = 2 * (base + i) + 1 - table_ref[HALF, 0]
        out_ref[i] = side_by_side(table_ref, row, lambda k: blocks_ref[i, 0, k])


def far_lhs_rows(table, blocks):
    step = 4
    return pl.pallas_call(
        far_lhs_kernel,
        grid_spec=pltpu.PrefetchScalarGridSpec(
            num_scalar_prefetch=1,
            grid=(X * Y // step,),
            in_specs=[
                pl.BlockSpec(
                    (step, 1, SLOTS, BS, BS),
                    lambda i, table_ref: (i, 1 - table_ref[HALF, 0], 0, 0, 0),
                )
            ],
            out_specs=pl.BlockSpec((step, BS, SLOTS * BS), lambda i, *_: (i, 0, 0)),
        ),
        out_shape=jax.ShapeDtypeStruct((X * Y, BS, SLOTS * BS), jnp.bfloat16),
        compiler_params=pltpu.CompilerParams(vmem_limit_bytes=6 << 20),
        cost_estimate=pl.CostEstimate(
            flops=0, bytes_accessed=4 << 20, transcendentals=0
        ),
        name="far_lhs",
    )(table, blocks)


def terms_kernel(
    table_ref, blocks_ref, lhs_ref, near_ref, across_ref, out_ref, stripe_ref, held, sem
):
    zh, side = table_ref[HALF, 0], table_ref[SIDE, 0]
    rows = X * Y
    loads = [
        pltpu.make_async_copy(blocks_ref.at[j, zh], held.at[j], sem.at[j])
        for j in range(rows)
    ]
    for load in loads:
        load.start()
    stripe_ref[:ZL] = near_ref[...]
    stripe_ref[ZL:] = across_ref[...]

    def spot(k, m):
        return jnp.where(side == 0, k * Y + m, m * Y + k)

    for k in range(X):
        for m in range(Y):
            j = spot(k, m)
            out_ref[k, 0, m] = product(
                table_ref, 2 * j + 1 - zh, lhs_ref[j], stripe_ref
            )
    for load in loads:
        load.wait()
    for k in range(X):
        for m in range(Y):
            j = spot(k, m)
            row = 2 * j + zh
            lhs = side_by_side(table_ref, row, lambda s: held[j, s])
            out_ref[k, 1, m] = product(table_ref, row, lhs, stripe_ref)


def total(parts):
    acc = parts[0].astype(jnp.float32)
    for part in parts[1:]:
        acc = acc + part.astype(jnp.float32)
    return acc


def stage_kernel(parts_ref, out_ref):
    for half in range(2):
        for m in range(Y):
            out_ref[m, half] = total(
                [parts_ref[k, half, m] for k in range(X)]
            ).astype(jnp.bfloat16)


def send_kernel(parts_ref, out_ref):
    out_ref[...] = total([parts_ref[k, 0] for k in range(Y)]).astype(jnp.bfloat16)


def finish_kernel(parts_ref, other_ref, weight_ref, bias_ref, out_ref):
    summed = total([parts_ref[k, 1] for k in range(Y)]) + other_ref[...].astype(
        jnp.float32
    )
    hidden = jnp.dot(
        summed.astype(jnp.bfloat16),
        weight_ref[...],
        preferred_element_type=jnp.float32,
    )
    out_ref[...] = jnp.maximum(hidden + bias_ref[...], 0.0).astype(jnp.bfloat16)


def along(first):
    by_x = [[x * Y + y for x in range(X)] for y in range(Y)]
    by_y = [[x * Y + y for y in range(Y)] for x in range(X)]
    sides = (by_x, by_y) if first else (by_y, by_x)
    return [[c * X * Y + i for i in g] for c, gs in enumerate(sides) for g in gs]


def exchange(value, first):
    return lax.all_to_all(
        value, ("core", "x", "y"), 0, 0, axis_index_groups=along(first)
    )


def shard_table(block_col, row_count):
    zl, core, zh = (
        lax.axis_index(a).astype(jnp.int32) for a in ("zl", "core", "zh")
    )
    col = block_col.T
    offset, side = (col >> 1) ^ zl, col & 1
    high, mid = (offset >> 2) & 1, (offset >> 1) & 1
    first = jnp.where(side == 0, high, mid)
    second = jnp.where(side == 0, mid, high)
    spots = first + 2 * second + 4 * (offset & 1) + 8 * (side ^ core)
    counts = row_count.T
    return jnp.concatenate(
        [spots, counts, jnp.full_like(counts, zh), jnp.full_like(counts, core)], axis=0
    )


def local(features, blocks, block_col, row_count, weight, out_bias):
    bf16 = jnp.bfloat16
    table = shard_table(block_col, row_count)
    blocks = pltpu.with_memory_space_constraint(
        blocks.reshape(X * Y, ZH, SLOTS, BS, BS), pltpu.HBM
    )
    own = whole(
        copy_kernel,
        [features[None]],
        jax.ShapeDtypeStruct((1, BS, F), bf16),
        "own",
        (0, 1 << 17),
    )
    held = own
    for step in range(3):
        came = lax.ppermute(
            features[None] if step == 0 else held,
            ("zl", "core"),
            [
                (z * CORE + c, (z ^ STEPS[c][step]) * CORE + c)
                for z in range(ZL)
                for c in range(CORE)
            ],
        )
        if step == 0:
            came, table = lax.optimization_barrier((came, table))
            far_lhs = far_lhs_rows(table, blocks)
        if step == 1:
            came, far_lhs = lax.optimization_barrier((came, far_lhs))
        held = jnp.concatenate([held, came], axis=0)
    across = lax.ppermute(held, "core", [(0, 1), (1, 0)])
    shape = (X, 2, Y, BS, F)
    terms = whole(
        terms_kernel,
        [table, blocks, far_lhs, held, across],
        jax.ShapeDtypeStruct(shape, bf16),
        "terms",
        (2 * X * Y * 2 * SLOTS * BS * BS * F, 6 << 20),
        limit=10 << 20,
        specs=[SMEM, ANY, VMEM, VMEM, VMEM],
        scratch=[
            pltpu.VMEM((CORE * ZL, BS, F), bf16),
            pltpu.VMEM((X * Y, SLOTS, BS, BS), bf16),
            pltpu.SemaphoreType.DMA((X * Y,)),
        ],
    )
    four = jax.ShapeDtypeStruct((Y, 2, BS, F), bf16)
    one = jax.ShapeDtypeStruct((BS, F), bf16)
    staged = whole(stage_kernel, [exchange(terms, True)], four, "stage", (0, 3 << 20))
    parts = exchange(staged, False)
    send = whole(send_kernel, [parts], one, "send", (0, 1 << 18))
    other = lax.ppermute(send, "zh", [(0, 1), (1, 0)])
    return whole(
        finish_kernel,
        [parts, other, weight, out_bias[None]],
        one,
        "finish",
        (2 * BS * F * F, 1 << 19),
    )


def solution(mesh):
    fine = Mesh(
        mesh.devices.reshape(ZL, CORE, X, Y, ZH), ("zl", "core", "x", "y", "zh")
    )
    row, col = ("zl", "core"), ("x", "y", "zh")
    return jax.shard_map(
        local,
        mesh=fine,
        in_specs=(
            P(row + col, None),
            P(row, col, None, None),
            P(row, col),
            P(row, col),
            P(),
            P(),
        ),
        out_specs=P(row + col, None),
        check_vma=False,
    )
```

time: 515 us -> 91.4 us (0.18)
  the two profiles are of different devices: /device:TPU:96 before, /device:TPU:32 now
where the time goes in v4:
time: 91.4 us; the launch traced here: 90.9 us
  starting transfers between devices  34 us (37%)
  blocking collectives  32.9 us (36%)
  waiting for transfers between devices  13.4 us (15%)
  Pallas kernels  7.92 us (9%)
  other arithmetic  1.51 us (2%)
  local copies, waits for them, and re-layouts  0.99 us (1%)
    all_to_all x2, blocking collectives, exchange(): lax.all_to_all(value, ('core', 'x', 'y'), 0, 0, axis_index_groups=along(f...  32.9 us
    ppermute x3, starting transfers between devices, local(): lax.ppermute(features[None] if step == 0 else held, ('zl', 'core'), [(z *...  18.1 us
    ppermute x1, starting transfers between devices, local(): other = lax.ppermute(send, 'zh', [(0, 1), (1, 0)])  14 us
    ppermute x3, waiting for transfers between devices, local(): lax.ppermute(features[None] if step == 0 else held, ('zl', 'core'), [(z *...  7.73 us
    pallas_call x5, Pallas kernels, whole(): pl.pallas_call(kernel, in_specs=specs or [VMEM] * len(ins), out_specs=jax...  4.81 us
    ppermute x1, waiting for transfers between devices, local(): other = lax.ppermute(send, 'zh', [(0, 1), (1, 0)])  3.81 us
    pallas_call x1, Pallas kernels, far_lhs_rows(): pl.pallas_call(far_lhs_kernel, grid_spec=pltpu.PrefetchScalarGridSpec(num...  3.11 us
    ppermute x1, starting transfers between devices, local(): across = lax.ppermute(held, 'core', [(0, 1), (1, 0)])  1.92 us
  transfers between devices with their start and end apart: 5, of which 5 were waited for; matrix products, arithmetic and copies ran while one was open for 2% of the time, Pallas kernels for 3%

profile of v4, /device:TPU:32, one launch (start us, length us, event | category | flops | bytes accessed | tf_op | source)
XLA Modules:
  0.0 90.9 jit_solution(7971911516928791999)
XLA Ops:
  0.0 9.1 %collective-permute-start = (bf16[1,128,256]{2,1,0:T(8,128)(2,1)}, bf16[1,128,256]{2,1,0:T(8,128)(2,1)S(1)}, u32[]{:S(2)}, u32[]{:S(2)}) collective-permute-start(bf16[1,128,256]{2,1,0:T(8,128)(2,1)} %bitcast.8), channel_id=1, source_target_pairs={{0,256},{32,160},{64,320},{96,224},{128,384},{160,32},{192,448},{2... | collective-permute-start | bytes 196616 | tf_op jit(solution)/shard_map/ppermute | solution.py:193
  9.1 0.1 pad.11.clone
  9.2 0.1 pad.12.clone
  9.3 0.7 add_bitcast_fusion
  9.9 0.7 add_add_fusion.table_ref
  10.7 0.8 copy-done.1
  11.5 1.3 %collective-permute-done = bf16[1,128,256]{2,1,0:T(8,128)(2,1)S(1)} collective-permute-done((bf16[1,128,256]{2,1,0:T(8,128)(2,1)}, bf16[1,128,256]{2,1,0:T(8,128)(2,1)S(1)}, u32[]{:S(2)}, u32[]{:S(2)}) %collective-permute-start) | collective-permute-done | bytes 65568 | tf_op jit(solution)/shard_map/ppermute | solution.py:193
  12.9 4.3 %collective-permute-start.1 = (bf16[2,128,256]{2,1,0:T(8,128)(2,1)S(1)}, bf16[2,128,256]{2,1,0:T(8,128)(2,1)S(1)}, u32[]{:S(2)}, u32[]{:S(2)}) collective-permute-start(bf16[2,128,256]{2,1,0:T(8,128)(2,1)S(1)} %pad_maximum_fusion.2), channel_id=1, source_target_pairs={{0,128},{32,288},{64,192},{96,352},{128,0},{160,416},{192,64},{224... | collective-permute-start | bytes 393224 | tf_op jit(solution)/shard_map/ppermute | solution.py:193
  17.2 3.1 %far_lhs.1.lhs_ref = bf16[16,128,512]{2,1,0:T(8,128)(2,1)S(1)} custom-call(s32[7,32]{1,0:T(8,128)S(1)} %add_add_fusion.table_ref, bf16[16,2,4,128,128]{4,3,2,1,0:T(8,128)(2,1)} %bitcast.11), custom_call_target="tpu_custom_call" | custom-call | bytes 4194304 | tf_op jit(solution)/shard_map/far_lhs/pallas_call | solution.py:63
  20.3 1.4 %collective-permute-done.1 = bf16[2,128,256]{2,1,0:T(8,128)(2,1)S(1)} collective-permute-done((bf16[2,128,256]{2,1,0:T(8,128)(2,1)S(1)}, bf16[2,128,256]{2,1,0:T(8,128)(2,1)S(1)}, u32[]{:S(2)}, u32[]{:S(2)}) %collective-permute-start.1) | collective-permute-done | bytes 131104 | tf_op jit(solution)/shard_map/ppermute | solution.py:193
  21.7 4.7 %collective-permute-start.2 = (bf16[4,128,256]{2,1,0:T(8,128)(2,1)S(1)}, bf16[4,128,256]{2,1,0:T(8,128)(2,1)S(1)}, u32[]{:S(2)}, u32[]{:S(2)}) collective-permute-start(bf16[4,128,256]{2,1,0:T(8,128)(2,1)S(1)} %pad_maximum_fusion.1), channel_id=1, source_target_pairs={{0,64},{32,96},{64,0},{96,32},{128,192},{160,224},{192,128},{224,1... | collective-permute-start | bytes 786440 | tf_op jit(solution)/shard_map/ppermute | solution.py:193
  26.5 5.0 %collective-permute-done.2 = bf16[4,128,256]{2,1,0:T(8,128)(2,1)S(1)} collective-permute-done((bf16[4,128,256]{2,1,0:T(8,128)(2,1)S(1)}, bf16[4,128,256]{2,1,0:T(8,128)(2,1)S(1)}, u32[]{:S(2)}, u32[]{:S(2)}) %collective-permute-start.2) | collective-permute-done | bytes 262176 | tf_op jit(solution)/shard_map/ppermute | solution.py:193
  31.5 0.1 pad_maximum_fusion.near_ref
  31.5 1.9 %collective-permute-start.3 = (bf16[8,128,256]{2,1,0:T(8,128)(2,1)S(1)}, bf16[8,128,256]{2,1,0:T(8,128)(2,1)S(1)}, u32[]{:S(2)}, u32[]{:S(2)}) collective-permute-start(bf16[8,128,256]{2,1,0:T(8,128)(2,1)S(1)} %pad_maximum_fusion.near_ref), channel_id=1, source_target_pairs={{0,32},{32,0},{1,33},{33,1},{2,34},{34,2},{3,35},{35,3},{4,36},{36... | collective-permute-start | bytes 1572872 | tf_op jit(solution)/shard_map/ppermute | solution.py:208
  33.4 1.9 %collective-permute-done.3.across_ref = bf16[8,128,256]{2,1,0:T(8,128)(2,1)S(1)} collective-permute-done((bf16[8,128,256]{2,1,0:T(8,128)(2,1)S(1)}, bf16[8,128,256]{2,1,0:T(8,128)(2,1)S(1)}, u32[]{:S(2)}, u32[]{:S(2)}) %collective-permute-start.3) | collective-permute-done | bytes 524320 | tf_op jit(solution)/shard_map/ppermute | solution.py:208
  35.3 3.7 %terms.1 = bf16[4,2,4,128,256]{4,3,2,1,0:T(8,128)(2,1)S(1)} custom-call(s32[7,32]{1,0:T(8,128)S(1)} %add_add_fusion.table_ref, bf16[16,2,4,128,128]{4,3,2,1,0:T(8,128)(2,1)} %bitcast.12, bf16[16,128,512]{2,1,0:T(8,128)(2,1)S(1)} %far_lhs.1.lhs_ref, bf16[8,128,256]{2,1,0:T(8,128)(2,1)S(1)} %pad_maximum_fusion.near_ref, ...), custom_call_target="tpu_custom_call" | custom-call | flops 1073741824 | bytes 6291456 | tf_op jit(solution)/shard_map/terms/pallas_call | solution.py:18
  39.0 20.6 %all_to_all.10.parts_ref = bf16[4,2,4,128,256]{4,3,2,1,0:T(8,128)(2,1)S(1)} all-to-all(bf16[4,2,4,128,256]{4,3,2,1,0:T(8,128)(2,1)S(1)} %terms.1), channel_id=1, replica_groups={{0,8,16,24},{2,10,18,26},{4,12,20,28},{6,14,22,30},{32,34,36,38},{40,42..., dimensions={0} | all-to-all | bytes 4194304 | tf_op jit(solution)/shard_map/all_to_all | solution.py:157
  59.6 0.3 stage.1
  59.9 12.4 %all_to_all.11.parts_ref = bf16[4,2,128,256]{3,2,1,0:T(8,128)(2,1)S(1)} all-to-all(bf16[4,2,128,256]{3,2,1,0:T(8,128)(2,1)S(1)} %stage.1), channel_id=1, replica_groups={{0,2,4,6},{8,10,12,14},{16,18,20,22},{24,26,28,30},{32,40,48,56},{34,42..., dimensions={0} | all-to-all | bytes 1048576 | tf_op jit(solution)/shard_map/all_to_all | solution.py:157
  72.3 14.0 %collective-permute-start.4 = (bf16[128,256]{1,0:T(8,128)(2,1)S(1)}, bf16[128,256]{1,0:T(8,128)(2,1)S(1)}, u32[]{:S(2)}, u32[]{:S(2)}) collective-permute-start(bf16[128,256]{1,0:T(8,128)(2,1)S(1)} %send.1), channel_id=1, source_target_pairs={{0,1},{1,0},{2,3},{3,2},{4,5},{5,4},{6,7},{7,6},{8,9},{9,8},{10,11... | collective-permute-start | bytes 196616 | tf_op jit(solution)/shard_map/ppermute | solution.py:229
  86.3 3.8 %collective-permute-done.4.other_ref = bf16[128,256]{1,0:T(8,128)(2,1)S(1)} collective-permute-done((bf16[128,256]{1,0:T(8,128)(2,1)S(1)}, bf16[128,256]{1,0:T(8,128)(2,1)S(1)}, u32[]{:S(2)}, u32[]{:S(2)}) %collective-permute-start.4) | collective-permute-done | bytes 65568 | tf_op jit(solution)/shard_map/ppermute | solution.py:229
  90.1 0.0 copy-done
  90.1 0.0 copy-done.2
  90.1 0.8 finish.1
  (7 shorter events, 0.1 us)
Async XLA Ops:
  0.0 12.8 %collective-permute-start = (bf16[1,128,256]{2,1,0:T(8,128)(2,1)}, bf16[1,128,256]{2,1,0:T(8,128)(2,1)S(1)}, u32[]{:S(2)}, u32[]{:S(2)}) collective-permute-start(bf16[1,128,256]{2,1,0:T(8,128)(2,1)} %bitcast.8), channel_id=1, source_target_pairs={{0,256},{32,160},{64,320},{96,224},{128,384},{160,32},{192,448},{2... | collective-permute-start | bytes 196616 | tf_op jit(solution)/shard_map/ppermute | solution.py:193
  10.7 0.8 copy-start.1
  12.9 8.9 %collective-permute-start.1 = (bf16[2,128,256]{2,1,0:T(8,128)(2,1)S(1)}, bf16[2,128,256]{2,1,0:T(8,128)(2,1)S(1)}, u32[]{:S(2)}, u32[]{:S(2)}) collective-permute-start(bf16[2,128,256]{2,1,0:T(8,128)(2,1)S(1)} %pad_maximum_fusion.2), channel_id=1, source_target_pairs={{0,128},{32,288},{64,192},{96,352},{128,0},{160,416},{192,64},{224... | collective-permute-start | bytes 393224 | tf_op jit(solution)/shard_map/ppermute | solution.py:193
  21.7 9.7 %collective-permute-start.2 = (bf16[4,128,256]{2,1,0:T(8,128)(2,1)S(1)}, bf16[4,128,256]{2,1,0:T(8,128)(2,1)S(1)}, u32[]{:S(2)}, u32[]{:S(2)}) collective-permute-start(bf16[4,128,256]{2,1,0:T(8,128)(2,1)S(1)} %pad_maximum_fusion.1), channel_id=1, source_target_pairs={{0,64},{32,96},{64,0},{96,32},{128,192},{160,224},{192,128},{224,1... | collective-permute-start | bytes 786440 | tf_op jit(solution)/shard_map/ppermute | solution.py:193
  31.5 3.8 %collective-permute-start.3 = (bf16[8,128,256]{2,1,0:T(8,128)(2,1)S(1)}, bf16[8,128,256]{2,1,0:T(8,128)(2,1)S(1)}, u32[]{:S(2)}, u32[]{:S(2)}) collective-permute-start(bf16[8,128,256]{2,1,0:T(8,128)(2,1)S(1)} %pad_maximum_fusion.near_ref), channel_id=1, source_target_pairs={{0,32},{32,0},{1,33},{33,1},{2,34},{34,2},{3,35},{35,3},{4,36},{36... | collective-permute-start | bytes 1572872 | tf_op jit(solution)/shard_map/ppermute | solution.py:208
  59.6 30.5 %copy-start = (bf16[256,256]{1,0:T(8,128)(2,1)S(1)}, bf16[256,256]{1,0:T(8,128)(2,1)}, u32[]{:S(2)}) copy-start(bf16[256,256]{1,0:T(8,128)(2,1)} %weight_ref.1) | copy-start | bytes 393220
  59.6 30.5 %copy-start.2 = (f32[256]{0:T(256)S(1)}, f32[256]{0:T(256)}, u32[]{:S(2)}) copy-start(f32[256]{0:T(256)} %param.11) | copy-start | bytes 3076
  72.3 17.8 %collective-permute-start.4 = (bf16[128,256]{1,0:T(8,128)(2,1)S(1)}, bf16[128,256]{1,0:T(8,128)(2,1)S(1)}, u32[]{:S(2)}, u32[]{:S(2)}) collective-permute-start(bf16[128,256]{1,0:T(8,128)(2,1)S(1)} %send.1), channel_id=1, source_target_pairs={{0,1},{1,0},{2,3},{3,2},{4,5},{5,4},{6,7},{7,6},{8,9},{9,8},{10,11... | collective-permute-start | bytes 196616 | tf_op jit(solution)/shard_map/ppermute | solution.py:229

commit v5 on v4

v5 whole, which is shorter than its diff:
```python
import jax
import jax.numpy as jnp
from jax import lax
from jax.experimental import pallas as pl
from jax.experimental.pallas import tpu as pltpu
from jax.sharding import Mesh, PartitionSpec as P

ZL, CORE, X, Y, ZH = 8, 2, 4, 4, 2
SLOTS, BS, F = 4, 128, 256
COUNT, HALF = SLOTS, SLOTS + 1
VMEM = pl.BlockSpec(memory_space=pltpu.VMEM)
SMEM = pl.BlockSpec(memory_space=pltpu.SMEM)
ANY = pl.BlockSpec(memory_space=pl.ANY)


def whole(
    kernel,
    ins,
    out_shape,
    name,
    cost,
    limit=4 << 20,
    specs=None,
    out_specs=None,
    scratch=(),
):
    return pl.pallas_call(
        kernel,
        in_specs=specs or [VMEM] * len(ins),
        out_specs=out_specs or jax.tree.map(lambda _: VMEM, out_shape),
        out_shape=out_shape,
        scratch_shapes=scratch,
        compiler_params=pltpu.CompilerParams(vmem_limit_bytes=limit),
        cost_estimate=pl.CostEstimate(
            flops=cost[0], bytes_accessed=cost[1], transcendentals=0
        ),
        name=name,
    )(*ins)


def copy_kernel(in_ref, out_ref):
    out_ref[...] = in_ref[...]


def side_by_side(table_ref, row, block_of):
    count = table_ref[COUNT, row]
    lhs = []
    for k in range(SLOTS):
        block = block_of(k)
        lhs.append(jnp.where(k < count, block, jnp.zeros_like(block)))
    return jnp.concatenate(lhs, axis=1)


def product(table_ref, row, lhs, stripe_ref):
    rhs = [stripe_ref[table_ref[k, row]] for k in range(SLOTS)]
    term = jnp.dot(
        lhs, jnp.concatenate(rhs, axis=0), preferred_element_type=jnp.float32
    )
    return term.astype(jnp.bfloat16)


def far_lhs_kernel(table_ref, blocks_ref, out_ref):
    step = blocks_ref.shape[0]
    base = pl.program_id(0) * step
    for i in range(step):
        row = 2 * (base + i) + 1 - table_ref[HALF, 0]
        out_ref[i] = side_by_side(table_ref, row, lambda k: blocks_ref[i, 0, k])


def far_lhs_rows(table, blocks):
    step = 4
    return pl.pallas_call(
        far_lhs_kernel,
        grid_spec=pltpu.PrefetchScalarGridSpec(
            num_scalar_prefetch=1,
            grid=(X * Y // step,),
            in_specs=[
                pl.BlockSpec(
                    (step, 1, SLOTS, BS, BS),
                    lambda i, table_ref: (i, 1 - table_ref[HALF, 0], 0, 0, 0),
                )
            ],
            out_specs=pl.BlockSpec((step, BS, SLOTS * BS), lambda i, *_: (i, 0, 0)),
        ),
        out_shape=jax.ShapeDtypeStruct((X * Y, BS, SLOTS * BS), jnp.bfloat16),
        compiler_params=pltpu.CompilerParams(vmem_limit_bytes=6 << 20),
        cost_estimate=pl.CostEstimate(
            flops=0, bytes_accessed=4 << 20, transcendentals=0
        ),
        name="far_lhs",
    )(table, blocks)


def far_kernel(
    table_ref, lhs_ref, near_ref, across_ref, stripe_ref, out_ref, made, sem
):
    stripe_ref[:ZL] = near_ref[...]
    stripe_ref[ZL:] = across_ref[...]
    group = X * Y // sem.shape[0]
    stores = []
    for g in range(sem.shape[0]):
        for j in range(g * group, (g + 1) * group):
            made[j] = product(
                table_ref, 2 * j + 1 - table_ref[HALF, 0], lhs_ref[j], stripe_ref
            )
        part = pl.ds(g * group, group)
        stores.append(
            pltpu.make_async_copy(made.at[part], out_ref.at[part], sem.at[g])
        )
        stores[-1].start()
    for store in stores:
        store.wait()


def near_kernel(table_ref, blocks_ref, stripe_ref, out_ref):
    step = blocks_ref.shape[0]
    base = pl.program_id(0) * step
    for i in range(step):
        row = 2 * (base + i) + table_ref[HALF, 0]
        lhs = side_by_side(table_ref, row, lambda k: blocks_ref[i, 0, k])
        out_ref[i] = product(table_ref, row, lhs, stripe_ref)


def near_half(table, blocks, stripe):
    step = 4
    return pl.pallas_call(
        near_kernel,
        grid_spec=pltpu.PrefetchScalarGridSpec(
            num_scalar_prefetch=1,
            grid=(X * Y // step,),
            in_specs=[
                pl.BlockSpec(
                    (step, 1, SLOTS, BS, BS),
                    lambda i, table_ref: (i, table_ref[HALF, 0], 0, 0, 0),
                ),
                VMEM,
            ],
            out_specs=pl.BlockSpec((step, BS, F), lambda i, *_: (i, 0, 0)),
        ),
        out_shape=jax.ShapeDtypeStruct((X * Y, BS, F), jnp.bfloat16),
        compiler_params=pltpu.CompilerParams(vmem_limit_bytes=8 << 20),
        cost_estimate=pl.CostEstimate(
            flops=2 * X * Y * SLOTS * BS * BS * F,
            bytes_accessed=4 << 20,
            transcendentals=0,
        ),
        name="near_terms",
    )(table, blocks, stripe)


def total(parts):
    acc = parts[0].astype(jnp.float32)
    for part in parts[1:]:
        acc = acc + part.astype(jnp.float32)
    return acc


def send_kernel(parts_ref, out_ref):
    out_ref[...] = total([parts_ref[k] for k in range(X * Y)]).astype(jnp.bfloat16)


def finish_kernel(parts_ref, other_ref, weight_ref, bias_ref, out_ref):
    summed = total([parts_ref[k] for k in range(X * Y)]) + other_ref[...].astype(
        jnp.float32
    )
    hidden = jnp.dot(
        summed.astype(jnp.bfloat16),
        weight_ref[...],
        preferred_element_type=jnp.float32,
    )
    out_ref[...] = jnp.maximum(hidden + bias_ref[...], 0.0).astype(jnp.bfloat16)


def shard_table(block_col, row_count):
    zl, core, zh = (
        lax.axis_index(a).astype(jnp.int32) for a in ("zl", "core", "zh")
    )
    offset = block_col.T ^ (CORE * zl + core)
    spots = (
        ((offset >> 3) & 1)
        | ((offset >> 1) & 2)
        | ((offset << 1) & 4)
        | ((offset << 3) & 8)
    )
    counts = row_count.T
    return jnp.concatenate([spots, counts, jnp.full_like(counts, zh)], axis=0)


def local(features, blocks, block_col, row_count, weight, out_bias):
    bf16 = jnp.bfloat16
    table = shard_table(block_col, row_count)
    blocks = pltpu.with_memory_space_constraint(
        blocks.reshape(X * Y, ZH, SLOTS, BS, BS), pltpu.HBM
    )
    own = whole(
        copy_kernel,
        [features[None]],
        jax.ShapeDtypeStruct((1, BS, F), bf16),
        "own",
        (0, 1 << 17),
    )
    held = own
    for bit in (4, 2, 1):
        came = lax.ppermute(
            features[None] if bit == 4 else held,
            "zl",
            [(z, z ^ bit) for z in range(ZL)],
        )
        if bit == 4:
            came, table = lax.optimization_barrier((came, table))
            far_lhs = far_lhs_rows(table, blocks)
        if bit == 2:
            came, far_lhs = lax.optimization_barrier((came, far_lhs))
        held = jnp.concatenate([held, came], axis=0)
    across = lax.ppermute(held, "core", [(0, 1), (1, 0)])
    half = (X * Y, BS, F)
    one = jax.ShapeDtypeStruct((BS, F), bf16)
    stripe, far_terms = whole(
        far_kernel,
        [table, far_lhs, held, across],
        [jax.ShapeDtypeStruct(half, bf16)] * 2,
        "far_terms",
        (2 * X * Y * SLOTS * BS * BS * F, 4 << 20),
        limit=8 << 20,
        specs=[SMEM, VMEM, VMEM, VMEM],
        out_specs=[VMEM, ANY],
        scratch=[pltpu.VMEM(half, bf16), pltpu.SemaphoreType.DMA((4,))],
    )
    near_terms = near_half(table, blocks, stripe)
    far_parts = lax.all_to_all(far_terms, ("x", "y"), 0, 0)
    near_parts = lax.all_to_all(near_terms, ("x", "y"), 0, 0)
    send = whole(send_kernel, [far_parts], one, "send", (0, 1 << 20))
    other = lax.ppermute(send, "zh", [(0, 1), (1, 0)])
    return whole(
        finish_kernel,
        [near_parts, other, weight, out_bias[None]],
        one,
        "finish",
        (2 * BS * F * F, 2 << 20),
    )


def solution(mesh):
    fine = Mesh(
        mesh.devices.reshape(ZL, CORE, X, Y, ZH), ("zl", "core", "x", "y", "zh")
    )
    row, col = ("zl", "core"), ("x", "y", "zh")
    return jax.shard_map(
        local,
        mesh=fine,
        in_specs=(
            P(row + col, None),
            P(row, col, None, None),
            P(row, col),
            P(row, col),
            P(),
            P(),
        ),
        out_specs=P(row + col, None),
        check_vma=False,
    )
```

time: 91.4 us -> 88.7 us (0.970)
  the two profiles are of different devices: /device:TPU:32 before, /device:TPU:2 now
where the time goes in v5:
time: 88.7 us; the launch traced here: 88.2 us
  starting transfers between devices  45.2 us (51%)
  waiting for transfers between devices  29.2 us (33%)
  Pallas kernels  11.1 us (13%)
  other arithmetic  1.51 us (2%)
  local copies, waits for them, and re-layouts  0.92 us (1%)
    ppermute x1, starting transfers between devices, local(): other = lax.ppermute(send, 'zh', [(0, 1), (1, 0)])  16.1 us
    ppermute x3, waiting for transfers between devices, local(): lax.ppermute(features[None] if bit == 4 else held, 'zl', [(z, z ^ bit) fo...  14.6 us
    ppermute x3, starting transfers between devices, local(): lax.ppermute(features[None] if bit == 4 else held, 'zl', [(z, z ^ bit) fo...  13.4 us
    all_to_all x1, waiting for transfers between devices, local(): far_parts = lax.all_to_all(far_terms, ('x', 'y'), 0, 0)  10.5 us
    all_to_all x1, starting transfers between devices, local(): far_parts = lax.all_to_all(far_terms, ('x', 'y'), 0, 0)  7.49 us
    all_to_all x1, starting transfers between devices, local(): near_parts = lax.all_to_all(near_terms, ('x', 'y'), 0, 0)  6.35 us
    pallas_call x1, Pallas kernels, near_half(): pl.pallas_call(near_kernel, grid_spec=pltpu.PrefetchScalarGridSpec(num_sc...  4.83 us
    pallas_call x4, Pallas kernels, whole(): pl.pallas_call(kernel, in_specs=specs or [VMEM] * len(ins), out_specs=out...  3.2 us
  transfers between devices with their start and end apart: 7, of which 6 were waited for; matrix products, arithmetic and copies ran while one was open for 2% of the time, Pallas kernels for 9%

profile of v5, /device:TPU:2, one launch (start us, length us, event | category | flops | bytes accessed | tf_op | source)
XLA Modules:
  0.0 88.2 jit_solution(15215758568782984408)
XLA Ops:
  0.0 9.1 %collective-permute-start = (bf16[1,128,256]{2,1,0:T(8,128)(2,1)}, bf16[1,128,256]{2,1,0:T(8,128)(2,1)S(1)}, u32[]{:S(2)}, u32[]{:S(2)}) collective-permute-start(bf16[1,128,256]{2,1,0:T(8,128)(2,1)} %bitcast.7), channel_id=1, source_target_pairs={{0,256},{64,320},{128,384},{192,448},{256,0},{320,64},{384,128},{4... | collective-permute-start | bytes 196616 | tf_op jit(solution)/shard_map/ppermute | solution.py:204
  9.1 0.1 pad.11.clone
  9.2 0.7 or_bitcast_fusion
  9.9 0.7 add_add_fusion.table_ref
  10.6 0.8 copy-done.1
  11.4 4.3 %collective-permute-done = bf16[1,128,256]{2,1,0:T(8,128)(2,1)S(1)} collective-permute-done((bf16[1,128,256]{2,1,0:T(8,128)(2,1)}, bf16[1,128,256]{2,1,0:T(8,128)(2,1)S(1)}, u32[]{:S(2)}, u32[]{:S(2)}) %collective-permute-start) | collective-permute-done | bytes 65568 | tf_op jit(solution)/shard_map/ppermute | solution.py:204
  15.8 2.4 %collective-permute-start.1 = (bf16[2,128,256]{2,1,0:T(8,128)(2,1)S(1)}, bf16[2,128,256]{2,1,0:T(8,128)(2,1)S(1)}, u32[]{:S(2)}, u32[]{:S(2)}) collective-permute-start(bf16[2,128,256]{2,1,0:T(8,128)(2,1)S(1)} %pad_maximum_fusion.2), channel_id=1, source_target_pairs={{0,128},{64,192},{128,0},{192,64},{256,384},{320,448},{384,256},{4... | collective-permute-start | bytes 393224 | tf_op jit(solution)/shard_map/ppermute | solution.py:204
  18.1 3.1 %far_lhs.1.lhs_ref = bf16[16,128,512]{2,1,0:T(8,128)(2,1)S(1)} custom-call(s32[6,32]{1,0:T(8,128)S(1)} %add_add_fusion.table_ref, bf16[16,2,4,128,128]{4,3,2,1,0:T(8,128)(2,1)} %bitcast.10), custom_call_target="tpu_custom_call" | custom-call | bytes 4194304 | tf_op jit(solution)/shard_map/far_lhs/pallas_call | solution.py:72
  21.3 3.8 %collective-permute-done.1 = bf16[2,128,256]{2,1,0:T(8,128)(2,1)S(1)} collective-permute-done((bf16[2,128,256]{2,1,0:T(8,128)(2,1)S(1)}, bf16[2,128,256]{2,1,0:T(8,128)(2,1)S(1)}, u32[]{:S(2)}, u32[]{:S(2)}) %collective-permute-start.1) | collective-permute-done | bytes 131104 | tf_op jit(solution)/shard_map/ppermute | solution.py:204
  25.1 1.9 %collective-permute-start.2 = (bf16[4,128,256]{2,1,0:T(8,128)(2,1)S(1)}, bf16[4,128,256]{2,1,0:T(8,128)(2,1)S(1)}, u32[]{:S(2)}, u32[]{:S(2)}) collective-permute-start(bf16[4,128,256]{2,1,0:T(8,128)(2,1)S(1)} %pad_maximum_fusion.1), channel_id=1, source_target_pairs={{0,64},{64,0},{128,192},{192,128},{256,320},{320,256},{384,448},{4... | collective-permute-start | bytes 786440 | tf_op jit(solution)/shard_map/ppermute | solution.py:204
  27.0 6.5 %collective-permute-done.2 = bf16[4,128,256]{2,1,0:T(8,128)(2,1)S(1)} collective-permute-done((bf16[4,128,256]{2,1,0:T(8,128)(2,1)S(1)}, bf16[4,128,256]{2,1,0:T(8,128)(2,1)S(1)}, u32[]{:S(2)}, u32[]{:S(2)}) %collective-permute-start.2) | collective-permute-done | bytes 262176 | tf_op jit(solution)/shard_map/ppermute | solution.py:204
  33.5 0.1 pad_maximum_fusion.near_ref
  33.6 1.9 %collective-permute-start.3 = (bf16[8,128,256]{2,1,0:T(8,128)(2,1)S(1)}, bf16[8,128,256]{2,1,0:T(8,128)(2,1)S(1)}, u32[]{:S(2)}, u32[]{:S(2)}) collective-permute-start(bf16[8,128,256]{2,1,0:T(8,128)(2,1)S(1)} %pad_maximum_fusion.near_ref), channel_id=1, source_target_pairs={{0,32},{32,0},{1,33},{33,1},{2,34},{34,2},{3,35},{35,3},{4,36},{36... | collective-permute-start | bytes 1572872 | tf_op jit(solution)/shard_map/ppermute | solution.py:215
  35.5 1.9 %collective-permute-done.3.across_ref = bf16[8,128,256]{2,1,0:T(8,128)(2,1)S(1)} collective-permute-done((bf16[8,128,256]{2,1,0:T(8,128)(2,1)S(1)}, bf16[8,128,256]{2,1,0:T(8,128)(2,1)S(1)}, u32[]{:S(2)}, u32[]{:S(2)}) %collective-permute-start.3) | collective-permute-done | bytes 524320 | tf_op jit(solution)/shard_map/ppermute | solution.py:215
  37.4 2.1 %far_terms.1 = (bf16[16,128,256]{2,1,0:T(8,128)(2,1)S(1)}, bf16[16,128,256]{2,1,0:T(8,128)(2,1)}) custom-call(s32[6,32]{1,0:T(8,128)S(1)} %add_add_fusion.table_ref, bf16[16,128,512]{2,1,0:T(8,128)(2,1)S(1)} %far_lhs.1.lhs_ref, bf16[8,128,256]{2,1,0:T(8,128)(2,1)S(1)} %pad_maximum_fusion.near_ref, bf16[8,128,256]{2,1,0:T(8,128)(2,1)S(1)} %collective-permute-done.3.across_ref), custom_call_target="tpu_custom_call" | custom-call | flops 536870912 | bytes 4194304 | tf_op jit(solution)/shard_map/far_terms/pallas_call | solution.py:27
  39.5 7.5 %all-to-all-start.1 = ((bf16[16,128,256]{2,1,0:T(8,128)(2,1)}), bf16[16,128,256]{2,1,0:T(8,128)(2,1)S(1)}, u32[]{:S(2)}, u32[]{:S(2)}) async-start(bf16[16,128,256]{2,1,0:T(8,128)(2,1)} %get-tuple-element.16), calls=%async_computation.1 | async-start | bytes 2097152 | tf_op jit(solution)/shard_map/all_to_all | solution.py:230
  47.0 0.0 copy-start.2
  47.0 4.8 %near_terms.1 = bf16[16,128,256]{2,1,0:T(8,128)(2,1)} custom-call(s32[6,32]{1,0:T(8,128)S(1)} %add_add_fusion.table_ref, bf16[16,2,4,128,128]{4,3,2,1,0:T(8,128)(2,1)} %bitcast.11, bf16[16,128,256]{2,1,0:T(8,128)(2,1)S(1)} %get-tuple-element.15.stripe_ref), custom_call_target="tpu_custom_call" | custom-call | flops 536870912 | bytes 4194304 | tf_op jit(solution)/shard_map/near_terms/pallas_call | solution.py:126
  51.8 10.5 %all-to-all-done.1.parts_ref = bf16[16,128,256]{2,1,0:T(8,128)(2,1)S(1)} async-done(((bf16[16,128,256]{2,1,0:T(8,128)(2,1)}), bf16[16,128,256]{2,1,0:T(8,128)(2,1)S(1)}, u32[]{:S(2)}, u32[]{:S(2)}) %all-to-all-start.1) | async-done | bytes 1048608 | tf_op jit(solution)/shard_map/all_to_all | solution.py:230
  62.3 6.3 %all-to-all-start = ((bf16[16,128,256]{2,1,0:T(8,128)(2,1)}), bf16[16,128,256]{2,1,0:T(8,128)(2,1)S(1)}, u32[]{:S(2)}, u32[]{:S(2)}) async-start(bf16[16,128,256]{2,1,0:T(8,128)(2,1)} %near_terms.1), calls=%async_computation | async-start | bytes 2097152 | tf_op jit(solution)/shard_map/all_to_all | solution.py:231
  68.7 0.1 send.1
  68.8 16.1 %collective-permute-start.4 = (bf16[128,256]{1,0:T(8,128)(2,1)S(1)}, bf16[128,256]{1,0:T(8,128)(2,1)S(1)}, u32[]{:S(2)}, u32[]{:S(2)}) collective-permute-start(bf16[128,256]{1,0:T(8,128)(2,1)S(1)} %send.1), channel_id=1, source_target_pairs={{0,1},{1,0},{2,3},{3,2},{4,5},{5,4},{6,7},{7,6},{8,9},{9,8},{10,11... | collective-permute-start | bytes 196616 | tf_op jit(solution)/shard_map/ppermute | solution.py:233
  84.9 2.3 %collective-permute-done.4.other_ref = bf16[128,256]{1,0:T(8,128)(2,1)S(1)} collective-permute-done((bf16[128,256]{1,0:T(8,128)(2,1)S(1)}, bf16[128,256]{1,0:T(8,128)(2,1)S(1)}, u32[]{:S(2)}, u32[]{:S(2)}) %collective-permute-start.4) | collective-permute-done | bytes 65568 | tf_op jit(solution)/shard_map/ppermute | solution.py:233
  87.2 0.9 %finish.1 = bf16[128,256]{1,0:T(8,128)(2,1)} custom-call(bf16[16,128,256]{2,1,0:T(8,128)(2,1)S(1)} %all-to-all-done.parts_ref, bf16[128,256]{1,0:T(8,128)(2,1)S(1)} %collective-permute-done.4.other_ref, bf16[256,256]{1,0:T(8,128)(2,1)S(1)} %copy-done, f32[1,256]{1,0:T(1,128)S(1)} %bitcast.9), custom_call_target="tpu_custom_call" | custom-call | flops 16777216 | bytes 2097152 | tf_op jit(solution)/shard_map/finish/pallas_call | solution.py:27
  (8 shorter events, 0.1 us)
Async XLA Ops:
  0.0 15.7 %collective-permute-start = (bf16[1,128,256]{2,1,0:T(8,128)(2,1)}, bf16[1,128,256]{2,1,0:T(8,128)(2,1)S(1)}, u32[]{:S(2)}, u32[]{:S(2)}) collective-permute-start(bf16[1,128,256]{2,1,0:T(8,128)(2,1)} %bitcast.7), channel_id=1, source_target_pairs={{0,256},{64,320},{128,384},{192,448},{256,0},{320,64},{384,128},{4... | collective-permute-start | bytes 196616 | tf_op jit(solution)/shard_map/ppermute | solution.py:204
  10.6 0.8 copy-start.1
  15.8 9.3 %collective-permute-start.1 = (bf16[2,128,256]{2,1,0:T(8,128)(2,1)S(1)}, bf16[2,128,256]{2,1,0:T(8,128)(2,1)S(1)}, u32[]{:S(2)}, u32[]{:S(2)}) collective-permute-start(bf16[2,128,256]{2,1,0:T(8,128)(2,1)S(1)} %pad_maximum_fusion.2), channel_id=1, source_target_pairs={{0,128},{64,192},{128,0},{192,64},{256,384},{320,448},{384,256},{4... | collective-permute-start | bytes 393224 | tf_op jit(solution)/shard_map/ppermute | solution.py:204
  25.1 8.4 %collective-permute-start.2 = (bf16[4,128,256]{2,1,0:T(8,128)(2,1)S(1)}, bf16[4,128,256]{2,1,0:T(8,128)(2,1)S(1)}, u32[]{:S(2)}, u32[]{:S(2)}) collective-permute-start(bf16[4,128,256]{2,1,0:T(8,128)(2,1)S(1)} %pad_maximum_fusion.1), channel_id=1, source_target_pairs={{0,64},{64,0},{128,192},{192,128},{256,320},{320,256},{384,448},{4... | collective-permute-start | bytes 786440 | tf_op jit(solution)/shard_map/ppermute | solution.py:204
  33.6 3.8 %collective-permute-start.3 = (bf16[8,128,256]{2,1,0:T(8,128)(2,1)S(1)}, bf16[8,128,256]{2,1,0:T(8,128)(2,1)S(1)}, u32[]{:S(2)}, u32[]{:S(2)}) collective-permute-start(bf16[8,128,256]{2,1,0:T(8,128)(2,1)S(1)} %pad_maximum_fusion.near_ref), channel_id=1, source_target_pairs={{0,32},{32,0},{1,33},{33,1},{2,34},{34,2},{3,35},{35,3},{4,36},{36... | collective-permute-start | bytes 1572872 | tf_op jit(solution)/shard_map/ppermute | solution.py:215
  39.5 22.8 %all-to-all-start.1 = ((bf16[16,128,256]{2,1,0:T(8,128)(2,1)}), bf16[16,128,256]{2,1,0:T(8,128)(2,1)S(1)}, u32[]{:S(2)}, u32[]{:S(2)}) async-start(bf16[16,128,256]{2,1,0:T(8,128)(2,1)} %get-tuple-element.16), calls=%async_computation.1 | async-start | bytes 2097152 | tf_op jit(solution)/shard_map/all_to_all | solution.py:230
  47.0 40.2 %copy-start = (bf16[256,256]{1,0:T(8,128)(2,1)S(1)}, bf16[256,256]{1,0:T(8,128)(2,1)}, u32[]{:S(2)}) copy-start(bf16[256,256]{1,0:T(8,128)(2,1)} %weight_ref.1) | copy-start | bytes 393220
  47.0 40.2 %copy-start.2 = (f32[256]{0:T(256)S(1)}, f32[256]{0:T(256)}, u32[]{:S(2)}) copy-start(f32[256]{0:T(256)} %param.11) | copy-start | bytes 3076
  62.3 22.6 %all-to-all-start = ((bf16[16,128,256]{2,1,0:T(8,128)(2,1)}), bf16[16,128,256]{2,1,0:T(8,128)(2,1)S(1)}, u32[]{:S(2)}, u32[]{:S(2)}) async-start(bf16[16,128,256]{2,1,0:T(8,128)(2,1)} %near_terms.1), calls=%async_computation | async-start | bytes 2097152 | tf_op jit(solution)/shard_map/all_to_all | solution.py:231
  68.8 18.4 %collective-permute-start.4 = (bf16[128,256]{1,0:T(8,128)(2,1)S(1)}, bf16[128,256]{1,0:T(8,128)(2,1)S(1)}, u32[]{:S(2)}, u32[]{:S(2)}) collective-permute-start(bf16[128,256]{1,0:T(8,128)(2,1)S(1)} %send.1), channel_id=1, source_target_pairs={{0,1},{1,0},{2,3},{3,2},{4,5},{5,4},{6,7},{7,6},{8,9},{9,8},{10,11... | collective-permute-start | bytes 196616 | tf_op jit(solution)/shard_map/ppermute | solution.py:233

commit v6 on v5

--- a/solution.py
+++ b/solution.py
@@ -7,7 +7,7 @@
 
 ZL, CORE, X, Y, ZH = 8, 2, 4, 4, 2
 SLOTS, BS, F = 4, 128, 256
-COUNT, HALF = SLOTS, SLOTS + 1
+COUNT, HALF, SIDE, PLACE = range(SLOTS, SLOTS + 4)
 VMEM = pl.BlockSpec(memory_space=pltpu.VMEM)
 SMEM = pl.BlockSpec(memory_space=pltpu.SMEM)
 ANY = pl.BlockSpec(memory_space=pl.ANY)
@@ -112,40 +112,24 @@
         store.wait()
 
 
-def near_kernel(table_ref, blocks_ref, stripe_ref, out_ref):
-    step = blocks_ref.shape[0]
-    base = pl.program_id(0) * step
-    for i in range(step):
-        row = 2 * (base + i) + table_ref[HALF, 0]
-        lhs = side_by_side(table_ref, row, lambda k: blocks_ref[i, 0, k])
-        out_ref[i] = product(table_ref, row, lhs, stripe_ref)
-
-
-def near_half(table, blocks, stripe):
-    step = 4
-    return pl.pallas_call(
-        near_kernel,
-        grid_spec=pltpu.PrefetchScalarGridSpec(
-            num_scalar_prefetch=1,
-            grid=(X * Y // step,),
-            in_specs=[
-                pl.BlockSpec(
-                    (step, 1, SLOTS, BS, BS),
-                    lambda i, table_ref: (i, table_ref[HALF, 0], 0, 0, 0),
-                ),
-                VMEM,
-            ],
-            out_specs=pl.BlockSpec((step, BS, F), lambda i, *_: (i, 0, 0)),
-        ),
-        out_shape=jax.ShapeDtypeStruct((X * Y, BS, F), jnp.bfloat16),
-        compiler_params=pltpu.CompilerParams(vmem_limit_bytes=8 << 20),
-        cost_estimate=pl.CostEstimate(
-            flops=2 * X * Y * SLOTS * BS * BS * F,
-            bytes_accessed=4 << 20,
-            transcendentals=0,
-        ),
-        name="near_terms",
-    )(table, blocks, stripe)
+def near_kernel(table_ref, blocks_ref, stripe_ref, *refs):
+    outs, (held, sem) = refs[:X], refs[X:]
+    zh, side, place = (table_ref[i, 0] for i in (HALF, SIDE, PLACE))
+    loads = [
+        pltpu.make_async_copy(blocks_ref.at[j, zh], held.at[j], sem.at[j])
+        for j in range(X * Y)
+    ]
+    for load in loads:
+        load.start()
+    for load in loads:
+        load.wait()
+    for d in range(X):
+        k = (place + d) % X
+        for m in range(Y):
+            j = jnp.where(side == 0, k * Y + m, m * Y + k)
+            row = 2 * j + zh
+            lhs = side_by_side(table_ref, row, lambda s: held[j, s])
+            outs[d][m] = product(table_ref, row, lhs, stripe_ref)
 
 
 def total(parts):
@@ -159,10 +143,18 @@
     out_ref[...] = total([parts_ref[k] for k in range(X * Y)]).astype(jnp.bfloat16)
 
 
+def near_sum_kernel(*refs):
+    parts, out_ref = refs[:-1], refs[-1]
+    for m in range(Y):
+        out_ref[m] = total([part[m] for part in parts]).astype(jnp.bfloat16)
+
+
+def widen_kernel(in_ref, out_ref):
+    out_ref[...] = in_ref[...].astype(jnp.float32)
+
+
 def finish_kernel(parts_ref, other_ref, weight_ref, bias_ref, out_ref):
-    summed = total([parts_ref[k] for k in range(X * Y)]) + other_ref[...].astype(
-        jnp.float32
-    )
+    summed = total([parts_ref[k] for k in range(Y)]) + other_ref[...]
     hidden = jnp.dot(
         summed.astype(jnp.bfloat16),
         weight_ref[...],
@@ -183,7 +175,22 @@
         | ((offset << 3) & 8)
     )
     counts = row_count.T
-    return jnp.concatenate([spots, counts, jnp.full_like(counts, zh)], axis=0)
+    place = jnp.where(core == 0, lax.axis_index("x"), lax.axis_index("y"))
+    return jnp.concatenate(
+        [spots, counts] + [jnp.full_like(counts, v) for v in (zh, core, place)], axis=0
+    )
+
+
+def along(first):
+    by_x = [[x * Y + y for x in range(X)] for y in range(Y)]
+    by_y = [[x * Y + y for y in range(Y)] for x in range(X)]
+    sides = (by_x, by_y) if first else (by_y, by_x)
+    return [[c * X * Y + i for i in g] for c, gs in enumerate(sides) for g in gs]
+
+
+def pass_on(value, d):
+    pairs = [(g[i], g[(i + d) % X]) for g in along(True) for i in range(X)]
+    return lax.ppermute(value, ("core", "x", "y"), pairs)
 
 
 def local(features, blocks, block_col, row_count, weight, out_bias):
@@ -226,11 +233,35 @@
         out_specs=[VMEM, ANY],
         scratch=[pltpu.VMEM(half, bf16), pltpu.SemaphoreType.DMA((4,))],
     )
-    near_terms = near_half(table, blocks, stripe)
     far_parts = lax.all_to_all(far_terms, ("x", "y"), 0, 0)
-    near_parts = lax.all_to_all(near_terms, ("x", "y"), 0, 0)
+    quarter = jax.ShapeDtypeStruct((Y, BS, F), bf16)
+    near_terms = whole(
+        near_kernel,
+        [table, blocks, stripe],
+        [quarter] * X,
+        "near_terms",
+        (2 * X * Y * SLOTS * BS * BS * F, 4 << 20),
+        limit=6 << 20,
+        specs=[SMEM, ANY, VMEM],
+        scratch=[
+            pltpu.VMEM((X * Y, SLOTS, BS, BS), bf16),
+            pltpu.SemaphoreType.DMA((X * Y,)),
+        ],
+    )
+    near = [near_terms[0]] + [pass_on(near_terms[d], d) for d in range(1, X)]
     send = whole(send_kernel, [far_parts], one, "send", (0, 1 << 20))
     other = lax.ppermute(send, "zh", [(0, 1), (1, 0)])
+    near = whole(near_sum_kernel, near, quarter, "near_sum", (0, 1 << 20))
+    near_parts = lax.all_to_all(
+        near, ("core", "x", "y"), 0, 0, axis_index_groups=along(False)
+    )
+    other = whole(
+        widen_kernel,
+        [other],
+        jax.ShapeDtypeStruct((BS, F), jnp.float32),
+        "widen",
+        (1 << 35, 1 << 26),
+    )
     return whole(
         finish_kernel,
         [near_parts, other, weight, out_bias[None]],

time: 88.7 us -> 92.3 us (1.041)
  the two profiles are of different devices: /device:TPU:2 before, /device:TPU:8 now
where the time goes in v6:
time: 92.3 us; the launch traced here: 91.6 us
  starting transfers between devices  54.8 us (59%)
  waiting for transfers between devices  24.2 us (26%)
  Pallas kernels  10.1 us (11%)
  local copies, waits for them, and re-layouts  1.53 us (2%)
    ppermute x1, starting transfers between devices, local(): other = lax.ppermute(send, 'zh', [(0, 1), (1, 0)])  16.1 us
    ppermute x3, waiting for transfers between devices, local(): lax.ppermute(features[None] if bit == 4 else held, 'zl', [(z, z ^ bit) fo...  14.7 us
    ppermute x3, starting transfers between devices, local(): lax.ppermute(features[None] if bit == 4 else held, 'zl', [(z, z ^ bit) fo...  13.4 us
    ppermute x3, starting transfers between devices, pass_on(): return lax.ppermute(value, ('core', 'x', 'y'), pairs)  11.3 us
    all_to_all x1, starting transfers between devices, local(): far_parts = lax.all_to_all(far_terms, ('x', 'y'), 0, 0)  7.4 us
    pallas_call x7, Pallas kernels, whole(): pl.pallas_call(kernel, in_specs=specs or [VMEM] * len(ins), out_specs=out...  7.03 us
    all_to_all x1, waiting for transfers between devices, local(): lax.all_to_all(near, ('core', 'x', 'y'), 0, 0, axis_index_groups=along(Fa...  5.2 us
    all_to_all x1, starting transfers between devices, local(): lax.all_to_all(near, ('core', 'x', 'y'), 0, 0, axis_index_groups=along(Fa...  4.65 us
  transfers between devices with their start and end apart: 10, of which 6 were waited for; matrix products, arithmetic and copies ran while one was open for 2% of the time, Pallas kernels for 8%

profile of v6, /device:TPU:8, one launch (start us, length us, event | category | flops | bytes accessed | tf_op | source)
XLA Modules:
  0.0 91.6 jit_solution(1405289736171124456)
XLA Ops:
  0.0 9.1 %collective-permute-start = (bf16[1,128,256]{2,1,0:T(8,128)(2,1)}, bf16[1,128,256]{2,1,0:T(8,128)(2,1)S(1)}, u32[]{:S(2)}, u32[]{:S(2)}) collective-permute-start(bf16[1,128,256]{2,1,0:T(8,128)(2,1)} %bitcast.6), channel_id=1, source_target_pairs={{0,256},{64,320},{128,384},{192,448},{256,0},{320,64},{384,128},{4... | collective-permute-start | bytes 196616 | tf_op jit(solution)/shard_map/ppermute | solution.py:211
  9.1 0.7 or_bitcast_fusion
  9.8 0.8 copy-done.1
  10.7 0.7 concatenate.14.table_ref
  11.3 4.4 %collective-permute-done = bf16[1,128,256]{2,1,0:T(8,128)(2,1)S(1)} collective-permute-done((bf16[1,128,256]{2,1,0:T(8,128)(2,1)}, bf16[1,128,256]{2,1,0:T(8,128)(2,1)S(1)}, u32[]{:S(2)}, u32[]{:S(2)}) %collective-permute-start) | collective-permute-done | bytes 65568 | tf_op jit(solution)/shard_map/ppermute | solution.py:211
  15.8 2.4 %collective-permute-start.1 = (bf16[2,128,256]{2,1,0:T(8,128)(2,1)S(1)}, bf16[2,128,256]{2,1,0:T(8,128)(2,1)S(1)}, u32[]{:S(2)}, u32[]{:S(2)}) collective-permute-start(bf16[2,128,256]{2,1,0:T(8,128)(2,1)S(1)} %pad_maximum_fusion.2), channel_id=1, source_target_pairs={{0,128},{64,192},{128,0},{192,64},{256,384},{320,448},{384,256},{4... | collective-permute-start | bytes 393224 | tf_op jit(solution)/shard_map/ppermute | solution.py:211
  18.1 3.1 %far_lhs.1.lhs_ref = bf16[16,128,512]{2,1,0:T(8,128)(2,1)S(1)} custom-call(s32[8,32]{1,0:T(8,128)S(1)} %concatenate.14.table_ref, bf16[16,2,4,128,128]{4,3,2,1,0:T(8,128)(2,1)} %bitcast.9), custom_call_target="tpu_custom_call" | custom-call | bytes 4194304 | tf_op jit(solution)/shard_map/far_lhs/pallas_call | solution.py:72
  21.3 3.8 %collective-permute-done.1 = bf16[2,128,256]{2,1,0:T(8,128)(2,1)S(1)} collective-permute-done((bf16[2,128,256]{2,1,0:T(8,128)(2,1)S(1)}, bf16[2,128,256]{2,1,0:T(8,128)(2,1)S(1)}, u32[]{:S(2)}, u32[]{:S(2)}) %collective-permute-start.1) | collective-permute-done | bytes 131104 | tf_op jit(solution)/shard_map/ppermute | solution.py:211
  25.1 1.9 %collective-permute-start.2 = (bf16[4,128,256]{2,1,0:T(8,128)(2,1)S(1)}, bf16[4,128,256]{2,1,0:T(8,128)(2,1)S(1)}, u32[]{:S(2)}, u32[]{:S(2)}) collective-permute-start(bf16[4,128,256]{2,1,0:T(8,128)(2,1)S(1)} %pad_maximum_fusion.1), channel_id=1, source_target_pairs={{0,64},{64,0},{128,192},{192,128},{256,320},{320,256},{384,448},{4... | collective-permute-start | bytes 786440 | tf_op jit(solution)/shard_map/ppermute | solution.py:211
  27.0 6.5 %collective-permute-done.2 = bf16[4,128,256]{2,1,0:T(8,128)(2,1)S(1)} collective-permute-done((bf16[4,128,256]{2,1,0:T(8,128)(2,1)S(1)}, bf16[4,128,256]{2,1,0:T(8,128)(2,1)S(1)}, u32[]{:S(2)}, u32[]{:S(2)}) %collective-permute-start.2) | collective-permute-done | bytes 262176 | tf_op jit(solution)/shard_map/ppermute | solution.py:211
  33.6 1.9 %collective-permute-start.3 = (bf16[8,128,256]{2,1,0:T(8,128)(2,1)S(1)}, bf16[8,128,256]{2,1,0:T(8,128)(2,1)S(1)}, u32[]{:S(2)}, u32[]{:S(2)}) collective-permute-start(bf16[8,128,256]{2,1,0:T(8,128)(2,1)S(1)} %pad_maximum_fusion.near_ref), channel_id=1, source_target_pairs={{0,32},{32,0},{1,33},{33,1},{2,34},{34,2},{3,35},{35,3},{4,36},{36... | collective-permute-start | bytes 1572872 | tf_op jit(solution)/shard_map/ppermute | solution.py:222
  35.5 1.9 %collective-permute-done.3.across_ref = bf16[8,128,256]{2,1,0:T(8,128)(2,1)S(1)} collective-permute-done((bf16[8,128,256]{2,1,0:T(8,128)(2,1)S(1)}, bf16[8,128,256]{2,1,0:T(8,128)(2,1)S(1)}, u32[]{:S(2)}, u32[]{:S(2)}) %collective-permute-start.3) | collective-permute-done | bytes 524320 | tf_op jit(solution)/shard_map/ppermute | solution.py:222
  37.4 2.1 %far_terms.1 = (bf16[16,128,256]{2,1,0:T(8,128)(2,1)S(1)}, bf16[16,128,256]{2,1,0:T(8,128)(2,1)}) custom-call(s32[8,32]{1,0:T(8,128)S(1)} %concatenate.14.table_ref, bf16[16,128,512]{2,1,0:T(8,128)(2,1)S(1)} %far_lhs.1.lhs_ref, bf16[8,128,256]{2,1,0:T(8,128)(2,1)S(1)} %pad_maximum_fusion.near_ref, bf16[8,128,256]{2,1,0:T(8,128)(2,1)S(1)} %collective-permute-done.3.across_ref), custom_call_target="tpu_custom_call" | custom-call | flops 536870912 | bytes 4194304 | tf_op jit(solution)/shard_map/far_terms/pallas_call | solution.py:27
  39.5 7.4 %all-to-all-start.1 = ((bf16[16,128,256]{2,1,0:T(8,128)(2,1)}), bf16[16,128,256]{2,1,0:T(8,128)(2,1)S(1)}, u32[]{:S(2)}, u32[]{:S(2)}) async-start(bf16[16,128,256]{2,1,0:T(8,128)(2,1)} %get-tuple-element.24), calls=%async_computation.1 | async-start | bytes 2097152 | tf_op jit(solution)/shard_map/all_to_all | solution.py:236
  46.9 3.1 %near_terms.1 = (bf16[4,128,256]{2,1,0:T(8,128)(2,1)S(1)}, bf16[4,128,256]{2,1,0:T(8,128)(2,1)S(1)}, bf16[4,128,256]{2,1,0:T(8,128)(2,1)S(1)}, bf16[4,128,256]{2,1,0:T(8,128)(2,1)S(1)}) custom-call(s32[8,32]{1,0:T(8,128)S(1)} %concatenate.14.table_ref, bf16[16,2,4,128,128]{4,3,2,1,0:T(8,128)(2,1)} %bitcast.10, ...), custom_call_target="tpu_custom_call" | custom-call | flops 536870912 | bytes 4194304 | tf_op jit(solution)/shard_map/near_terms/pallas_call | solution.py:27
  50.0 3.4 %collective-permute-start.4 = (bf16[4,128,256]{2,1,0:T(8,128)(2,1)S(1)}, bf16[4,128,256]{2,1,0:T(8,128)(2,1)S(1)}, u32[]{:S(2)}, u32[]{:S(2)}) collective-permute-start(bf16[4,128,256]{2,1,0:T(8,128)(2,1)S(1)} %get-tuple-element.21), channel_id=1, source_target_pairs={{0,8},{8,16},{16,24},{24,0},{2,10},{10,18},{18,26},{26,2},{4,12},{... | collective-permute-start | bytes 786440 | tf_op jit(solution)/shard_map/ppermute | solution.py:193
  53.4 4.6 %collective-permute-start.5 = (bf16[4,128,256]{2,1,0:T(8,128)(2,1)S(1)}, bf16[4,128,256]{2,1,0:T(8,128)(2,1)S(1)}, u32[]{:S(2)}, u32[]{:S(2)}) collective-permute-start(bf16[4,128,256]{2,1,0:T(8,128)(2,1)S(1)} %get-tuple-element.22), channel_id=1, source_target_pairs={{0,16},{8,24},{16,0},{24,8},{2,18},{10,26},{18,2},{26,10},{4,20},{... | collective-permute-start | bytes 786440 | tf_op jit(solution)/shard_map/ppermute | solution.py:193
  58.0 3.4 %collective-permute-start.6 = (bf16[4,128,256]{2,1,0:T(8,128)(2,1)S(1)}, bf16[4,128,256]{2,1,0:T(8,128)(2,1)S(1)}, u32[]{:S(2)}, u32[]{:S(2)}) collective-permute-start(bf16[4,128,256]{2,1,0:T(8,128)(2,1)S(1)} %get-tuple-element.23), channel_id=1, source_target_pairs={{0,24},{8,0},{16,8},{24,16},{2,26},{10,2},{18,10},{26,18},{4,28},{... | collective-permute-start | bytes 786440 | tf_op jit(solution)/shard_map/ppermute | solution.py:193
  61.4 2.5 %all-to-all-done.1.parts_ref = bf16[16,128,256]{2,1,0:T(8,128)(2,1)S(1)} async-done(((bf16[16,128,256]{2,1,0:T(8,128)(2,1)}), bf16[16,128,256]{2,1,0:T(8,128)(2,1)S(1)}, u32[]{:S(2)}, u32[]{:S(2)}) %all-to-all-start.1) | async-done | bytes 1048608 | tf_op jit(solution)/shard_map/all_to_all | solution.py:236
  64.0 16.1 %collective-permute-start.7 = (bf16[128,256]{1,0:T(8,128)(2,1)S(1)}, bf16[128,256]{1,0:T(8,128)(2,1)S(1)}, u32[]{:S(2)}, u32[]{:S(2)}) collective-permute-start(bf16[128,256]{1,0:T(8,128)(2,1)S(1)} %send.1), channel_id=1, source_target_pairs={{0,1},{1,0},{2,3},{3,2},{4,5},{5,4},{6,7},{7,6},{8,9},{9,8},{10,11... | collective-permute-start | bytes 196616 | tf_op jit(solution)/shard_map/ppermute | solution.py:253
  80.1 0.8 near_sum.1
  80.9 4.6 %all-to-all-start = ((bf16[4,128,256]{2,1,0:T(8,128)(2,1)}), bf16[4,128,256]{2,1,0:T(8,128)(2,1)S(1)}, u32[]{:S(2)}, u32[]{:S(2)}) async-start(bf16[4,128,256]{2,1,0:T(8,128)(2,1)} %near_sum.1), calls=%async_computation | async-start | bytes 524288 | tf_op jit(solution)/shard_map/all_to_all | solution.py:255
  85.6 5.2 %all-to-all-done.parts_ref = bf16[4,128,256]{2,1,0:T(8,128)(2,1)S(1)} async-done(((bf16[4,128,256]{2,1,0:T(8,128)(2,1)}), bf16[4,128,256]{2,1,0:T(8,128)(2,1)S(1)}, u32[]{:S(2)}, u32[]{:S(2)}) %all-to-all-start) | async-done | bytes 262176 | tf_op jit(solution)/shard_map/all_to_all | solution.py:255
  90.8 0.8 finish.1
  (18 shorter events, 0.3 us)
Async XLA Ops:
  0.0 15.7 %collective-permute-start = (bf16[1,128,256]{2,1,0:T(8,128)(2,1)}, bf16[1,128,256]{2,1,0:T(8,128)(2,1)S(1)}, u32[]{:S(2)}, u32[]{:S(2)}) collective-permute-start(bf16[1,128,256]{2,1,0:T(8,128)(2,1)} %bitcast.6), channel_id=1, source_target_pairs={{0,256},{64,320},{128,384},{192,448},{256,0},{320,64},{384,128},{4... | collective-permute-start | bytes 196616 | tf_op jit(solution)/shard_map/ppermute | solution.py:211
  9.8 0.8 copy-start.1
  15.8 9.3 %collective-permute-start.1 = (bf16[2,128,256]{2,1,0:T(8,128)(2,1)S(1)}, bf16[2,128,256]{2,1,0:T(8,128)(2,1)S(1)}, u32[]{:S(2)}, u32[]{:S(2)}) collective-permute-start(bf16[2,128,256]{2,1,0:T(8,128)(2,1)S(1)} %pad_maximum_fusion.2), channel_id=1, source_target_pairs={{0,128},{64,192},{128,0},{192,64},{256,384},{320,448},{384,256},{4... | collective-permute-start | bytes 393224 | tf_op jit(solution)/shard_map/ppermute | solution.py:211
  25.1 8.4 %collective-permute-start.2 = (bf16[4,128,256]{2,1,0:T(8,128)(2,1)S(1)}, bf16[4,128,256]{2,1,0:T(8,128)(2,1)S(1)}, u32[]{:S(2)}, u32[]{:S(2)}) collective-permute-start(bf16[4,128,256]{2,1,0:T(8,128)(2,1)S(1)} %pad_maximum_fusion.1), channel_id=1, source_target_pairs={{0,64},{64,0},{128,192},{192,128},{256,320},{320,256},{384,448},{4... | collective-permute-start | bytes 786440 | tf_op jit(solution)/shard_map/ppermute | solution.py:211
  33.6 3.8 %collective-permute-start.3 = (bf16[8,128,256]{2,1,0:T(8,128)(2,1)S(1)}, bf16[8,128,256]{2,1,0:T(8,128)(2,1)S(1)}, u32[]{:S(2)}, u32[]{:S(2)}) collective-permute-start(bf16[8,128,256]{2,1,0:T(8,128)(2,1)S(1)} %pad_maximum_fusion.near_ref), channel_id=1, source_target_pairs={{0,32},{32,0},{1,33},{33,1},{2,34},{34,2},{3,35},{35,3},{4,36},{36... | collective-permute-start | bytes 1572872 | tf_op jit(solution)/shard_map/ppermute | solution.py:222
  39.5 24.4 %all-to-all-start.1 = ((bf16[16,128,256]{2,1,0:T(8,128)(2,1)}), bf16[16,128,256]{2,1,0:T(8,128)(2,1)S(1)}, u32[]{:S(2)}, u32[]{:S(2)}) async-start(bf16[16,128,256]{2,1,0:T(8,128)(2,1)} %get-tuple-element.24), calls=%async_computation.1 | async-start | bytes 2097152 | tf_op jit(solution)/shard_map/all_to_all | solution.py:236
  50.0 30.1 %collective-permute-start.4 = (bf16[4,128,256]{2,1,0:T(8,128)(2,1)S(1)}, bf16[4,128,256]{2,1,0:T(8,128)(2,1)S(1)}, u32[]{:S(2)}, u32[]{:S(2)}) collective-permute-start(bf16[4,128,256]{2,1,0:T(8,128)(2,1)S(1)} %get-tuple-element.21), channel_id=1, source_target_pairs={{0,8},{8,16},{16,24},{24,0},{2,10},{10,18},{18,26},{26,2},{4,12},{... | collective-permute-start | bytes 786440 | tf_op jit(solution)/shard_map/ppermute | solution.py:193
  53.4 26.7 %collective-permute-start.5 = (bf16[4,128,256]{2,1,0:T(8,128)(2,1)S(1)}, bf16[4,128,256]{2,1,0:T(8,128)(2,1)S(1)}, u32[]{:S(2)}, u32[]{:S(2)}) collective-permute-start(bf16[4,128,256]{2,1,0:T(8,128)(2,1)S(1)} %get-tuple-element.22), channel_id=1, source_target_pairs={{0,16},{8,24},{16,0},{24,8},{2,18},{10,26},{18,2},{26,10},{4,20},{... | collective-permute-start | bytes 786440 | tf_op jit(solution)/shard_map/ppermute | solution.py:193
  58.0 22.1 %collective-permute-start.6 = (bf16[4,128,256]{2,1,0:T(8,128)(2,1)S(1)}, bf16[4,128,256]{2,1,0:T(8,128)(2,1)S(1)}, u32[]{:S(2)}, u32[]{:S(2)}) collective-permute-start(bf16[4,128,256]{2,1,0:T(8,128)(2,1)S(1)} %get-tuple-element.23), channel_id=1, source_target_pairs={{0,24},{8,0},{16,8},{24,16},{2,26},{10,2},{18,10},{26,18},{4,28},{... | collective-permute-start | bytes 786440 | tf_op jit(solution)/shard_map/ppermute | solution.py:193
  64.0 21.6 %collective-permute-start.7 = (bf16[128,256]{1,0:T(8,128)(2,1)S(1)}, bf16[128,256]{1,0:T(8,128)(2,1)S(1)}, u32[]{:S(2)}, u32[]{:S(2)}) collective-permute-start(bf16[128,256]{1,0:T(8,128)(2,1)S(1)} %send.1), channel_id=1, source_target_pairs={{0,1},{1,0},{2,3},{3,2},{4,5},{5,4},{6,7},{7,6},{8,9},{9,8},{10,11... | collective-permute-start | bytes 196616 | tf_op jit(solution)/shard_map/ppermute | solution.py:253
  80.9 9.9 %all-to-all-start = ((bf16[4,128,256]{2,1,0:T(8,128)(2,1)}), bf16[4,128,256]{2,1,0:T(8,128)(2,1)S(1)}, u32[]{:S(2)}, u32[]{:S(2)}) async-start(bf16[4,128,256]{2,1,0:T(8,128)(2,1)} %near_sum.1), calls=%async_computation | async-start | bytes 524288 | tf_op jit(solution)/shard_map/all_to_all | solution.py:255
  85.6 5.2 %copy-start = (bf16[256,256]{1,0:T(8,128)(2,1)S(1)}, bf16[256,256]{1,0:T(8,128)(2,1)}, u32[]{:S(2)}) copy-start(bf16[256,256]{1,0:T(8,128)(2,1)} %weight_ref.1) | copy-start | bytes 393220
  85.6 5.2 %copy-start.2 = (f32[256]{0:T(256)S(1)}, f32[256]{0:T(256)}, u32[]{:S(2)}) copy-start(f32[256]{0:T(256)} %param.11) | copy-start | bytes 3076

commit v7 on v6

--- a/solution.py
+++ b/solution.py
@@ -91,11 +91,16 @@
     )(table, blocks)
 
 
-def far_kernel(
-    table_ref, lhs_ref, near_ref, across_ref, stripe_ref, out_ref, made, sem
-):
-    stripe_ref[:ZL] = near_ref[...]
-    stripe_ref[ZL:] = across_ref[...]
+def far_kernel(table_ref, lhs_ref, *refs):
+    trio, p6, ones, p7, core0, core1 = refs[:6]
+    stripe_ref, out_ref, made, sem = refs[6:]
+    near = {0: trio.at[0], 4: trio.at[1], 2: trio.at[2], 6: p6.at[0]}
+    near |= {1: ones.at[0], 5: ones.at[1], 3: ones.at[2], 7: p7.at[0]}
+    across = {d: core0.at[i] for i, d in enumerate((0, 4, 2, 6))}
+    across |= {d: core1.at[i] for i, d in enumerate((1, 5, 3, 7))}
+    for d in range(ZL):
+        stripe_ref[CORE * d] = near[d][...]
+        stripe_ref[CORE * d + 1] = across[d][...]
     group = X * Y // sem.shape[0]
     stores = []
     for g in range(sem.shape[0]):
@@ -149,12 +154,10 @@
         out_ref[m] = total([part[m] for part in parts]).astype(jnp.bfloat16)
 
 
-def widen_kernel(in_ref, out_ref):
-    out_ref[...] = in_ref[...].astype(jnp.float32)
-
-
 def finish_kernel(parts_ref, other_ref, weight_ref, bias_ref, out_ref):
-    summed = total([parts_ref[k] for k in range(Y)]) + other_ref[...]
+    summed = total([parts_ref[k] for k in range(Y)]) + other_ref[...].astype(
+        jnp.float32
+    )
     hidden = jnp.dot(
         summed.astype(jnp.bfloat16),
         weight_ref[...],
@@ -167,13 +170,7 @@
     zl, core, zh = (
         lax.axis_index(a).astype(jnp.int32) for a in ("zl", "core", "zh")
     )
-    offset = block_col.T ^ (CORE * zl + core)
-    spots = (
-        ((offset >> 3) & 1)
-        | ((offset >> 1) & 2)
-        | ((offset << 1) & 4)
-        | ((offset << 3) & 8)
-    )
+    spots = block_col.T ^ (CORE * zl + core)
     counts = row_count.T
     place = jnp.where(core == 0, lax.axis_index("x"), lax.axis_index("y"))
     return jnp.concatenate(
@@ -206,30 +203,32 @@
         "own",
         (0, 1 << 17),
     )
-    held = own
-    for bit in (4, 2, 1):
-        came = lax.ppermute(
-            features[None] if bit == 4 else held,
-            "zl",
-            [(z, z ^ bit) for z in range(ZL)],
-        )
-        if bit == 4:
-            came, table = lax.optimization_barrier((came, table))
-            far_lhs = far_lhs_rows(table, blocks)
-        if bit == 2:
-            came, far_lhs = lax.optimization_barrier((came, far_lhs))
-        held = jnp.concatenate([held, came], axis=0)
-    across = lax.ppermute(held, "core", [(0, 1), (1, 0)])
+    def hop(value, bit):
+        return lax.ppermute(value, "zl", [(z, z ^ bit) for z in range(ZL)])
+
+    def cross(value):
+        return lax.ppermute(value, "core", [(0, 1), (1, 0)])
+
+    p4, p2 = hop(features[None], 4), hop(features[None], 2)
+    p4, table = lax.optimization_barrier((p4, table))
+    p6 = hop(p4, 2)
+    far_lhs = far_lhs_rows(table, blocks)
+    trio = jnp.concatenate([own, p4, p2], axis=0)
+    ones = hop(trio, 1)
+    p6, far_lhs = lax.optimization_barrier((p6, far_lhs))
+    p7 = hop(p6, 1)
+    core0 = cross(jnp.concatenate([trio, p6], axis=0))
+    core1 = cross(jnp.concatenate([ones, p7], axis=0))
     half = (X * Y, BS, F)
     one = jax.ShapeDtypeStruct((BS, F), bf16)
     stripe, far_terms = whole(
         far_kernel,
-        [table, far_lhs, held, across],
+        [table, far_lhs, trio, p6, ones, p7, core0, core1],
         [jax.ShapeDtypeStruct(half, bf16)] * 2,
         "far_terms",
         (2 * X * Y * SLOTS * BS * BS * F, 4 << 20),
         limit=8 << 20,
-        specs=[SMEM, VMEM, VMEM, VMEM],
+        specs=[SMEM] + [VMEM] * 7,
         out_specs=[VMEM, ANY],
         scratch=[pltpu.VMEM(half, bf16), pltpu.SemaphoreType.DMA((4,))],
     )
@@ -255,13 +254,6 @@
     near_parts = lax.all_to_all(
         near, ("core", "x", "y"), 0, 0, axis_index_groups=along(False)
     )
-    other = whole(
-        widen_kernel,
-        [other],
-        jax.ShapeDtypeStruct((BS, F), jnp.float32),
-        "widen",
-        (1 << 35, 1 << 26),
-    )
     return whole(
         finish_kernel,
         [near_parts, other, weight, out_bias[None]],

time: 92.3 us -> 93.8 us (1.016)
  the two profiles are of different devices: /device:TPU:8 before, /device:TPU:7 now
where the time goes in v7:
time: 93.8 us; the launch traced here: 93.1 us
  starting transfers between devices  65.5 us (70%)
  waiting for transfers between devices  15 us (16%)
  Pallas kernels  10.2 us (11%)
  local copies, waits for them, and re-layouts  1.53 us (2%)
    ppermute x5, starting transfers between devices, hop(): return lax.ppermute(value, 'zl', [(z, z ^ bit) for z in range(ZL)])  23.8 us
    ppermute x1, starting transfers between devices, local(): other = lax.ppermute(send, 'zh', [(0, 1), (1, 0)])  12.5 us
    ppermute x3, starting transfers between devices, pass_on(): return lax.ppermute(value, ('core', 'x', 'y'), pairs)  10.5 us
    ppermute x2, starting transfers between devices, cross(): return lax.ppermute(value, 'core', [(0, 1), (1, 0)])  7.56 us
    ppermute x3, waiting for transfers between devices, pass_on(): return lax.ppermute(value, ('core', 'x', 'y'), pairs)  7.09 us
    pallas_call x6, Pallas kernels, whole(): pl.pallas_call(kernel, in_specs=specs or [VMEM] * len(ins), out_specs=out...  7.04 us
    all_to_all x1, starting transfers between devices, local(): far_parts = lax.all_to_all(far_terms, ('x', 'y'), 0, 0)  6.88 us
    ppermute x1, waiting for transfers between devices, local(): other = lax.ppermute(send, 'zh', [(0, 1), (1, 0)])  5.22 us
  transfers between devices with their start and end apart: 13, of which 5 were waited for; matrix products, arithmetic and copies ran while one was open for 2% of the time, Pallas kernels for 8%

profile of v7, /device:TPU:7, one launch (start us, length us, event | category | flops | bytes accessed | tf_op | source)
XLA Modules:
  0.0 93.1 jit_solution(96170423122943334)
XLA Ops:
  0.0 4.9 %collective-permute-start.2 = (bf16[1,128,256]{2,1,0:T(8,128)(2,1)}, bf16[1,128,256]{2,1,0:T(8,128)(2,1)S(1)}, u32[]{:S(2)}, u32[]{:S(2)}) collective-permute-start(bf16[1,128,256]{2,1,0:T(8,128)(2,1)} %bitcast.6), channel_id=1, source_target_pairs={{0,128},{64,192},{128,0},{192,64},{256,384},{320,448},{384,256},{4... | collective-permute-start | bytes 196616 | tf_op jit(solution)/shard_map/ppermute | solution.py:207
  4.9 8.8 %collective-permute-start = (bf16[1,128,256]{2,1,0:T(8,128)(2,1)}, bf16[1,128,256]{2,1,0:T(8,128)(2,1)S(1)}, u32[]{:S(2)}, u32[]{:S(2)}) collective-permute-start(bf16[1,128,256]{2,1,0:T(8,128)(2,1)} %bitcast.7), channel_id=1, source_target_pairs={{0,256},{64,320},{128,384},{192,448},{256,0},{320,64},{384,128},{4... | collective-permute-start | bytes 196616 | tf_op jit(solution)/shard_map/ppermute | solution.py:207
  14.4 0.8 copy-done.1
  16.0 6.3 %collective-permute-start.3 = (bf16[3,128,256]{2,1,0:T(8,128)(2,1)S(1)}, bf16[3,128,256]{2,1,0:T(8,128)(2,1)S(1)}, u32[]{:S(2)}, u32[]{:S(2)}) collective-permute-start(bf16[3,128,256]{2,1,0:T(8,128)(2,1)S(1)} %pad_maximum_fusion.2.refs_0_), channel_id=1, source_target_pairs={{0,64},{64,0},{128,192},{192,128},{256,320},{320,256},{384,448},{4... | collective-permute-start | bytes 589832 | tf_op jit(solution)/shard_map/ppermute | solution.py:207
  22.3 1.9 %collective-permute-start.1 = (bf16[1,128,256]{2,1,0:T(8,128)(2,1)S(1)}, bf16[1,128,256]{2,1,0:T(8,128)(2,1)S(1)}, u32[]{:S(2)}, u32[]{:S(2)}) collective-permute-start(bf16[1,128,256]{2,1,0:T(8,128)(2,1)S(1)} %collective-permute-done), channel_id=1, source_target_pairs={{0,128},{64,192},{128,0},{192,64},{256,384},{320,448},{384,256},{4... | collective-permute-start | bytes 196616 | tf_op jit(solution)/shard_map/ppermute | solution.py:207
  24.2 3.1 %far_lhs.1.lhs_ref = bf16[16,128,512]{2,1,0:T(8,128)(2,1)S(1)} custom-call(s32[8,32]{1,0:T(8,128)S(1)} %concatenate.13.table_ref, bf16[16,2,4,128,128]{4,3,2,1,0:T(8,128)(2,1)} %bitcast.10), custom_call_target="tpu_custom_call" | custom-call | bytes 4194304 | tf_op jit(solution)/shard_map/far_lhs/pallas_call | solution.py:72
  27.4 1.4 %collective-permute-done.1.refs_1_ = bf16[1,128,256]{2,1,0:T(8,128)(2,1)S(1)} collective-permute-done((bf16[1,128,256]{2,1,0:T(8,128)(2,1)S(1)}, bf16[1,128,256]{2,1,0:T(8,128)(2,1)S(1)}, u32[]{:S(2)}, u32[]{:S(2)}) %collective-permute-start.1) | collective-permute-done | bytes 65568 | tf_op jit(solution)/shard_map/ppermute | solution.py:207
  28.8 1.9 %collective-permute-start.4 = (bf16[1,128,256]{2,1,0:T(8,128)(2,1)S(1)}, bf16[1,128,256]{2,1,0:T(8,128)(2,1)S(1)}, u32[]{:S(2)}, u32[]{:S(2)}) collective-permute-start(bf16[1,128,256]{2,1,0:T(8,128)(2,1)S(1)} %collective-permute-done.1.refs_1_), channel_id=1, source_target_pairs={{0,64},{64,0},{128,192},{192,128},{256,320},{320,256},{384,448},{4... | collective-permute-start | bytes 196616 | tf_op jit(solution)/shard_map/ppermute | solution.py:207
  30.7 5.4 %collective-permute-start.5 = (bf16[4,128,256]{2,1,0:T(8,128)(2,1)S(1)}, bf16[4,128,256]{2,1,0:T(8,128)(2,1)S(1)}, u32[]{:S(2)}, u32[]{:S(2)}) collective-permute-start(bf16[4,128,256]{2,1,0:T(8,128)(2,1)S(1)} %pad_maximum_fusion), channel_id=1, source_target_pairs={{0,32},{32,0},{1,33},{33,1},{2,34},{34,2},{3,35},{35,3},{4,36},{36... | collective-permute-start | bytes 786440 | tf_op jit(solution)/shard_map/ppermute | solution.py:210
  36.2 2.2 %collective-permute-start.6 = (bf16[4,128,256]{2,1,0:T(8,128)(2,1)S(1)}, bf16[4,128,256]{2,1,0:T(8,128)(2,1)S(1)}, u32[]{:S(2)}, u32[]{:S(2)}) collective-permute-start(bf16[4,128,256]{2,1,0:T(8,128)(2,1)S(1)} %pad_maximum_fusion.1), channel_id=1, source_target_pairs={{0,32},{32,0},{1,33},{33,1},{2,34},{34,2},{3,35},{35,3},{4,36},{36... | collective-permute-start | bytes 786440 | tf_op jit(solution)/shard_map/ppermute | solution.py:210
  38.4 1.3 %collective-permute-done.6.refs_5_ = bf16[4,128,256]{2,1,0:T(8,128)(2,1)S(1)} collective-permute-done((bf16[4,128,256]{2,1,0:T(8,128)(2,1)S(1)}, bf16[4,128,256]{2,1,0:T(8,128)(2,1)S(1)}, u32[]{:S(2)}, u32[]{:S(2)}) %collective-permute-start.6) | collective-permute-done | bytes 262176 | tf_op jit(solution)/shard_map/ppermute | solution.py:210
  39.6 2.1 %far_terms.1 = (bf16[16,128,256]{2,1,0:T(8,128)(2,1)S(1)}, bf16[16,128,256]{2,1,0:T(8,128)(2,1)}) custom-call(s32[8,32]{1,0:T(8,128)S(1)} %concatenate.13.table_ref, bf16[16,128,512]{2,1,0:T(8,128)(2,1)S(1)} %far_lhs.1.lhs_ref, bf16[3,128,256]{2,1,0:T(8,128)(2,1)S(1)} %pad_maximum_fusion.2.refs_0_, bf16[1,128,256]{2,1,0:T(8,128)(2,1)S(1)} %collective-permute-done.1.refs_1_, ...), custom_call_target="tpu_custom_call" | custom-call | flops 536870912 | bytes 4194304 | tf_op jit(solution)/shard_map/far_terms/pallas_call | solution.py:27
  41.8 6.9 %all-to-all-start.1 = ((bf16[16,128,256]{2,1,0:T(8,128)(2,1)}), bf16[16,128,256]{2,1,0:T(8,128)(2,1)S(1)}, u32[]{:S(2)}, u32[]{:S(2)}) async-start(bf16[16,128,256]{2,1,0:T(8,128)(2,1)} %get-tuple-element.24), calls=%async_computation.1 | async-start | bytes 2097152 | tf_op jit(solution)/shard_map/all_to_all | solution.py:235
  48.6 3.1 %near_terms.1 = (bf16[4,128,256]{2,1,0:T(8,128)(2,1)S(1)}, bf16[4,128,256]{2,1,0:T(8,128)(2,1)S(1)}, bf16[4,128,256]{2,1,0:T(8,128)(2,1)S(1)}, bf16[4,128,256]{2,1,0:T(8,128)(2,1)S(1)}) custom-call(s32[8,32]{1,0:T(8,128)S(1)} %concatenate.13.table_ref, bf16[16,2,4,128,128]{4,3,2,1,0:T(8,128)(2,1)} %bitcast.11, ...), custom_call_target="tpu_custom_call" | custom-call | flops 536870912 | bytes 4194304 | tf_op jit(solution)/shard_map/near_terms/pallas_call | solution.py:27
  51.8 3.1 %collective-permute-start.7 = (bf16[4,128,256]{2,1,0:T(8,128)(2,1)S(1)}, bf16[4,128,256]{2,1,0:T(8,128)(2,1)S(1)}, u32[]{:S(2)}, u32[]{:S(2)}) collective-permute-start(bf16[4,128,256]{2,1,0:T(8,128)(2,1)S(1)} %get-tuple-element.21), channel_id=1, source_target_pairs={{0,8},{8,16},{16,24},{24,0},{2,10},{10,18},{18,26},{26,2},{4,12},{... | collective-permute-start | bytes 786440 | tf_op jit(solution)/shard_map/ppermute | solution.py:190
  54.9 4.3 %collective-permute-start.8 = (bf16[4,128,256]{2,1,0:T(8,128)(2,1)S(1)}, bf16[4,128,256]{2,1,0:T(8,128)(2,1)S(1)}, u32[]{:S(2)}, u32[]{:S(2)}) collective-permute-start(bf16[4,128,256]{2,1,0:T(8,128)(2,1)S(1)} %get-tuple-element.22), channel_id=1, source_target_pairs={{0,16},{8,24},{16,0},{24,8},{2,18},{10,26},{18,2},{26,10},{4,20},{... | collective-permute-start | bytes 786440 | tf_op jit(solution)/shard_map/ppermute | solution.py:190
  59.2 3.1 %collective-permute-start.9 = (bf16[4,128,256]{2,1,0:T(8,128)(2,1)S(1)}, bf16[4,128,256]{2,1,0:T(8,128)(2,1)S(1)}, u32[]{:S(2)}, u32[]{:S(2)}) collective-permute-start(bf16[4,128,256]{2,1,0:T(8,128)(2,1)S(1)} %get-tuple-element.23), channel_id=1, source_target_pairs={{0,24},{8,0},{16,8},{24,16},{2,26},{10,2},{18,10},{26,18},{4,28},{... | collective-permute-start | bytes 786440 | tf_op jit(solution)/shard_map/ppermute | solution.py:190
  62.3 4.2 %collective-permute-done.7.refs_1_ = bf16[4,128,256]{2,1,0:T(8,128)(2,1)S(1)} collective-permute-done((bf16[4,128,256]{2,1,0:T(8,128)(2,1)S(1)}, bf16[4,128,256]{2,1,0:T(8,128)(2,1)S(1)}, u32[]{:S(2)}, u32[]{:S(2)}) %collective-permute-start.7) | collective-permute-done | bytes 262176 | tf_op jit(solution)/shard_map/ppermute | solution.py:190
  66.5 2.8 %collective-permute-done.8.refs_2_ = bf16[4,128,256]{2,1,0:T(8,128)(2,1)S(1)} collective-permute-done((bf16[4,128,256]{2,1,0:T(8,128)(2,1)S(1)}, bf16[4,128,256]{2,1,0:T(8,128)(2,1)S(1)}, u32[]{:S(2)}, u32[]{:S(2)}) %collective-permute-start.8) | collective-permute-done | bytes 262176 | tf_op jit(solution)/shard_map/ppermute | solution.py:190
  69.4 0.9 near_sum.1
  70.2 4.2 %all-to-all-start = ((bf16[4,128,256]{2,1,0:T(8,128)(2,1)}), bf16[4,128,256]{2,1,0:T(8,128)(2,1)S(1)}, u32[]{:S(2)}, u32[]{:S(2)}) async-start(bf16[4,128,256]{2,1,0:T(8,128)(2,1)} %near_sum.1), calls=%async_computation | async-start | bytes 524288 | tf_op jit(solution)/shard_map/all_to_all | solution.py:254
  74.6 12.5 %collective-permute-start.10 = (bf16[128,256]{1,0:T(8,128)(2,1)S(1)}, bf16[128,256]{1,0:T(8,128)(2,1)S(1)}, u32[]{:S(2)}, u32[]{:S(2)}) collective-permute-start(bf16[128,256]{1,0:T(8,128)(2,1)S(1)} %send.1), channel_id=1, source_target_pairs={{0,1},{1,0},{2,3},{3,2},{4,5},{5,4},{6,7},{7,6},{8,9},{9,8},{10,11... | collective-permute-start | bytes 196616 | tf_op jit(solution)/shard_map/ppermute | solution.py:252
  87.1 5.2 %collective-permute-done.10.other_ref = bf16[128,256]{1,0:T(8,128)(2,1)S(1)} collective-permute-done((bf16[128,256]{1,0:T(8,128)(2,1)S(1)}, bf16[128,256]{1,0:T(8,128)(2,1)S(1)}, u32[]{:S(2)}, u32[]{:S(2)}) %collective-permute-start.10) | collective-permute-done | bytes 65568 | tf_op jit(solution)/shard_map/ppermute | solution.py:252
  92.3 0.8 finish.1
  (23 shorter events, 1.6 us)
Async XLA Ops:
  0.0 16.0 %collective-permute-start.2 = (bf16[1,128,256]{2,1,0:T(8,128)(2,1)}, bf16[1,128,256]{2,1,0:T(8,128)(2,1)S(1)}, u32[]{:S(2)}, u32[]{:S(2)}) collective-permute-start(bf16[1,128,256]{2,1,0:T(8,128)(2,1)} %bitcast.6), channel_id=1, source_target_pairs={{0,128},{64,192},{128,0},{192,64},{256,384},{320,448},{384,256},{4... | collective-permute-start | bytes 196616 | tf_op jit(solution)/shard_map/ppermute | solution.py:207
  4.9 11.1 %collective-permute-start = (bf16[1,128,256]{2,1,0:T(8,128)(2,1)}, bf16[1,128,256]{2,1,0:T(8,128)(2,1)S(1)}, u32[]{:S(2)}, u32[]{:S(2)}) collective-permute-start(bf16[1,128,256]{2,1,0:T(8,128)(2,1)} %bitcast.7), channel_id=1, source_target_pairs={{0,256},{64,320},{128,384},{192,448},{256,0},{320,64},{384,128},{4... | collective-permute-start | bytes 196616 | tf_op jit(solution)/shard_map/ppermute | solution.py:207
  14.4 0.8 copy-start.1
  16.0 20.1 %collective-permute-start.3 = (bf16[3,128,256]{2,1,0:T(8,128)(2,1)S(1)}, bf16[3,128,256]{2,1,0:T(8,128)(2,1)S(1)}, u32[]{:S(2)}, u32[]{:S(2)}) collective-permute-start(bf16[3,128,256]{2,1,0:T(8,128)(2,1)S(1)} %pad_maximum_fusion.2.refs_0_), channel_id=1, source_target_pairs={{0,64},{64,0},{128,192},{192,128},{256,320},{320,256},{384,448},{4... | collective-permute-start | bytes 589832 | tf_op jit(solution)/shard_map/ppermute | solution.py:207
  22.3 6.4 %collective-permute-start.1 = (bf16[1,128,256]{2,1,0:T(8,128)(2,1)S(1)}, bf16[1,128,256]{2,1,0:T(8,128)(2,1)S(1)}, u32[]{:S(2)}, u32[]{:S(2)}) collective-permute-start(bf16[1,128,256]{2,1,0:T(8,128)(2,1)S(1)} %collective-permute-done), channel_id=1, source_target_pairs={{0,128},{64,192},{128,0},{192,64},{256,384},{320,448},{384,256},{4... | collective-permute-start | bytes 196616 | tf_op jit(solution)/shard_map/ppermute | solution.py:207
  28.8 7.4 %collective-permute-start.4 = (bf16[1,128,256]{2,1,0:T(8,128)(2,1)S(1)}, bf16[1,128,256]{2,1,0:T(8,128)(2,1)S(1)}, u32[]{:S(2)}, u32[]{:S(2)}) collective-permute-start(bf16[1,128,256]{2,1,0:T(8,128)(2,1)S(1)} %collective-permute-done.1.refs_1_), channel_id=1, source_target_pairs={{0,64},{64,0},{128,192},{192,128},{256,320},{320,256},{384,448},{4... | collective-permute-start | bytes 196616 | tf_op jit(solution)/shard_map/ppermute | solution.py:207
  30.7 7.6 %collective-permute-start.5 = (bf16[4,128,256]{2,1,0:T(8,128)(2,1)S(1)}, bf16[4,128,256]{2,1,0:T(8,128)(2,1)S(1)}, u32[]{:S(2)}, u32[]{:S(2)}) collective-permute-start(bf16[4,128,256]{2,1,0:T(8,128)(2,1)S(1)} %pad_maximum_fusion), channel_id=1, source_target_pairs={{0,32},{32,0},{1,33},{33,1},{2,34},{34,2},{3,35},{35,3},{4,36},{36... | collective-permute-start | bytes 786440 | tf_op jit(solution)/shard_map/ppermute | solution.py:210
  36.2 3.4 %collective-permute-start.6 = (bf16[4,128,256]{2,1,0:T(8,128)(2,1)S(1)}, bf16[4,128,256]{2,1,0:T(8,128)(2,1)S(1)}, u32[]{:S(2)}, u32[]{:S(2)}) collective-permute-start(bf16[4,128,256]{2,1,0:T(8,128)(2,1)S(1)} %pad_maximum_fusion.1), channel_id=1, source_target_pairs={{0,32},{32,0},{1,33},{33,1},{2,34},{34,2},{3,35},{35,3},{4,36},{36... | collective-permute-start | bytes 786440 | tf_op jit(solution)/shard_map/ppermute | solution.py:210
  41.8 28.5 %all-to-all-start.1 = ((bf16[16,128,256]{2,1,0:T(8,128)(2,1)}), bf16[16,128,256]{2,1,0:T(8,128)(2,1)S(1)}, u32[]{:S(2)}, u32[]{:S(2)}) async-start(bf16[16,128,256]{2,1,0:T(8,128)(2,1)} %get-tuple-element.24), calls=%async_computation.1 | async-start | bytes 2097152 | tf_op jit(solution)/shard_map/all_to_all | solution.py:235
  48.6 43.7 %copy-start = (bf16[256,256]{1,0:T(8,128)(2,1)S(1)}, bf16[256,256]{1,0:T(8,128)(2,1)}, u32[]{:S(2)}) copy-start(bf16[256,256]{1,0:T(8,128)(2,1)} %weight_ref.1) | copy-start | bytes 393220
  48.6 43.7 %copy-start.2 = (f32[256]{0:T(256)S(1)}, f32[256]{0:T(256)}, u32[]{:S(2)}) copy-start(f32[256]{0:T(256)} %param.11) | copy-start | bytes 3076
  51.8 14.8 %collective-permute-start.7 = (bf16[4,128,256]{2,1,0:T(8,128)(2,1)S(1)}, bf16[4,128,256]{2,1,0:T(8,128)(2,1)S(1)}, u32[]{:S(2)}, u32[]{:S(2)}) collective-permute-start(bf16[4,128,256]{2,1,0:T(8,128)(2,1)S(1)} %get-tuple-element.21), channel_id=1, source_target_pairs={{0,8},{8,16},{16,24},{24,0},{2,10},{10,18},{18,26},{26,2},{4,12},{... | collective-permute-start | bytes 786440 | tf_op jit(solution)/shard_map/ppermute | solution.py:190
  54.9 14.5 %collective-permute-start.8 = (bf16[4,128,256]{2,1,0:T(8,128)(2,1)S(1)}, bf16[4,128,256]{2,1,0:T(8,128)(2,1)S(1)}, u32[]{:S(2)}, u32[]{:S(2)}) collective-permute-start(bf16[4,128,256]{2,1,0:T(8,128)(2,1)S(1)} %get-tuple-element.22), channel_id=1, source_target_pairs={{0,16},{8,24},{16,0},{24,8},{2,18},{10,26},{18,2},{26,10},{4,20},{... | collective-permute-start | bytes 786440 | tf_op jit(solution)/shard_map/ppermute | solution.py:190
  59.2 10.2 %collective-permute-start.9 = (bf16[4,128,256]{2,1,0:T(8,128)(2,1)S(1)}, bf16[4,128,256]{2,1,0:T(8,128)(2,1)S(1)}, u32[]{:S(2)}, u32[]{:S(2)}) collective-permute-start(bf16[4,128,256]{2,1,0:T(8,128)(2,1)S(1)} %get-tuple-element.23), channel_id=1, source_target_pairs={{0,24},{8,0},{16,8},{24,16},{2,26},{10,2},{18,10},{26,18},{4,28},{... | collective-permute-start | bytes 786440 | tf_op jit(solution)/shard_map/ppermute | solution.py:190
  70.2 16.9 %all-to-all-start = ((bf16[4,128,256]{2,1,0:T(8,128)(2,1)}), bf16[4,128,256]{2,1,0:T(8,128)(2,1)S(1)}, u32[]{:S(2)}, u32[]{:S(2)}) async-start(bf16[4,128,256]{2,1,0:T(8,128)(2,1)} %near_sum.1), calls=%async_computation | async-start | bytes 524288 | tf_op jit(solution)/shard_map/all_to_all | solution.py:254
  74.6 17.8 %collective-permute-start.10 = (bf16[128,256]{1,0:T(8,128)(2,1)S(1)}, bf16[128,256]{1,0:T(8,128)(2,1)S(1)}, u32[]{:S(2)}, u32[]{:S(2)}) collective-permute-start(bf16[128,256]{1,0:T(8,128)(2,1)S(1)} %send.1), channel_id=1, source_target_pairs={{0,1},{1,0},{2,3},{3,2},{4,5},{5,4},{6,7},{7,6},{8,9},{9,8},{10,11... | collective-permute-start | bytes 196616 | tf_op jit(solution)/shard_map/ppermute | solution.py:252

commit v8 on v5

--- a/solution.py
+++ b/solution.py
@@ -8,6 +8,7 @@
 ZL, CORE, X, Y, ZH = 8, 2, 4, 4, 2
 SLOTS, BS, F = 4, 128, 256
 COUNT, HALF = SLOTS, SLOTS + 1
+LONG = (1 << 35, 1 << 26)
 VMEM = pl.BlockSpec(memory_space=pltpu.VMEM)
 SMEM = pl.BlockSpec(memory_space=pltpu.SMEM)
 ANY = pl.BlockSpec(memory_space=pl.ANY)
@@ -91,11 +92,16 @@
     )(table, blocks)
 
 
-def far_kernel(
-    table_ref, lhs_ref, near_ref, across_ref, stripe_ref, out_ref, made, sem
-):
-    stripe_ref[:ZL] = near_ref[...]
-    stripe_ref[ZL:] = across_ref[...]
+def far_kernel(table_ref, lhs_ref, *refs):
+    trio, p6, ones, p7, core0, core1 = refs[:6]
+    stripe_ref, out_ref, made, sem = refs[6:]
+    near = {0: trio.at[0], 4: trio.at[1], 2: trio.at[2], 6: p6.at[0]}
+    near |= {1: ones.at[0], 5: ones.at[1], 3: ones.at[2], 7: p7.at[0]}
+    across = {d: core0.at[i] for i, d in enumerate((0, 4, 2, 6))}
+    across |= {d: core1.at[i] for i, d in enumerate((1, 5, 3, 7))}
+    for d in range(ZL):
+        stripe_ref[CORE * d] = near[d][...]
+        stripe_ref[CORE * d + 1] = across[d][...]
     group = X * Y // sem.shape[0]
     stores = []
     for g in range(sem.shape[0]):
@@ -175,13 +181,7 @@
     zl, core, zh = (
         lax.axis_index(a).astype(jnp.int32) for a in ("zl", "core", "zh")
     )
-    offset = block_col.T ^ (CORE * zl + core)
-    spots = (
-        ((offset >> 3) & 1)
-        | ((offset >> 1) & 2)
-        | ((offset << 1) & 4)
-        | ((offset << 3) & 8)
-    )
+    spots = block_col.T ^ (CORE * zl + core)
     counts = row_count.T
     return jnp.concatenate([spots, counts, jnp.full_like(counts, zh)], axis=0)
 
@@ -197,32 +197,34 @@
         [features[None]],
         jax.ShapeDtypeStruct((1, BS, F), bf16),
         "own",
-        (0, 1 << 17),
-    )
-    held = own
-    for bit in (4, 2, 1):
-        came = lax.ppermute(
-            features[None] if bit == 4 else held,
-            "zl",
-            [(z, z ^ bit) for z in range(ZL)],
-        )
-        if bit == 4:
-            came, table = lax.optimization_barrier((came, table))
-            far_lhs = far_lhs_rows(table, blocks)
-        if bit == 2:
-            came, far_lhs = lax.optimization_barrier((came, far_lhs))
-        held = jnp.concatenate([held, came], axis=0)
-    across = lax.ppermute(held, "core", [(0, 1), (1, 0)])
+        LONG,
+    )
+    def hop(value, bit):
+        return lax.ppermute(value, "zl", [(z, z ^ bit) for z in range(ZL)])
+
+    def cross(value):
+        return lax.ppermute(value, "core", [(0, 1), (1, 0)])
+
+    p4, p2 = hop(features[None], 4), hop(own, 2)
+    p4, table = lax.optimization_barrier((p4, table))
+    p6 = hop(p4, 2)
+    far_lhs = far_lhs_rows(table, blocks)
+    trio = jnp.concatenate([own, p4, p2], axis=0)
+    ones = hop(trio, 1)
+    p6, far_lhs = lax.optimization_barrier((p6, far_lhs))
+    p7 = hop(p6, 1)
+    core0 = cross(jnp.concatenate([trio, p6], axis=0))
+    core1 = cross(jnp.concatenate([ones, p7], axis=0))
     half = (X * Y, BS, F)
     one = jax.ShapeDtypeStruct((BS, F), bf16)
     stripe, far_terms = whole(
         far_kernel,
-        [table, far_lhs, held, across],
+        [table, far_lhs, trio, p6, ones, p7, core0, core1],
         [jax.ShapeDtypeStruct(half, bf16)] * 2,
         "far_terms",
         (2 * X * Y * SLOTS * BS * BS * F, 4 << 20),
         limit=8 << 20,
-        specs=[SMEM, VMEM, VMEM, VMEM],
+        specs=[SMEM] + [VMEM] * 7,
         out_specs=[VMEM, ANY],
         scratch=[pltpu.VMEM(half, bf16), pltpu.SemaphoreType.DMA((4,))],
     )

time: 88.7 us -> 87.7 us (0.989)
  the two profiles are of different devices: /device:TPU:2 before, /device:TPU:34 now
where the time goes in v8:
time: 87.7 us; the launch traced here: 87.1 us
  starting transfers between devices  53.6 us (61%)
  waiting for transfers between devices  21.1 us (24%)
  Pallas kernels  11.1 us (13%)
  local copies, waits for them, and re-layouts  0.93 us (1%)
    ppermute x5, starting transfers between devices, hop(): return lax.ppermute(value, 'zl', [(z, z ^ bit) for z in range(ZL)])  24.9 us
    ppermute x1, starting transfers between devices, local(): other = lax.ppermute(send, 'zh', [(0, 1), (1, 0)])  11 us
    all_to_all x1, waiting for transfers between devices, local(): far_parts = lax.all_to_all(far_terms, ('x', 'y'), 0, 0)  10.5 us
    all_to_all x1, starting transfers between devices, local(): far_parts = lax.all_to_all(far_terms, ('x', 'y'), 0, 0)  7.49 us
    all_to_all x1, starting transfers between devices, local(): near_parts = lax.all_to_all(near_terms, ('x', 'y'), 0, 0)  6.35 us
    pallas_call x1, Pallas kernels, near_half(): pl.pallas_call(near_kernel, grid_spec=pltpu.PrefetchScalarGridSpec(num_sc...  4.83 us
    ppermute x2, starting transfers between devices, cross(): return lax.ppermute(value, 'core', [(0, 1), (1, 0)])  3.84 us
    pallas_call x4, Pallas kernels, whole(): pl.pallas_call(kernel, in_specs=specs or [VMEM] * len(ins), out_specs=out...  3.2 us
  transfers between devices with their start and end apart: 10, of which 8 were waited for; matrix products, arithmetic and copies ran while one was open for 0% of the time, Pallas kernels for 9%

profile of v8, /device:TPU:34, one launch (start us, length us, event | category | flops | bytes accessed | tf_op | source)
XLA Modules:
  0.0 87.1 jit_solution(16725766297227020317)
XLA Ops:
  0.0 9.1 %collective-permute-start = (bf16[1,128,256]{2,1,0:T(8,128)(2,1)}, bf16[1,128,256]{2,1,0:T(8,128)(2,1)S(1)}, u32[]{:S(2)}, u32[]{:S(2)}) collective-permute-start(bf16[1,128,256]{2,1,0:T(8,128)(2,1)} %bitcast.8), channel_id=1, source_target_pairs={{0,256},{64,320},{128,384},{192,448},{256,0},{320,64},{384,128},{4... | collective-permute-start | bytes 196616 | tf_op jit(solution)/shard_map/ppermute | solution.py:203
  9.1 0.8 copy-done.2
  10.0 5.3 %collective-permute-start.2 = (bf16[1,128,256]{2,1,0:T(8,128)(2,1)S(1)}, bf16[1,128,256]{2,1,0:T(8,128)(2,1)S(1)}, u32[]{:S(2)}, u32[]{:S(2)}) collective-permute-start(bf16[1,128,256]{2,1,0:T(8,128)(2,1)S(1)} %own.1), channel_id=1, source_target_pairs={{0,128},{64,192},{128,0},{192,64},{256,384},{320,448},{384,256},{4... | collective-permute-start | bytes 196616 | tf_op jit(solution)/shard_map/ppermute | solution.py:203
  15.4 0.2 collective-permute-done
  15.7 1.9 %collective-permute-done.2 = bf16[1,128,256]{2,1,0:T(8,128)(2,1)S(1)} collective-permute-done((bf16[1,128,256]{2,1,0:T(8,128)(2,1)S(1)}, bf16[1,128,256]{2,1,0:T(8,128)(2,1)S(1)}, u32[]{:S(2)}, u32[]{:S(2)}) %collective-permute-start.2) | collective-permute-done | bytes 65568 | tf_op jit(solution)/shard_map/ppermute | solution.py:203
  17.5 3.5 %collective-permute-start.3 = (bf16[3,128,256]{2,1,0:T(8,128)(2,1)S(1)}, bf16[3,128,256]{2,1,0:T(8,128)(2,1)S(1)}, u32[]{:S(2)}, u32[]{:S(2)}) collective-permute-start(bf16[3,128,256]{2,1,0:T(8,128)(2,1)S(1)} %pad_maximum_fusion.2.refs_0_), channel_id=1, source_target_pairs={{0,64},{64,0},{128,192},{192,128},{256,320},{320,256},{384,448},{4... | collective-permute-start | bytes 589832 | tf_op jit(solution)/shard_map/ppermute | solution.py:203
  21.0 3.5 %collective-permute-start.1 = (bf16[1,128,256]{2,1,0:T(8,128)(2,1)S(1)}, bf16[1,128,256]{2,1,0:T(8,128)(2,1)S(1)}, u32[]{:S(2)}, u32[]{:S(2)}) collective-permute-start(bf16[1,128,256]{2,1,0:T(8,128)(2,1)S(1)} %collective-permute-done), channel_id=1, source_target_pairs={{0,128},{64,192},{128,0},{192,64},{256,384},{320,448},{384,256},{4... | collective-permute-start | bytes 196616 | tf_op jit(solution)/shard_map/ppermute | solution.py:203
  24.5 3.1 %far_lhs.1.lhs_ref = bf16[16,128,512]{2,1,0:T(8,128)(2,1)S(1)} custom-call(s32[6,32]{1,0:T(8,128)S(1)} %add_add_fusion.table_ref, bf16[16,2,4,128,128]{4,3,2,1,0:T(8,128)(2,1)} %bitcast.10), custom_call_target="tpu_custom_call" | custom-call | bytes 4194304 | tf_op jit(solution)/shard_map/far_lhs/pallas_call | solution.py:73
  27.7 0.4 collective-permute-done.1.refs_1_
  28.1 3.5 %collective-permute-start.4 = (bf16[1,128,256]{2,1,0:T(8,128)(2,1)S(1)}, bf16[1,128,256]{2,1,0:T(8,128)(2,1)S(1)}, u32[]{:S(2)}, u32[]{:S(2)}) collective-permute-start(bf16[1,128,256]{2,1,0:T(8,128)(2,1)S(1)} %collective-permute-done.1.refs_1_), channel_id=1, source_target_pairs={{0,64},{64,0},{128,192},{192,128},{256,320},{320,256},{384,448},{4... | collective-permute-start | bytes 196616 | tf_op jit(solution)/shard_map/ppermute | solution.py:203
  31.6 1.9 %collective-permute-start.5 = (bf16[4,128,256]{2,1,0:T(8,128)(2,1)S(1)}, bf16[4,128,256]{2,1,0:T(8,128)(2,1)S(1)}, u32[]{:S(2)}, u32[]{:S(2)}) collective-permute-start(bf16[4,128,256]{2,1,0:T(8,128)(2,1)S(1)} %pad_maximum_fusion), channel_id=1, source_target_pairs={{0,32},{32,0},{1,33},{33,1},{2,34},{34,2},{3,35},{35,3},{4,36},{36... | collective-permute-start | bytes 786440 | tf_op jit(solution)/shard_map/ppermute | solution.py:206
  33.6 0.6 collective-permute-done.4.refs_3_
  34.2 1.9 %collective-permute-start.6 = (bf16[4,128,256]{2,1,0:T(8,128)(2,1)S(1)}, bf16[4,128,256]{2,1,0:T(8,128)(2,1)S(1)}, u32[]{:S(2)}, u32[]{:S(2)}) collective-permute-start(bf16[4,128,256]{2,1,0:T(8,128)(2,1)S(1)} %pad_maximum_fusion.1), channel_id=1, source_target_pairs={{0,32},{32,0},{1,33},{33,1},{2,34},{34,2},{3,35},{35,3},{4,36},{36... | collective-permute-start | bytes 786440 | tf_op jit(solution)/shard_map/ppermute | solution.py:206
  36.2 1.5 %collective-permute-done.6.refs_5_ = bf16[4,128,256]{2,1,0:T(8,128)(2,1)S(1)} collective-permute-done((bf16[4,128,256]{2,1,0:T(8,128)(2,1)S(1)}, bf16[4,128,256]{2,1,0:T(8,128)(2,1)S(1)}, u32[]{:S(2)}, u32[]{:S(2)}) %collective-permute-start.6) | collective-permute-done | bytes 262176 | tf_op jit(solution)/shard_map/ppermute | solution.py:206
  37.7 2.1 %far_terms.1 = (bf16[16,128,256]{2,1,0:T(8,128)(2,1)S(1)}, bf16[16,128,256]{2,1,0:T(8,128)(2,1)}) custom-call(s32[6,32]{1,0:T(8,128)S(1)} %add_add_fusion.table_ref, bf16[16,128,512]{2,1,0:T(8,128)(2,1)S(1)} %far_lhs.1.lhs_ref, bf16[3,128,256]{2,1,0:T(8,128)(2,1)S(1)} %pad_maximum_fusion.2.refs_0_, bf16[1,128,256]{2,1,0:T(8,128)(2,1)S(1)} %collective-permute-done.1.refs_1_, ...), custom_call_target="tpu_custom_call" | custom-call | flops 536870912 | bytes 4194304 | tf_op jit(solution)/shard_map/far_terms/pallas_call | solution.py:28
  39.8 7.5 %all-to-all-start.1 = ((bf16[16,128,256]{2,1,0:T(8,128)(2,1)}), bf16[16,128,256]{2,1,0:T(8,128)(2,1)S(1)}, u32[]{:S(2)}, u32[]{:S(2)}) async-start(bf16[16,128,256]{2,1,0:T(8,128)(2,1)} %get-tuple-element.16), calls=%async_computation.1 | async-start | bytes 2097152 | tf_op jit(solution)/shard_map/all_to_all | solution.py:232
  47.3 4.8 %near_terms.1 = bf16[16,128,256]{2,1,0:T(8,128)(2,1)} custom-call(s32[6,32]{1,0:T(8,128)S(1)} %add_add_fusion.table_ref, bf16[16,2,4,128,128]{4,3,2,1,0:T(8,128)(2,1)} %bitcast.11, bf16[16,128,256]{2,1,0:T(8,128)(2,1)S(1)} %get-tuple-element.15.stripe_ref), custom_call_target="tpu_custom_call" | custom-call | flops 536870912 | bytes 4194304 | tf_op jit(solution)/shard_map/near_terms/pallas_call | solution.py:132
  52.2 10.5 %all-to-all-done.1.parts_ref = bf16[16,128,256]{2,1,0:T(8,128)(2,1)S(1)} async-done(((bf16[16,128,256]{2,1,0:T(8,128)(2,1)}), bf16[16,128,256]{2,1,0:T(8,128)(2,1)S(1)}, u32[]{:S(2)}, u32[]{:S(2)}) %all-to-all-start.1) | async-done | bytes 1048608 | tf_op jit(solution)/shard_map/all_to_all | solution.py:232
  62.6 6.3 %all-to-all-start = ((bf16[16,128,256]{2,1,0:T(8,128)(2,1)}), bf16[16,128,256]{2,1,0:T(8,128)(2,1)S(1)}, u32[]{:S(2)}, u32[]{:S(2)}) async-start(bf16[16,128,256]{2,1,0:T(8,128)(2,1)} %near_terms.1), calls=%async_computation | async-start | bytes 2097152 | tf_op jit(solution)/shard_map/all_to_all | solution.py:233
  69.0 0.1 send.1
  69.1 11.0 %collective-permute-start.7 = (bf16[128,256]{1,0:T(8,128)(2,1)S(1)}, bf16[128,256]{1,0:T(8,128)(2,1)S(1)}, u32[]{:S(2)}, u32[]{:S(2)}) collective-permute-start(bf16[128,256]{1,0:T(8,128)(2,1)S(1)} %send.1), channel_id=1, source_target_pairs={{0,1},{1,0},{2,3},{3,2},{4,5},{5,4},{6,7},{7,6},{8,9},{9,8},{10,11... | collective-permute-start | bytes 196616 | tf_op jit(solution)/shard_map/ppermute | solution.py:235
  80.2 2.8 %all-to-all-done.parts_ref = bf16[16,128,256]{2,1,0:T(8,128)(2,1)S(1)} async-done(((bf16[16,128,256]{2,1,0:T(8,128)(2,1)}), bf16[16,128,256]{2,1,0:T(8,128)(2,1)S(1)}, u32[]{:S(2)}, u32[]{:S(2)}) %all-to-all-start) | async-done | bytes 1048608 | tf_op jit(solution)/shard_map/all_to_all | solution.py:233
  83.0 3.2 %collective-permute-done.7.other_ref = bf16[128,256]{1,0:T(8,128)(2,1)S(1)} collective-permute-done((bf16[128,256]{1,0:T(8,128)(2,1)S(1)}, bf16[128,256]{1,0:T(8,128)(2,1)S(1)}, u32[]{:S(2)}, u32[]{:S(2)}) %collective-permute-start.7) | collective-permute-done | bytes 65568 | tf_op jit(solution)/shard_map/ppermute | solution.py:235
  86.2 0.9 %finish.1 = bf16[128,256]{1,0:T(8,128)(2,1)} custom-call(bf16[16,128,256]{2,1,0:T(8,128)(2,1)S(1)} %all-to-all-done.parts_ref, bf16[128,256]{1,0:T(8,128)(2,1)S(1)} %collective-permute-done.7.other_ref, bf16[256,256]{1,0:T(8,128)(2,1)S(1)} %copy-done, f32[1,256]{1,0:T(1,128)S(1)} %bitcast.7), custom_call_target="tpu_custom_call" | custom-call | flops 16777216 | bytes 2097152 | tf_op jit(solution)/shard_map/finish/pallas_call | solution.py:28
  (18 shorter events, 0.3 us)
Async XLA Ops:
  0.0 15.7 %collective-permute-start = (bf16[1,128,256]{2,1,0:T(8,128)(2,1)}, bf16[1,128,256]{2,1,0:T(8,128)(2,1)S(1)}, u32[]{:S(2)}, u32[]{:S(2)}) collective-permute-start(bf16[1,128,256]{2,1,0:T(8,128)(2,1)} %bitcast.8), channel_id=1, source_target_pairs={{0,256},{64,320},{128,384},{192,448},{256,0},{320,64},{384,128},{4... | collective-permute-start | bytes 196616 | tf_op jit(solution)/shard_map/ppermute | solution.py:203
  9.1 0.9 copy-start.2
  9.9 5.4 %copy-start.3 = (s32[32,4]{0,1:T(4,128)S(1)}, s32[32,4]{0,1:T(4,128)}, u32[]{:S(2)}) copy-start(s32[32,4]{0,1:T(4,128)} %param.8) | copy-start | bytes 1540
  9.9 5.4 %copy-start.4 = (s32[32,1]{0,1:T(1,128)S(1)}, s32[32,1]{0,1:T(1,128)}, u32[]{:S(2)}) copy-start(s32[32,1]{0,1:T(1,128)} %param.9) | copy-start | bytes 388
  10.0 7.5 %collective-permute-start.2 = (bf16[1,128,256]{2,1,0:T(8,128)(2,1)S(1)}, bf16[1,128,256]{2,1,0:T(8,128)(2,1)S(1)}, u32[]{:S(2)}, u32[]{:S(2)}) collective-permute-start(bf16[1,128,256]{2,1,0:T(8,128)(2,1)S(1)} %own.1), channel_id=1, source_target_pairs={{0,128},{64,192},{128,0},{192,64},{256,384},{320,448},{384,256},{4... | collective-permute-start | bytes 196616 | tf_op jit(solution)/shard_map/ppermute | solution.py:203
  17.5 16.7 %collective-permute-start.3 = (bf16[3,128,256]{2,1,0:T(8,128)(2,1)S(1)}, bf16[3,128,256]{2,1,0:T(8,128)(2,1)S(1)}, u32[]{:S(2)}, u32[]{:S(2)}) collective-permute-start(bf16[3,128,256]{2,1,0:T(8,128)(2,1)S(1)} %pad_maximum_fusion.2.refs_0_), channel_id=1, source_target_pairs={{0,64},{64,0},{128,192},{192,128},{256,320},{320,256},{384,448},{4... | collective-permute-start | bytes 589832 | tf_op jit(solution)/shard_map/ppermute | solution.py:203
  21.0 7.1 %collective-permute-start.1 = (bf16[1,128,256]{2,1,0:T(8,128)(2,1)S(1)}, bf16[1,128,256]{2,1,0:T(8,128)(2,1)S(1)}, u32[]{:S(2)}, u32[]{:S(2)}) collective-permute-start(bf16[1,128,256]{2,1,0:T(8,128)(2,1)S(1)} %collective-permute-done), channel_id=1, source_target_pairs={{0,128},{64,192},{128,0},{192,64},{256,384},{320,448},{384,256},{4... | collective-permute-start | bytes 196616 | tf_op jit(solution)/shard_map/ppermute | solution.py:203
  28.1 6.1 %collective-permute-start.4 = (bf16[1,128,256]{2,1,0:T(8,128)(2,1)S(1)}, bf16[1,128,256]{2,1,0:T(8,128)(2,1)S(1)}, u32[]{:S(2)}, u32[]{:S(2)}) collective-permute-start(bf16[1,128,256]{2,1,0:T(8,128)(2,1)S(1)} %collective-permute-done.1.refs_1_), channel_id=1, source_target_pairs={{0,64},{64,0},{128,192},{192,128},{256,320},{320,256},{384,448},{4... | collective-permute-start | bytes 196616 | tf_op jit(solution)/shard_map/ppermute | solution.py:203
  31.6 4.5 %collective-permute-start.5 = (bf16[4,128,256]{2,1,0:T(8,128)(2,1)S(1)}, bf16[4,128,256]{2,1,0:T(8,128)(2,1)S(1)}, u32[]{:S(2)}, u32[]{:S(2)}) collective-permute-start(bf16[4,128,256]{2,1,0:T(8,128)(2,1)S(1)} %pad_maximum_fusion), channel_id=1, source_target_pairs={{0,32},{32,0},{1,33},{33,1},{2,34},{34,2},{3,35},{35,3},{4,36},{36... | collective-permute-start | bytes 786440 | tf_op jit(solution)/shard_map/ppermute | solution.py:206
  34.2 3.4 %collective-permute-start.6 = (bf16[4,128,256]{2,1,0:T(8,128)(2,1)S(1)}, bf16[4,128,256]{2,1,0:T(8,128)(2,1)S(1)}, u32[]{:S(2)}, u32[]{:S(2)}) collective-permute-start(bf16[4,128,256]{2,1,0:T(8,128)(2,1)S(1)} %pad_maximum_fusion.1), channel_id=1, source_target_pairs={{0,32},{32,0},{1,33},{33,1},{2,34},{34,2},{3,35},{35,3},{4,36},{36... | collective-permute-start | bytes 786440 | tf_op jit(solution)/shard_map/ppermute | solution.py:206
  39.8 22.8 %all-to-all-start.1 = ((bf16[16,128,256]{2,1,0:T(8,128)(2,1)}), bf16[16,128,256]{2,1,0:T(8,128)(2,1)S(1)}, u32[]{:S(2)}, u32[]{:S(2)}) async-start(bf16[16,128,256]{2,1,0:T(8,128)(2,1)} %get-tuple-element.16), calls=%async_computation.1 | async-start | bytes 2097152 | tf_op jit(solution)/shard_map/all_to_all | solution.py:232
  47.3 38.9 %copy-start = (bf16[256,256]{1,0:T(8,128)(2,1)S(1)}, bf16[256,256]{1,0:T(8,128)(2,1)}, u32[]{:S(2)}) copy-start(bf16[256,256]{1,0:T(8,128)(2,1)} %weight_ref.1) | copy-start | bytes 393220
  47.3 38.9 %copy-start.1 = (f32[256]{0:T(256)S(1)}, f32[256]{0:T(256)}, u32[]{:S(2)}) copy-start(f32[256]{0:T(256)} %param.11) | copy-start | bytes 3076
  62.6 20.4 %all-to-all-start = ((bf16[16,128,256]{2,1,0:T(8,128)(2,1)}), bf16[16,128,256]{2,1,0:T(8,128)(2,1)S(1)}, u32[]{:S(2)}, u32[]{:S(2)}) async-start(bf16[16,128,256]{2,1,0:T(8,128)(2,1)} %near_terms.1), calls=%async_computation | async-start | bytes 2097152 | tf_op jit(solution)/shard_map/all_to_all | solution.py:233
  69.1 17.1 %collective-permute-start.7 = (bf16[128,256]{1,0:T(8,128)(2,1)S(1)}, bf16[128,256]{1,0:T(8,128)(2,1)S(1)}, u32[]{:S(2)}, u32[]{:S(2)}) collective-permute-start(bf16[128,256]{1,0:T(8,128)(2,1)S(1)} %send.1), channel_id=1, source_target_pairs={{0,1},{1,0},{2,3},{3,2},{4,5},{5,4},{6,7},{7,6},{8,9},{9,8},{10,11... | collective-permute-start | bytes 196616 | tf_op jit(solution)/shard_map/ppermute | solution.py:235

commit v9 on v8

--- a/solution.py
+++ b/solution.py
@@ -93,15 +93,10 @@
 
 
 def far_kernel(table_ref, lhs_ref, *refs):
-    trio, p6, ones, p7, core0, core1 = refs[:6]
-    stripe_ref, out_ref, made, sem = refs[6:]
-    near = {0: trio.at[0], 4: trio.at[1], 2: trio.at[2], 6: p6.at[0]}
-    near |= {1: ones.at[0], 5: ones.at[1], 3: ones.at[2], 7: p7.at[0]}
-    across = {d: core0.at[i] for i, d in enumerate((0, 4, 2, 6))}
-    across |= {d: core1.at[i] for i, d in enumerate((1, 5, 3, 7))}
-    for d in range(ZL):
-        stripe_ref[CORE * d] = near[d][...]
-        stripe_ref[CORE * d + 1] = across[d][...]
+    held, across, stripe_ref, out_ref, made, sem = refs
+    for i, d in enumerate((0, 4, 2, 6, 1, 5, 3, 7)):
+        stripe_ref[CORE * d] = held[i]
+        stripe_ref[CORE * d + 1] = across[i]
     group = X * Y // sem.shape[0]
     stores = []
     for g in range(sem.shape[0]):
@@ -209,22 +204,20 @@
     p4, table = lax.optimization_barrier((p4, table))
     p6 = hop(p4, 2)
     far_lhs = far_lhs_rows(table, blocks)
-    trio = jnp.concatenate([own, p4, p2], axis=0)
-    ones = hop(trio, 1)
     p6, far_lhs = lax.optimization_barrier((p6, far_lhs))
-    p7 = hop(p6, 1)
-    core0 = cross(jnp.concatenate([trio, p6], axis=0))
-    core1 = cross(jnp.concatenate([ones, p7], axis=0))
+    even = jnp.concatenate([own, p4, p2, p6], axis=0)
+    held = jnp.concatenate([even, hop(even, 1)], axis=0)
+    across = cross(held)
     half = (X * Y, BS, F)
     one = jax.ShapeDtypeStruct((BS, F), bf16)
     stripe, far_terms = whole(
         far_kernel,
-        [table, far_lhs, trio, p6, ones, p7, core0, core1],
+        [table, far_lhs, held, across],
         [jax.ShapeDtypeStruct(half, bf16)] * 2,
         "far_terms",
         (2 * X * Y * SLOTS * BS * BS * F, 4 << 20),
         limit=8 << 20,
-        specs=[SMEM] + [VMEM] * 7,
+        specs=[SMEM, VMEM, VMEM, VMEM],
         out_specs=[VMEM, ANY],
         scratch=[pltpu.VMEM(half, bf16), pltpu.SemaphoreType.DMA((4,))],
     )

time: 87.7 us -> 85.4 us (0.974)
  the two profiles are of different devices: /device:TPU:34 before, /device:TPU:2 now
where the time goes in v9:
time: 85.4 us; the launch traced here: 84.8 us
  starting transfers between devices  49.8 us (58%)
  waiting for transfers between devices  22.7 us (27%)
  Pallas kernels  11.1 us (13%)
  local copies, waits for them, and re-layouts  0.98 us (1%)
    ppermute x4, starting transfers between devices, hop(): return lax.ppermute(value, 'zl', [(z, z ^ bit) for z in range(ZL)])  20.5 us
    ppermute x1, starting transfers between devices, local(): other = lax.ppermute(send, 'zh', [(0, 1), (1, 0)])  13.5 us
    all_to_all x1, waiting for transfers between devices, local(): far_parts = lax.all_to_all(far_terms, ('x', 'y'), 0, 0)  10.5 us
    all_to_all x1, starting transfers between devices, local(): far_parts = lax.all_to_all(far_terms, ('x', 'y'), 0, 0)  7.49 us
    ppermute x4, waiting for transfers between devices, hop(): return lax.ppermute(value, 'zl', [(z, z ^ bit) for z in range(ZL)])  7.09 us
    all_to_all x1, starting transfers between devices, local(): near_parts = lax.all_to_all(near_terms, ('x', 'y'), 0, 0)  6.35 us
    pallas_call x1, Pallas kernels, near_half(): pl.pallas_call(near_kernel, grid_spec=pltpu.PrefetchScalarGridSpec(num_sc...  4.82 us
    pallas_call x4, Pallas kernels, whole(): pl.pallas_call(kernel, in_specs=specs or [VMEM] * len(ins), out_specs=out...  3.2 us
  transfers between devices with their start and end apart: 8, of which 7 were waited for; matrix products, arithmetic and copies ran while one was open for 0% of the time, Pallas kernels for 9%

profile of v9, /device:TPU:2, one launch (start us, length us, event | category | flops | bytes accessed | tf_op | source)
XLA Modules:
  0.0 84.8 jit_solution(1029432903422448655)
XLA Ops:
  0.0 9.1 %collective-permute-start = (bf16[1,128,256]{2,1,0:T(8,128)(2,1)}, bf16[1,128,256]{2,1,0:T(8,128)(2,1)S(1)}, u32[]{:S(2)}, u32[]{:S(2)}) collective-permute-start(bf16[1,128,256]{2,1,0:T(8,128)(2,1)} %bitcast.8), channel_id=1, source_target_pairs={{0,256},{64,320},{128,384},{192,448},{256,0},{320,64},{384,128},{4... | collective-permute-start | bytes 196616 | tf_op jit(solution)/shard_map/ppermute | solution.py:198
  9.1 0.8 copy-done.2
  10.0 5.3 %collective-permute-start.2 = (bf16[1,128,256]{2,1,0:T(8,128)(2,1)S(1)}, bf16[1,128,256]{2,1,0:T(8,128)(2,1)S(1)}, u32[]{:S(2)}, u32[]{:S(2)}) collective-permute-start(bf16[1,128,256]{2,1,0:T(8,128)(2,1)S(1)} %own.1), channel_id=1, source_target_pairs={{0,128},{64,192},{128,0},{192,64},{256,384},{320,448},{384,256},{4... | collective-permute-start | bytes 196616 | tf_op jit(solution)/shard_map/ppermute | solution.py:198
  15.3 0.1 pad.6.clone
  15.4 0.1 add_add_fusion.table_ref
  15.4 0.3 collective-permute-done
  15.7 2.4 %collective-permute-start.1 = (bf16[1,128,256]{2,1,0:T(8,128)(2,1)S(1)}, bf16[1,128,256]{2,1,0:T(8,128)(2,1)S(1)}, u32[]{:S(2)}, u32[]{:S(2)}) collective-permute-start(bf16[1,128,256]{2,1,0:T(8,128)(2,1)S(1)} %collective-permute-done), channel_id=1, source_target_pairs={{0,128},{64,192},{128,0},{192,64},{256,384},{320,448},{384,256},{4... | collective-permute-start | bytes 196616 | tf_op jit(solution)/shard_map/ppermute | solution.py:198
  18.1 3.1 %far_lhs.1.lhs_ref = bf16[16,128,512]{2,1,0:T(8,128)(2,1)S(1)} custom-call(s32[6,32]{1,0:T(8,128)S(1)} %add_add_fusion.table_ref, bf16[16,2,4,128,128]{4,3,2,1,0:T(8,128)(2,1)} %bitcast.10), custom_call_target="tpu_custom_call" | custom-call | bytes 4194304 | tf_op jit(solution)/shard_map/far_lhs/pallas_call | solution.py:73
  21.2 1.6 %collective-permute-done.1 = bf16[1,128,256]{2,1,0:T(8,128)(2,1)S(1)} collective-permute-done((bf16[1,128,256]{2,1,0:T(8,128)(2,1)S(1)}, bf16[1,128,256]{2,1,0:T(8,128)(2,1)S(1)}, u32[]{:S(2)}, u32[]{:S(2)}) %collective-permute-start.1) | collective-permute-done | bytes 65568 | tf_op jit(solution)/shard_map/ppermute | solution.py:198
  22.9 3.7 %collective-permute-start.3 = (bf16[4,128,256]{2,1,0:T(8,128)(2,1)S(1)}, bf16[4,128,256]{2,1,0:T(8,128)(2,1)S(1)}, u32[]{:S(2)}, u32[]{:S(2)}) collective-permute-start(bf16[4,128,256]{2,1,0:T(8,128)(2,1)S(1)} %pad_maximum_fusion), channel_id=1, source_target_pairs={{0,64},{64,0},{128,192},{192,128},{256,320},{320,256},{384,448},{4... | collective-permute-start | bytes 786440 | tf_op jit(solution)/shard_map/ppermute | solution.py:198
  26.6 5.2 %collective-permute-done.3 = bf16[4,128,256]{2,1,0:T(8,128)(2,1)S(1)} collective-permute-done((bf16[4,128,256]{2,1,0:T(8,128)(2,1)S(1)}, bf16[4,128,256]{2,1,0:T(8,128)(2,1)S(1)}, u32[]{:S(2)}, u32[]{:S(2)}) %collective-permute-start.3) | collective-permute-done | bytes 262176 | tf_op jit(solution)/shard_map/ppermute | solution.py:198
  31.9 1.9 %collective-permute-start.4 = (bf16[8,128,256]{2,1,0:T(8,128)(2,1)S(1)}, bf16[8,128,256]{2,1,0:T(8,128)(2,1)S(1)}, u32[]{:S(2)}, u32[]{:S(2)}) collective-permute-start(bf16[8,128,256]{2,1,0:T(8,128)(2,1)S(1)} %constant_dynamic-update-slice_fusion.refs_0_), channel_id=1, source_target_pairs={{0,32},{32,0},{1,33},{33,1},{2,34},{34,2},{3,35},{35,3},{4,36},{36... | collective-permute-start | bytes 1572872 | tf_op jit(solution)/shard_map/ppermute | solution.py:201
  33.8 1.9 %collective-permute-done.4.refs_1_ = bf16[8,128,256]{2,1,0:T(8,128)(2,1)S(1)} collective-permute-done((bf16[8,128,256]{2,1,0:T(8,128)(2,1)S(1)}, bf16[8,128,256]{2,1,0:T(8,128)(2,1)S(1)}, u32[]{:S(2)}, u32[]{:S(2)}) %collective-permute-start.4) | collective-permute-done | bytes 524320 | tf_op jit(solution)/shard_map/ppermute | solution.py:201
  35.7 2.1 %far_terms.1 = (bf16[16,128,256]{2,1,0:T(8,128)(2,1)S(1)}, bf16[16,128,256]{2,1,0:T(8,128)(2,1)}) custom-call(s32[6,32]{1,0:T(8,128)S(1)} %add_add_fusion.table_ref, bf16[16,128,512]{2,1,0:T(8,128)(2,1)S(1)} %far_lhs.1.lhs_ref, bf16[8,128,256]{2,1,0:T(8,128)(2,1)S(1)} %constant_dynamic-update-slice_fusion.refs_0_, ...), custom_call_target="tpu_custom_call" | custom-call | flops 536870912 | bytes 4194304 | tf_op jit(solution)/shard_map/far_terms/pallas_call | solution.py:28
  37.8 7.5 %all-to-all-start.1 = ((bf16[16,128,256]{2,1,0:T(8,128)(2,1)}), bf16[16,128,256]{2,1,0:T(8,128)(2,1)S(1)}, u32[]{:S(2)}, u32[]{:S(2)}) async-start(bf16[16,128,256]{2,1,0:T(8,128)(2,1)} %get-tuple-element.16), calls=%async_computation.1 | async-start | bytes 2097152 | tf_op jit(solution)/shard_map/all_to_all | solution.py:225
  45.3 0.0 copy-start.1
  45.3 4.8 %near_terms.1 = bf16[16,128,256]{2,1,0:T(8,128)(2,1)} custom-call(s32[6,32]{1,0:T(8,128)S(1)} %add_add_fusion.table_ref, bf16[16,2,4,128,128]{4,3,2,1,0:T(8,128)(2,1)} %bitcast.11, bf16[16,128,256]{2,1,0:T(8,128)(2,1)S(1)} %get-tuple-element.15.stripe_ref), custom_call_target="tpu_custom_call" | custom-call | flops 536870912 | bytes 4194304 | tf_op jit(solution)/shard_map/near_terms/pallas_call | solution.py:127
  50.2 10.5 %all-to-all-done.1.parts_ref = bf16[16,128,256]{2,1,0:T(8,128)(2,1)S(1)} async-done(((bf16[16,128,256]{2,1,0:T(8,128)(2,1)}), bf16[16,128,256]{2,1,0:T(8,128)(2,1)S(1)}, u32[]{:S(2)}, u32[]{:S(2)}) %all-to-all-start.1) | async-done | bytes 1048608 | tf_op jit(solution)/shard_map/all_to_all | solution.py:225
  60.6 6.3 %all-to-all-start = ((bf16[16,128,256]{2,1,0:T(8,128)(2,1)}), bf16[16,128,256]{2,1,0:T(8,128)(2,1)S(1)}, u32[]{:S(2)}, u32[]{:S(2)}) async-start(bf16[16,128,256]{2,1,0:T(8,128)(2,1)} %near_terms.1), calls=%async_computation | async-start | bytes 2097152 | tf_op jit(solution)/shard_map/all_to_all | solution.py:226
  67.0 0.1 send.1
  67.1 13.5 %collective-permute-start.5 = (bf16[128,256]{1,0:T(8,128)(2,1)S(1)}, bf16[128,256]{1,0:T(8,128)(2,1)S(1)}, u32[]{:S(2)}, u32[]{:S(2)}) collective-permute-start(bf16[128,256]{1,0:T(8,128)(2,1)S(1)} %send.1), channel_id=1, source_target_pairs={{0,1},{1,0},{2,3},{3,2},{4,5},{5,4},{6,7},{7,6},{8,9},{9,8},{10,11... | collective-permute-start | bytes 196616 | tf_op jit(solution)/shard_map/ppermute | solution.py:228
  80.7 0.3 all-to-all-done.parts_ref
  81.0 2.9 %collective-permute-done.5.other_ref = bf16[128,256]{1,0:T(8,128)(2,1)S(1)} collective-permute-done((bf16[128,256]{1,0:T(8,128)(2,1)S(1)}, bf16[128,256]{1,0:T(8,128)(2,1)S(1)}, u32[]{:S(2)}, u32[]{:S(2)}) %collective-permute-start.5) | collective-permute-done | bytes 65568 | tf_op jit(solution)/shard_map/ppermute | solution.py:228
  83.9 0.9 %finish.1 = bf16[128,256]{1,0:T(8,128)(2,1)} custom-call(bf16[16,128,256]{2,1,0:T(8,128)(2,1)S(1)} %all-to-all-done.parts_ref, bf16[128,256]{1,0:T(8,128)(2,1)S(1)} %collective-permute-done.5.other_ref, bf16[256,256]{1,0:T(8,128)(2,1)S(1)} %copy-done, f32[1,256]{1,0:T(1,128)S(1)} %bitcast.7), custom_call_target="tpu_custom_call" | custom-call | flops 16777216 | bytes 2097152 | tf_op jit(solution)/shard_map/finish/pallas_call | solution.py:28
  (17 shorter events, 0.1 us)
Async XLA Ops:
  0.0 15.7 %collective-permute-start = (bf16[1,128,256]{2,1,0:T(8,128)(2,1)}, bf16[1,128,256]{2,1,0:T(8,128)(2,1)S(1)}, u32[]{:S(2)}, u32[]{:S(2)}) collective-permute-start(bf16[1,128,256]{2,1,0:T(8,128)(2,1)} %bitcast.8), channel_id=1, source_target_pairs={{0,256},{64,320},{128,384},{192,448},{256,0},{320,64},{384,128},{4... | collective-permute-start | bytes 196616 | tf_op jit(solution)/shard_map/ppermute | solution.py:198
  9.1 0.9 %copy-start.2 = (bf16[128,256]{1,0:T(8,128)(2,1)S(1)}, bf16[128,256]{1,0:T(8,128)(2,1)}, u32[]{:S(2)}) copy-start(bf16[128,256]{1,0:T(8,128)(2,1)} %param.6) | copy-start | bytes 196612
  9.9 5.4 %copy-start.3 = (s32[32,4]{0,1:T(4,128)S(1)}, s32[32,4]{0,1:T(4,128)}, u32[]{:S(2)}) copy-start(s32[32,4]{0,1:T(4,128)} %param.8) | copy-start | bytes 1540
  9.9 5.4 %copy-start.4 = (s32[32,1]{0,1:T(1,128)S(1)}, s32[32,1]{0,1:T(1,128)}, u32[]{:S(2)}) copy-start(s32[32,1]{0,1:T(1,128)} %param.9) | copy-start | bytes 388
  10.0 12.9 %collective-permute-start.2 = (bf16[1,128,256]{2,1,0:T(8,128)(2,1)S(1)}, bf16[1,128,256]{2,1,0:T(8,128)(2,1)S(1)}, u32[]{:S(2)}, u32[]{:S(2)}) collective-permute-start(bf16[1,128,256]{2,1,0:T(8,128)(2,1)S(1)} %own.1), channel_id=1, source_target_pairs={{0,128},{64,192},{128,0},{192,64},{256,384},{320,448},{384,256},{4... | collective-permute-start | bytes 196616 | tf_op jit(solution)/shard_map/ppermute | solution.py:198
  15.7 7.2 %collective-permute-start.1 = (bf16[1,128,256]{2,1,0:T(8,128)(2,1)S(1)}, bf16[1,128,256]{2,1,0:T(8,128)(2,1)S(1)}, u32[]{:S(2)}, u32[]{:S(2)}) collective-permute-start(bf16[1,128,256]{2,1,0:T(8,128)(2,1)S(1)} %collective-permute-done), channel_id=1, source_target_pairs={{0,128},{64,192},{128,0},{192,64},{256,384},{320,448},{384,256},{4... | collective-permute-start | bytes 196616 | tf_op jit(solution)/shard_map/ppermute | solution.py:198
  22.9 9.0 %collective-permute-start.3 = (bf16[4,128,256]{2,1,0:T(8,128)(2,1)S(1)}, bf16[4,128,256]{2,1,0:T(8,128)(2,1)S(1)}, u32[]{:S(2)}, u32[]{:S(2)}) collective-permute-start(bf16[4,128,256]{2,1,0:T(8,128)(2,1)S(1)} %pad_maximum_fusion), channel_id=1, source_target_pairs={{0,64},{64,0},{128,192},{192,128},{256,320},{320,256},{384,448},{4... | collective-permute-start | bytes 786440 | tf_op jit(solution)/shard_map/ppermute | solution.py:198
  31.9 3.8 %collective-permute-start.4 = (bf16[8,128,256]{2,1,0:T(8,128)(2,1)S(1)}, bf16[8,128,256]{2,1,0:T(8,128)(2,1)S(1)}, u32[]{:S(2)}, u32[]{:S(2)}) collective-permute-start(bf16[8,128,256]{2,1,0:T(8,128)(2,1)S(1)} %constant_dynamic-update-slice_fusion.refs_0_), channel_id=1, source_target_pairs={{0,32},{32,0},{1,33},{33,1},{2,34},{34,2},{3,35},{35,3},{4,36},{36... | collective-permute-start | bytes 1572872 | tf_op jit(solution)/shard_map/ppermute | solution.py:201
  37.8 22.8 %all-to-all-start.1 = ((bf16[16,128,256]{2,1,0:T(8,128)(2,1)}), bf16[16,128,256]{2,1,0:T(8,128)(2,1)S(1)}, u32[]{:S(2)}, u32[]{:S(2)}) async-start(bf16[16,128,256]{2,1,0:T(8,128)(2,1)} %get-tuple-element.16), calls=%async_computation.1 | async-start | bytes 2097152 | tf_op jit(solution)/shard_map/all_to_all | solution.py:225
  45.3 38.6 %copy-start = (bf16[256,256]{1,0:T(8,128)(2,1)S(1)}, bf16[256,256]{1,0:T(8,128)(2,1)}, u32[]{:S(2)}) copy-start(bf16[256,256]{1,0:T(8,128)(2,1)} %weight_ref.1) | copy-start | bytes 393220
  45.3 38.6 %copy-start.1 = (f32[256]{0:T(256)S(1)}, f32[256]{0:T(256)}, u32[]{:S(2)}) copy-start(f32[256]{0:T(256)} %param.11) | copy-start | bytes 3076
  60.6 20.4 %all-to-all-start = ((bf16[16,128,256]{2,1,0:T(8,128)(2,1)}), bf16[16,128,256]{2,1,0:T(8,128)(2,1)S(1)}, u32[]{:S(2)}, u32[]{:S(2)}) async-start(bf16[16,128,256]{2,1,0:T(8,128)(2,1)} %near_terms.1), calls=%async_computation | async-start | bytes 2097152 | tf_op jit(solution)/shard_map/all_to_all | solution.py:226
  67.1 16.8 %collective-permute-start.5 = (bf16[128,256]{1,0:T(8,128)(2,1)S(1)}, bf16[128,256]{1,0:T(8,128)(2,1)S(1)}, u32[]{:S(2)}, u32[]{:S(2)}) collective-permute-start(bf16[128,256]{1,0:T(8,128)(2,1)S(1)} %send.1), channel_id=1, source_target_pairs={{0,1},{1,0},{2,3},{3,2},{4,5},{5,4},{6,7},{7,6},{8,9},{9,8},{10,11... | collective-permute-start | bytes 196616 | tf_op jit(solution)/shard_map/ppermute | solution.py:228

commit v10 on v9

--- a/solution.py
+++ b/solution.py
@@ -7,7 +7,7 @@
 
 ZL, CORE, X, Y, ZH = 8, 2, 4, 4, 2
 SLOTS, BS, F = 4, 128, 256
-COUNT, HALF = SLOTS, SLOTS + 1
+COUNT, HALF, SIDE = range(SLOTS, SLOTS + 3)
 LONG = (1 << 35, 1 << 26)
 VMEM = pl.BlockSpec(memory_space=pltpu.VMEM)
 SMEM = pl.BlockSpec(memory_space=pltpu.SMEM)
@@ -92,6 +92,10 @@
     )(table, blocks)
 
 
+def turned(j):
+    return j % X * X + j // X
+
+
 def far_kernel(table_ref, lhs_ref, *refs):
     held, across, stripe_ref, out_ref, made, sem = refs
     for i, d in enumerate((0, 4, 2, 6, 1, 5, 3, 7)):
@@ -101,9 +105,9 @@
     stores = []
     for g in range(sem.shape[0]):
         for j in range(g * group, (g + 1) * group):
-            made[j] = product(
-                table_ref, 2 * j + 1 - table_ref[HALF, 0], lhs_ref[j], stripe_ref
-            )
+            pair = jnp.where(table_ref[SIDE, 0] == 0, j, turned(j))
+            row = 2 * pair + 1 - table_ref[HALF, 0]
+            made[j] = product(table_ref, row, lhs_ref[pair], stripe_ref)
         part = pl.ds(g * group, group)
         stores.append(
             pltpu.make_async_copy(made.at[part], out_ref.at[part], sem.at[g])
@@ -117,13 +121,15 @@
     step = blocks_ref.shape[0]
     base = pl.program_id(0) * step
     for i in range(step):
-        row = 2 * (base + i) + table_ref[HALF, 0]
+        pair = base + i
+        row = 2 * pair + table_ref[HALF, 0]
         lhs = side_by_side(table_ref, row, lambda k: blocks_ref[i, 0, k])
-        out_ref[i] = product(table_ref, row, lhs, stripe_ref)
+        spot = jnp.where(table_ref[SIDE, 0] == 0, pair, i * X + pl.program_id(0))
+        out_ref[spot] = product(table_ref, row, lhs, stripe_ref)
 
 
 def near_half(table, blocks, stripe):
-    step = 4
+    step = Y
     return pl.pallas_call(
         near_kernel,
         grid_spec=pltpu.PrefetchScalarGridSpec(
@@ -136,7 +142,7 @@
                 ),
                 VMEM,
             ],
-            out_specs=pl.BlockSpec((step, BS, F), lambda i, *_: (i, 0, 0)),
+            out_specs=pl.BlockSpec((X * Y, BS, F), lambda i, *_: (0, 0, 0)),
         ),
         out_shape=jax.ShapeDtypeStruct((X * Y, BS, F), jnp.bfloat16),
         compiler_params=pltpu.CompilerParams(vmem_limit_bytes=8 << 20),
@@ -178,7 +184,15 @@
     )
     spots = block_col.T ^ (CORE * zl + core)
     counts = row_count.T
-    return jnp.concatenate([spots, counts, jnp.full_like(counts, zh)], axis=0)
+    return jnp.concatenate(
+        [spots, counts, jnp.full_like(counts, zh), jnp.full_like(counts, core)], axis=0
+    )
+
+
+def exchange(value):
+    plane = range(X * Y)
+    groups = [list(plane), [X * Y + turned(j) for j in plane]]
+    return lax.all_to_all(value, ("core", "x", "y"), 0, 0, axis_index_groups=groups)
 
 
 def local(features, blocks, block_col, row_count, weight, out_bias):
@@ -222,8 +236,7 @@
         scratch=[pltpu.VMEM(half, bf16), pltpu.SemaphoreType.DMA((4,))],
     )
     near_terms = near_half(table, blocks, stripe)
-    far_parts = lax.all_to_all(far_terms, ("x", "y"), 0, 0)
-    near_parts = lax.all_to_all(near_terms, ("x", "y"), 0, 0)
+    far_parts, near_parts = exchange(far_terms), exchange(near_terms)
     send = whole(send_kernel, [far_parts], one, "send", (0, 1 << 20))
     other = lax.ppermute(send, "zh", [(0, 1), (1, 0)])
     return whole(

time: 85.4 us -> 86.1 us (level)
  waiting for transfers between devices: 22.7 us -> 24.4 us
  starting transfers between devices: 49.8 us -> 48.8 us
    all_to_all x2, waiting for transfers between devices: 10.8 us -> 12.8 us  [exchange(): lax.all_to_all(value, ('core', 'x', 'y'), 0, 0, axis_index_groups=groups)]
where the time goes in v10:
time: 86.1 us; the launch traced here: 85.6 us
  starting transfers between devices  48.8 us (57%)
  waiting for transfers between devices  24.4 us (28%)
  Pallas kernels  11 us (13%)
  local copies, waits for them, and re-layouts  1.05 us (1%)
    ppermute x4, starting transfers between devices, hop(): return lax.ppermute(value, 'zl', [(z, z ^ bit) for z in range(ZL)])  20.4 us
    ppermute x1, starting transfers between devices, local(): other = lax.ppermute(send, 'zh', [(0, 1), (1, 0)])  13.5 us
    all_to_all x2, starting transfers between devices, exchange(): lax.all_to_all(value, ('core', 'x', 'y'), 0, 0, axis_index_groups=groups)  13 us
    all_to_all x2, waiting for transfers between devices, exchange(): lax.all_to_all(value, ('core', 'x', 'y'), 0, 0, axis_index_groups=groups)  12.8 us
    ppermute x4, waiting for transfers between devices, hop(): return lax.ppermute(value, 'zl', [(z, z ^ bit) for z in range(ZL)])  7.09 us
    pallas_call x1, Pallas kernels, near_half(): pl.pallas_call(near_kernel, grid_spec=pltpu.PrefetchScalarGridSpec(num_sc...  4.73 us
    pallas_call x4, Pallas kernels, whole(): pl.pallas_call(kernel, in_specs=specs or [VMEM] * len(ins), out_specs=out...  3.2 us
    pallas_call x1, Pallas kernels, far_lhs_rows(): pl.pallas_call(far_lhs_kernel, grid_spec=pltpu.PrefetchScalarGridSpec(num...  3.11 us
  transfers between devices with their start and end apart: 8, of which 7 were waited for; matrix products, arithmetic and copies ran while one was open for 0% of the time, Pallas kernels for 9%

profile of v10, /device:TPU:2, one launch (start us, length us, event | category | flops | bytes accessed | tf_op | source)
XLA Modules:
  0.0 85.6 jit_solution(17465817577755292630)
XLA Ops:
  0.0 9.1 %collective-permute-start = (bf16[1,128,256]{2,1,0:T(8,128)(2,1)}, bf16[1,128,256]{2,1,0:T(8,128)(2,1)S(1)}, u32[]{:S(2)}, u32[]{:S(2)}) collective-permute-start(bf16[1,128,256]{2,1,0:T(8,128)(2,1)} %bitcast.9), channel_id=1, source_target_pairs={{0,256},{64,320},{128,384},{192,448},{256,0},{320,64},{384,128},{4... | collective-permute-start | bytes 196616 | tf_op jit(solution)/shard_map/ppermute | solution.py:212
  9.1 0.8 copy-done.2
  10.0 5.3 %collective-permute-start.2 = (bf16[1,128,256]{2,1,0:T(8,128)(2,1)S(1)}, bf16[1,128,256]{2,1,0:T(8,128)(2,1)S(1)}, u32[]{:S(2)}, u32[]{:S(2)}) collective-permute-start(bf16[1,128,256]{2,1,0:T(8,128)(2,1)S(1)} %own.1), channel_id=1, source_target_pairs={{0,128},{64,192},{128,0},{192,64},{256,384},{320,448},{384,256},{4... | collective-permute-start | bytes 196616 | tf_op jit(solution)/shard_map/ppermute | solution.py:212
  15.3 0.1 pad.6.clone
  15.4 0.1 pad.7.clone
  15.4 0.1 add_add_fusion.table_ref
  15.5 0.2 collective-permute-done
  15.7 2.4 %collective-permute-start.1 = (bf16[1,128,256]{2,1,0:T(8,128)(2,1)S(1)}, bf16[1,128,256]{2,1,0:T(8,128)(2,1)S(1)}, u32[]{:S(2)}, u32[]{:S(2)}) collective-permute-start(bf16[1,128,256]{2,1,0:T(8,128)(2,1)S(1)} %collective-permute-done), channel_id=1, source_target_pairs={{0,128},{64,192},{128,0},{192,64},{256,384},{320,448},{384,256},{4... | collective-permute-start | bytes 196616 | tf_op jit(solution)/shard_map/ppermute | solution.py:212
  18.1 3.1 %far_lhs.1.lhs_ref = bf16[16,128,512]{2,1,0:T(8,128)(2,1)S(1)} custom-call(s32[7,32]{1,0:T(8,128)S(1)} %add_add_fusion.table_ref, bf16[16,2,4,128,128]{4,3,2,1,0:T(8,128)(2,1)} %bitcast.11), custom_call_target="tpu_custom_call" | custom-call | bytes 4194304 | tf_op jit(solution)/shard_map/far_lhs/pallas_call | solution.py:73
  21.2 1.7 %collective-permute-done.1 = bf16[1,128,256]{2,1,0:T(8,128)(2,1)S(1)} collective-permute-done((bf16[1,128,256]{2,1,0:T(8,128)(2,1)S(1)}, bf16[1,128,256]{2,1,0:T(8,128)(2,1)S(1)}, u32[]{:S(2)}, u32[]{:S(2)}) %collective-permute-start.1) | collective-permute-done | bytes 65568 | tf_op jit(solution)/shard_map/ppermute | solution.py:212
  23.0 3.6 %collective-permute-start.3 = (bf16[4,128,256]{2,1,0:T(8,128)(2,1)S(1)}, bf16[4,128,256]{2,1,0:T(8,128)(2,1)S(1)}, u32[]{:S(2)}, u32[]{:S(2)}) collective-permute-start(bf16[4,128,256]{2,1,0:T(8,128)(2,1)S(1)} %pad_maximum_fusion), channel_id=1, source_target_pairs={{0,64},{64,0},{128,192},{192,128},{256,320},{320,256},{384,448},{4... | collective-permute-start | bytes 786440 | tf_op jit(solution)/shard_map/ppermute | solution.py:212
  26.6 5.2 %collective-permute-done.3 = bf16[4,128,256]{2,1,0:T(8,128)(2,1)S(1)} collective-permute-done((bf16[4,128,256]{2,1,0:T(8,128)(2,1)S(1)}, bf16[4,128,256]{2,1,0:T(8,128)(2,1)S(1)}, u32[]{:S(2)}, u32[]{:S(2)}) %collective-permute-start.3) | collective-permute-done | bytes 262176 | tf_op jit(solution)/shard_map/ppermute | solution.py:212
  31.9 1.9 %collective-permute-start.4 = (bf16[8,128,256]{2,1,0:T(8,128)(2,1)S(1)}, bf16[8,128,256]{2,1,0:T(8,128)(2,1)S(1)}, u32[]{:S(2)}, u32[]{:S(2)}) collective-permute-start(bf16[8,128,256]{2,1,0:T(8,128)(2,1)S(1)} %constant_dynamic-update-slice_fusion.refs_0_), channel_id=1, source_target_pairs={{0,32},{32,0},{1,33},{33,1},{2,34},{34,2},{3,35},{35,3},{4,36},{36... | collective-permute-start | bytes 1572872 | tf_op jit(solution)/shard_map/ppermute | solution.py:215
  33.8 1.9 %collective-permute-done.4.refs_1_ = bf16[8,128,256]{2,1,0:T(8,128)(2,1)S(1)} collective-permute-done((bf16[8,128,256]{2,1,0:T(8,128)(2,1)S(1)}, bf16[8,128,256]{2,1,0:T(8,128)(2,1)S(1)}, u32[]{:S(2)}, u32[]{:S(2)}) %collective-permute-start.4) | collective-permute-done | bytes 524320 | tf_op jit(solution)/shard_map/ppermute | solution.py:215
  35.7 2.1 %far_terms.1 = (bf16[16,128,256]{2,1,0:T(8,128)(2,1)S(1)}, bf16[16,128,256]{2,1,0:T(8,128)(2,1)}) custom-call(s32[7,32]{1,0:T(8,128)S(1)} %add_add_fusion.table_ref, bf16[16,128,512]{2,1,0:T(8,128)(2,1)S(1)} %far_lhs.1.lhs_ref, bf16[8,128,256]{2,1,0:T(8,128)(2,1)S(1)} %constant_dynamic-update-slice_fusion.refs_0_, ...), custom_call_target="tpu_custom_call" | custom-call | flops 536870912 | bytes 4194304 | tf_op jit(solution)/shard_map/far_terms/pallas_call | solution.py:28
  37.8 7.5 %all-to-all-start.1 = ((bf16[16,128,256]{2,1,0:T(8,128)(2,1)}), bf16[16,128,256]{2,1,0:T(8,128)(2,1)S(1)}, u32[]{:S(2)}, u32[]{:S(2)}) async-start(bf16[16,128,256]{2,1,0:T(8,128)(2,1)} %get-tuple-element.16), calls=%async_computation.1 | async-start | bytes 2097152 | tf_op jit(solution)/shard_map/all_to_all | solution.py:195
  45.3 4.7 %near_terms.1 = bf16[16,128,256]{2,1,0:T(8,128)(2,1)} custom-call(s32[7,32]{1,0:T(8,128)S(1)} %add_add_fusion.table_ref, bf16[16,2,4,128,128]{4,3,2,1,0:T(8,128)(2,1)} %bitcast.12, bf16[16,128,256]{2,1,0:T(8,128)(2,1)S(1)} %get-tuple-element.15.stripe_ref), custom_call_target="tpu_custom_call" | custom-call | flops 536870912 | bytes 4194304 | tf_op jit(solution)/shard_map/near_terms/pallas_call | solution.py:133
  50.1 11.2 %all-to-all-done.1.parts_ref = bf16[16,128,256]{2,1,0:T(8,128)(2,1)S(1)} async-done(((bf16[16,128,256]{2,1,0:T(8,128)(2,1)}), bf16[16,128,256]{2,1,0:T(8,128)(2,1)S(1)}, u32[]{:S(2)}, u32[]{:S(2)}) %all-to-all-start.1) | async-done | bytes 1048608 | tf_op jit(solution)/shard_map/all_to_all | solution.py:195
  61.3 5.5 %all-to-all-start = ((bf16[16,128,256]{2,1,0:T(8,128)(2,1)}), bf16[16,128,256]{2,1,0:T(8,128)(2,1)S(1)}, u32[]{:S(2)}, u32[]{:S(2)}) async-start(bf16[16,128,256]{2,1,0:T(8,128)(2,1)} %near_terms.1), calls=%async_computation | async-start | bytes 2097152 | tf_op jit(solution)/shard_map/all_to_all | solution.py:195
  66.8 0.1 send.1
  66.9 13.5 %collective-permute-start.5 = (bf16[128,256]{1,0:T(8,128)(2,1)S(1)}, bf16[128,256]{1,0:T(8,128)(2,1)S(1)}, u32[]{:S(2)}, u32[]{:S(2)}) collective-permute-start(bf16[128,256]{1,0:T(8,128)(2,1)S(1)} %send.1), channel_id=1, source_target_pairs={{0,1},{1,0},{2,3},{3,2},{4,5},{5,4},{6,7},{7,6},{8,9},{9,8},{10,11... | collective-permute-start | bytes 196616 | tf_op jit(solution)/shard_map/ppermute | solution.py:241
  80.5 1.6 %all-to-all-done.parts_ref = bf16[16,128,256]{2,1,0:T(8,128)(2,1)S(1)} async-done(((bf16[16,128,256]{2,1,0:T(8,128)(2,1)}), bf16[16,128,256]{2,1,0:T(8,128)(2,1)S(1)}, u32[]{:S(2)}, u32[]{:S(2)}) %all-to-all-start) | async-done | bytes 1048608 | tf_op jit(solution)/shard_map/all_to_all | solution.py:195
  82.0 2.6 %collective-permute-done.5.other_ref = bf16[128,256]{1,0:T(8,128)(2,1)S(1)} collective-permute-done((bf16[128,256]{1,0:T(8,128)(2,1)S(1)}, bf16[128,256]{1,0:T(8,128)(2,1)S(1)}, u32[]{:S(2)}, u32[]{:S(2)}) %collective-permute-start.5) | collective-permute-done | bytes 65568 | tf_op jit(solution)/shard_map/ppermute | solution.py:241
  84.7 0.9 %finish.1 = bf16[128,256]{1,0:T(8,128)(2,1)} custom-call(bf16[16,128,256]{2,1,0:T(8,128)(2,1)S(1)} %all-to-all-done.parts_ref, bf16[128,256]{1,0:T(8,128)(2,1)S(1)} %collective-permute-done.5.other_ref, bf16[256,256]{1,0:T(8,128)(2,1)S(1)} %copy-done, f32[1,256]{1,0:T(1,128)S(1)} %bitcast.8), custom_call_target="tpu_custom_call" | custom-call | flops 16777216 | bytes 2097152 | tf_op jit(solution)/shard_map/finish/pallas_call | solution.py:28
  (18 shorter events, 0.1 us)
Async XLA Ops:
  0.0 15.7 %collective-permute-start = (bf16[1,128,256]{2,1,0:T(8,128)(2,1)}, bf16[1,128,256]{2,1,0:T(8,128)(2,1)S(1)}, u32[]{:S(2)}, u32[]{:S(2)}) collective-permute-start(bf16[1,128,256]{2,1,0:T(8,128)(2,1)} %bitcast.9), channel_id=1, source_target_pairs={{0,256},{64,320},{128,384},{192,448},{256,0},{320,64},{384,128},{4... | collective-permute-start | bytes 196616 | tf_op jit(solution)/shard_map/ppermute | solution.py:212
  9.1 0.9 copy-start.2
  9.9 5.5 %copy-start.3 = (s32[32,4]{0,1:T(4,128)S(1)}, s32[32,4]{0,1:T(4,128)}, u32[]{:S(2)}) copy-start(s32[32,4]{0,1:T(4,128)} %param.8) | copy-start | bytes 1540
  9.9 5.5 %copy-start.4 = (s32[32,1]{0,1:T(1,128)S(1)}, s32[32,1]{0,1:T(1,128)}, u32[]{:S(2)}) copy-start(s32[32,1]{0,1:T(1,128)} %param.9) | copy-start | bytes 388
  10.0 13.0 %collective-permute-start.2 = (bf16[1,128,256]{2,1,0:T(8,128)(2,1)S(1)}, bf16[1,128,256]{2,1,0:T(8,128)(2,1)S(1)}, u32[]{:S(2)}, u32[]{:S(2)}) collective-permute-start(bf16[1,128,256]{2,1,0:T(8,128)(2,1)S(1)} %own.1), channel_id=1, source_target_pairs={{0,128},{64,192},{128,0},{192,64},{256,384},{320,448},{384,256},{4... | collective-permute-start | bytes 196616 | tf_op jit(solution)/shard_map/ppermute | solution.py:212
  15.7 7.2 %collective-permute-start.1 = (bf16[1,128,256]{2,1,0:T(8,128)(2,1)S(1)}, bf16[1,128,256]{2,1,0:T(8,128)(2,1)S(1)}, u32[]{:S(2)}, u32[]{:S(2)}) collective-permute-start(bf16[1,128,256]{2,1,0:T(8,128)(2,1)S(1)} %collective-permute-done), channel_id=1, source_target_pairs={{0,128},{64,192},{128,0},{192,64},{256,384},{320,448},{384,256},{4... | collective-permute-start | bytes 196616 | tf_op jit(solution)/shard_map/ppermute | solution.py:212
  23.0 8.9 %collective-permute-start.3 = (bf16[4,128,256]{2,1,0:T(8,128)(2,1)S(1)}, bf16[4,128,256]{2,1,0:T(8,128)(2,1)S(1)}, u32[]{:S(2)}, u32[]{:S(2)}) collective-permute-start(bf16[4,128,256]{2,1,0:T(8,128)(2,1)S(1)} %pad_maximum_fusion), channel_id=1, source_target_pairs={{0,64},{64,0},{128,192},{192,128},{256,320},{320,256},{384,448},{4... | collective-permute-start | bytes 786440 | tf_op jit(solution)/shard_map/ppermute | solution.py:212
  31.9 3.8 %collective-permute-start.4 = (bf16[8,128,256]{2,1,0:T(8,128)(2,1)S(1)}, bf16[8,128,256]{2,1,0:T(8,128)(2,1)S(1)}, u32[]{:S(2)}, u32[]{:S(2)}) collective-permute-start(bf16[8,128,256]{2,1,0:T(8,128)(2,1)S(1)} %constant_dynamic-update-slice_fusion.refs_0_), channel_id=1, source_target_pairs={{0,32},{32,0},{1,33},{33,1},{2,34},{34,2},{3,35},{35,3},{4,36},{36... | collective-permute-start | bytes 1572872 | tf_op jit(solution)/shard_map/ppermute | solution.py:215
  37.8 23.5 %all-to-all-start.1 = ((bf16[16,128,256]{2,1,0:T(8,128)(2,1)}), bf16[16,128,256]{2,1,0:T(8,128)(2,1)S(1)}, u32[]{:S(2)}, u32[]{:S(2)}) async-start(bf16[16,128,256]{2,1,0:T(8,128)(2,1)} %get-tuple-element.16), calls=%async_computation.1 | async-start | bytes 2097152 | tf_op jit(solution)/shard_map/all_to_all | solution.py:195
  45.3 39.3 %copy-start = (bf16[256,256]{1,0:T(8,128)(2,1)S(1)}, bf16[256,256]{1,0:T(8,128)(2,1)}, u32[]{:S(2)}) copy-start(bf16[256,256]{1,0:T(8,128)(2,1)} %weight_ref.1) | copy-start | bytes 393220
  45.3 39.3 %copy-start.1 = (f32[256]{0:T(256)S(1)}, f32[256]{0:T(256)}, u32[]{:S(2)}) copy-start(f32[256]{0:T(256)} %param.11) | copy-start | bytes 3076
  61.3 20.7 %all-to-all-start = ((bf16[16,128,256]{2,1,0:T(8,128)(2,1)}), bf16[16,128,256]{2,1,0:T(8,128)(2,1)S(1)}, u32[]{:S(2)}, u32[]{:S(2)}) async-start(bf16[16,128,256]{2,1,0:T(8,128)(2,1)} %near_terms.1), calls=%async_computation | async-start | bytes 2097152 | tf_op jit(solution)/shard_map/all_to_all | solution.py:195
  66.9 17.7 %collective-permute-start.5 = (bf16[128,256]{1,0:T(8,128)(2,1)S(1)}, bf16[128,256]{1,0:T(8,128)(2,1)S(1)}, u32[]{:S(2)}, u32[]{:S(2)}) collective-permute-start(bf16[128,256]{1,0:T(8,128)(2,1)S(1)} %send.1), channel_id=1, source_target_pairs={{0,1},{1,0},{2,3},{3,2},{4,5},{5,4},{6,7},{7,6},{8,9},{9,8},{10,11... | collective-permute-start | bytes 196616 | tf_op jit(solution)/shard_map/ppermute | solution.py:241

commit v11 on v9

--- a/solution.py
+++ b/solution.py
@@ -60,25 +60,27 @@
     return term.astype(jnp.bfloat16)
 
 
-def far_lhs_kernel(table_ref, blocks_ref, out_ref):
-    step = blocks_ref.shape[0]
-    base = pl.program_id(0) * step
-    for i in range(step):
-        row = 2 * (base + i) + 1 - table_ref[HALF, 0]
-        out_ref[i] = side_by_side(table_ref, row, lambda k: blocks_ref[i, 0, k])
-
-
-def far_lhs_rows(table, blocks):
+def lhs_rows(table, blocks, far):
     step = 4
+
+    def half(table_ref):
+        return 1 - table_ref[HALF, 0] if far else table_ref[HALF, 0]
+
+    def kernel(table_ref, blocks_ref, out_ref):
+        base = pl.program_id(0) * step
+        for i in range(step):
+            row = 2 * (base + i) + half(table_ref)
+            out_ref[i] = side_by_side(table_ref, row, lambda k: blocks_ref[i, 0, k])
+
     return pl.pallas_call(
-        far_lhs_kernel,
+        kernel,
         grid_spec=pltpu.PrefetchScalarGridSpec(
             num_scalar_prefetch=1,
             grid=(X * Y // step,),
             in_specs=[
                 pl.BlockSpec(
                     (step, 1, SLOTS, BS, BS),
-                    lambda i, table_ref: (i, 1 - table_ref[HALF, 0], 0, 0, 0),
+                    lambda i, table_ref: (i, half(table_ref), 0, 0, 0),
                 )
             ],
             out_specs=pl.BlockSpec((step, BS, SLOTS * BS), lambda i, *_: (i, 0, 0)),
@@ -88,65 +90,40 @@
         cost_estimate=pl.CostEstimate(
             flops=0, bytes_accessed=4 << 20, transcendentals=0
         ),
-        name="far_lhs",
+        name="far_lhs" if far else "near_lhs",
     )(table, blocks)
 
 
-def far_kernel(table_ref, lhs_ref, *refs):
-    held, across, stripe_ref, out_ref, made, sem = refs
+def terms_kernel(
+    table_ref,
+    far_lhs_ref,
+    near_lhs_ref,
+    held_ref,
+    across_ref,
+    far_ref,
+    near_ref,
+    stripe_ref,
+    made,
+    sem,
+):
+    zh = table_ref[HALF, 0]
     for i, d in enumerate((0, 4, 2, 6, 1, 5, 3, 7)):
-        stripe_ref[CORE * d] = held[i]
-        stripe_ref[CORE * d + 1] = across[i]
+        stripe_ref[CORE * d] = held_ref[i]
+        stripe_ref[CORE * d + 1] = across_ref[i]
     group = X * Y // sem.shape[0]
     stores = []
     for g in range(sem.shape[0]):
         for j in range(g * group, (g + 1) * group):
-            made[j] = product(
-                table_ref, 2 * j + 1 - table_ref[HALF, 0], lhs_ref[j], stripe_ref
-            )
+            made[j] = product(table_ref, 2 * j + zh, near_lhs_ref[j], stripe_ref)
         part = pl.ds(g * group, group)
         stores.append(
-            pltpu.make_async_copy(made.at[part], out_ref.at[part], sem.at[g])
+            pltpu.make_async_copy(made.at[part], near_ref.at[part], sem.at[g])
         )
         stores[-1].start()
+    for j in range(X * Y):
+        far_ref[j] = product(table_ref, 2 * j + 1 - zh, far_lhs_ref[j], stripe_ref)
     for store in stores:
         store.wait()
-
-
-def near_kernel(table_ref, blocks_ref, stripe_ref, out_ref):
-    step = blocks_ref.shape[0]
-    base = pl.program_id(0) * step
-    for i in range(step):
-        row = 2 * (base + i) + table_ref[HALF, 0]
-        lhs = side_by_side(table_ref, row, lambda k: blocks_ref[i, 0, k])
-        out_ref[i] = product(table_ref, row, lhs, stripe_ref)
-
-
-def near_half(table, blocks, stripe):
-    step = 4
-    return pl.pallas_call(
-        near_kernel,
-        grid_spec=pltpu.PrefetchScalarGridSpec(
-            num_scalar_prefetch=1,
-            grid=(X * Y // step,),
-            in_specs=[
-                pl.BlockSpec(
-                    (step, 1, SLOTS, BS, BS),
-                    lambda i, table_ref: (i, table_ref[HALF, 0], 0, 0, 0),
-                ),
-                VMEM,
-            ],
-            out_specs=pl.BlockSpec((step, BS, F), lambda i, *_: (i, 0, 0)),
-        ),
-        out_shape=jax.ShapeDtypeStruct((X * Y, BS, F), jnp.bfloat16),
-        compiler_params=pltpu.CompilerParams(vmem_limit_bytes=8 << 20),
-        cost_estimate=pl.CostEstimate(
-            flops=2 * X * Y * SLOTS * BS * BS * F,
-            bytes_accessed=4 << 20,
-            transcendentals=0,
-        ),
-        name="near_terms",
-    )(table, blocks, stripe)
 
 
 def total(parts):
@@ -203,25 +180,31 @@
     p4, p2 = hop(features[None], 4), hop(own, 2)
     p4, table = lax.optimization_barrier((p4, table))
     p6 = hop(p4, 2)
-    far_lhs = far_lhs_rows(table, blocks)
+    far_lhs = lhs_rows(table, blocks, True)
     p6, far_lhs = lax.optimization_barrier((p6, far_lhs))
     even = jnp.concatenate([own, p4, p2, p6], axis=0)
-    held = jnp.concatenate([even, hop(even, 1)], axis=0)
+    even, table = lax.optimization_barrier((even, table))
+    near_lhs = lhs_rows(table, blocks, False)
+    odd, near_lhs = lax.optimization_barrier((hop(even, 1), near_lhs))
+    held = jnp.concatenate([even, odd], axis=0)
     across = cross(held)
     half = (X * Y, BS, F)
     one = jax.ShapeDtypeStruct((BS, F), bf16)
-    stripe, far_terms = whole(
-        far_kernel,
-        [table, far_lhs, held, across],
+    far_terms, near_terms = whole(
+        terms_kernel,
+        [table, far_lhs, near_lhs, held, across],
         [jax.ShapeDtypeStruct(half, bf16)] * 2,
-        "far_terms",
-        (2 * X * Y * SLOTS * BS * BS * F, 4 << 20),
+        "terms",
+        (4 * X * Y * SLOTS * BS * BS * F, 7 << 20),
         limit=8 << 20,
-        specs=[SMEM, VMEM, VMEM, VMEM],
+        specs=[SMEM] + [VMEM] * 4,
         out_specs=[VMEM, ANY],
-        scratch=[pltpu.VMEM(half, bf16), pltpu.SemaphoreType.DMA((4,))],
-    )
-    near_terms = near_half(table, blocks, stripe)
+        scratch=[
+            pltpu.VMEM((CORE * ZL, BS, F), bf16),
+            pltpu.VMEM(half, bf16),
+            pltpu.SemaphoreType.DMA((2,)),
+        ],
+    )
     far_parts = lax.all_to_all(far_terms, ("x", "y"), 0, 0)
     near_parts = lax.all_to_all(near_terms, ("x", "y"), 0, 0)
     send = whole(send_kernel, [far_parts], one, "send", (0, 1 << 20))

time: 85.4 us -> 89 us (1.042)
  blocking collectives: 0 us -> 22.4 us
  waiting for transfers between devices: 22.7 us -> 11.9 us
  starting transfers between devices: 49.8 us -> 41.8 us
  other arithmetic: 0.11 us -> 1.45 us
  Pallas kernels: 11.1 us -> 9.87 us
    all_to_all x0 -> x1, blocking collectives: none -> 22.4 us  [local(): far_parts = lax.all_to_all(far_terms, ('x', 'y'), 0, 0)]
    all_to_all x1 -> x0, waiting for transfers between devices: 10.5 us -> none  [local(): far_parts = lax.all_to_all(far_terms, ('x', 'y'), 0, 0)]
    all_to_all x1 -> x0, starting transfers between devices: 7.49 us -> none  [local(): far_parts = lax.all_to_all(far_terms, ('x', 'y'), 0, 0)]
    pallas_call x2, Pallas kernels: 7.93 us -> 6.22 us  [lhs_rows(): pl.pallas_call(kernel, grid_spec=pltpu.PrefetchScalarGridSpec(num_scalar_...]
  transfers between devices with their start and end apart: 8 -> 7, of which waited for: 7 -> 4; matrix products, arithmetic and copies ran while one was open for 0% -> 2% of each run, Pallas kernels for 9% -> 7%
where the time goes in v11:
time: 89 us; the launch traced here: 88.5 us
  starting transfers between devices  41.8 us (47%)
  blocking collectives  22.4 us (25%)
  waiting for transfers between devices  11.9 us (13%)
  Pallas kernels  9.87 us (11%)
  other arithmetic  1.45 us (2%)
  local copies, waits for them, and re-layouts  0.95 us (1%)
    all_to_all x1, blocking collectives, local(): far_parts = lax.all_to_all(far_terms, ('x', 'y'), 0, 0)  22.4 us
    ppermute x4, starting transfers between devices, hop(): return lax.ppermute(value, 'zl', [(z, z ^ bit) for z in range(ZL)])  19.8 us
    ppermute x1, starting transfers between devices, local(): other = lax.ppermute(send, 'zh', [(0, 1), (1, 0)])  14.1 us
    ppermute x4, waiting for transfers between devices, hop(): return lax.ppermute(value, 'zl', [(z, z ^ bit) for z in range(ZL)])  7 us
    pallas_call x2, Pallas kernels, lhs_rows(): pl.pallas_call(kernel, grid_spec=pltpu.PrefetchScalarGridSpec(num_scalar_...  6.22 us
    all_to_all x1, starting transfers between devices, local(): near_parts = lax.all_to_all(near_terms, ('x', 'y'), 0, 0)  5.97 us
    pallas_call x4, Pallas kernels, whole(): pl.pallas_call(kernel, in_specs=specs or [VMEM] * len(ins), out_specs=out...  3.65 us
    ppermute x1, waiting for transfers between devices, local(): other = lax.ppermute(send, 'zh', [(0, 1), (1, 0)])  2.97 us
  transfers between devices with their start and end apart: 7, of which 4 were waited for; matrix products, arithmetic and copies ran while one was open for 2% of the time, Pallas kernels for 7%

profile of v11, /device:TPU:2, one launch (start us, length us, event | category | flops | bytes accessed | tf_op | source)
XLA Modules:
  0.0 88.5 jit_solution(13281620035733329177)
XLA Ops:
  0.0 9.1 %collective-permute-start = (bf16[1,128,256]{2,1,0:T(8,128)(2,1)}, bf16[1,128,256]{2,1,0:T(8,128)(2,1)S(1)}, u32[]{:S(2)}, u32[]{:S(2)}) collective-permute-start(bf16[1,128,256]{2,1,0:T(8,128)(2,1)} %bitcast.8), channel_id=1, source_target_pairs={{0,256},{64,320},{128,384},{192,448},{256,0},{320,64},{384,128},{4... | collective-permute-start | bytes 196616 | tf_op jit(solution)/shard_map/ppermute | solution.py:175
  9.1 0.1 pad.6.clone
  9.2 0.7 xor_bitcast_fusion
  9.9 0.7 add_add_fusion.table_ref
  10.6 5.2 %collective-permute-done = bf16[1,128,256]{2,1,0:T(8,128)(2,1)S(1)} collective-permute-done((bf16[1,128,256]{2,1,0:T(8,128)(2,1)}, bf16[1,128,256]{2,1,0:T(8,128)(2,1)S(1)}, u32[]{:S(2)}, u32[]{:S(2)}) %collective-permute-start) | collective-permute-done | bytes 65568 | tf_op jit(solution)/shard_map/ppermute | solution.py:175
  15.7 2.4 %collective-permute-start.2 = (bf16[1,128,256]{2,1,0:T(8,128)(2,1)S(1)}, bf16[1,128,256]{2,1,0:T(8,128)(2,1)S(1)}, u32[]{:S(2)}, u32[]{:S(2)}) collective-permute-start(bf16[1,128,256]{2,1,0:T(8,128)(2,1)S(1)} %collective-permute-done), channel_id=1, source_target_pairs={{0,128},{64,192},{128,0},{192,64},{256,384},{320,448},{384,256},{4... | collective-permute-start | bytes 196616 | tf_op jit(solution)/shard_map/ppermute | solution.py:175
  18.1 0.0 copy-start.2
  18.1 0.8 copy-done.2
  19.0 4.4 %collective-permute-start.1 = (bf16[1,128,256]{2,1,0:T(8,128)(2,1)S(1)}, bf16[1,128,256]{2,1,0:T(8,128)(2,1)S(1)}, u32[]{:S(2)}, u32[]{:S(2)}) collective-permute-start(bf16[1,128,256]{2,1,0:T(8,128)(2,1)S(1)} %own.1), channel_id=1, source_target_pairs={{0,128},{64,192},{128,0},{192,64},{256,384},{320,448},{384,256},{4... | collective-permute-start | bytes 196616 | tf_op jit(solution)/shard_map/ppermute | solution.py:175
  23.3 3.1 %far_lhs.1.far_lhs_ref = bf16[16,128,512]{2,1,0:T(8,128)(2,1)S(1)} custom-call(s32[6,32]{1,0:T(8,128)S(1)} %add_add_fusion.table_ref, bf16[16,2,4,128,128]{4,3,2,1,0:T(8,128)(2,1)} %bitcast.10), custom_call_target="tpu_custom_call" | custom-call | bytes 4194304 | tf_op jit(solution)/shard_map/far_lhs/pallas_call | solution.py:75
  26.5 0.0 collective-permute-done.2
  26.5 4.0 %collective-permute-start.3 = (bf16[4,128,256]{2,1,0:T(8,128)(2,1)S(1)}, bf16[4,128,256]{2,1,0:T(8,128)(2,1)S(1)}, u32[]{:S(2)}, u32[]{:S(2)}) collective-permute-start(bf16[4,128,256]{2,1,0:T(8,128)(2,1)S(1)} %pad_maximum_fusion), channel_id=1, source_target_pairs={{0,64},{64,0},{128,192},{192,128},{256,320},{320,256},{384,448},{4... | collective-permute-start | bytes 786440 | tf_op jit(solution)/shard_map/ppermute | solution.py:175
  30.5 3.1 %near_lhs.1.near_lhs_ref = bf16[16,128,512]{2,1,0:T(8,128)(2,1)S(1)} custom-call(s32[6,32]{1,0:T(8,128)S(1)} %add_add_fusion.table_ref, bf16[16,2,4,128,128]{4,3,2,1,0:T(8,128)(2,1)} %bitcast.11), custom_call_target="tpu_custom_call" | custom-call | bytes 4194304 | tf_op jit(solution)/shard_map/near_lhs/pallas_call | solution.py:75
  33.7 1.8 %collective-permute-done.3 = bf16[4,128,256]{2,1,0:T(8,128)(2,1)S(1)} collective-permute-done((bf16[4,128,256]{2,1,0:T(8,128)(2,1)S(1)}, bf16[4,128,256]{2,1,0:T(8,128)(2,1)S(1)}, u32[]{:S(2)}, u32[]{:S(2)}) %collective-permute-start.3) | collective-permute-done | bytes 262176 | tf_op jit(solution)/shard_map/ppermute | solution.py:175
  35.5 1.9 %collective-permute-start.4 = (bf16[8,128,256]{2,1,0:T(8,128)(2,1)S(1)}, bf16[8,128,256]{2,1,0:T(8,128)(2,1)S(1)}, u32[]{:S(2)}, u32[]{:S(2)}) collective-permute-start(bf16[8,128,256]{2,1,0:T(8,128)(2,1)S(1)} %constant_dynamic-update-slice_fusion.held_ref), channel_id=1, source_target_pairs={{0,32},{32,0},{1,33},{33,1},{2,34},{34,2},{3,35},{35,3},{4,36},{36... | collective-permute-start | bytes 1572872 | tf_op jit(solution)/shard_map/ppermute | solution.py:178
  37.5 1.9 %collective-permute-done.4.across_ref = bf16[8,128,256]{2,1,0:T(8,128)(2,1)S(1)} collective-permute-done((bf16[8,128,256]{2,1,0:T(8,128)(2,1)S(1)}, bf16[8,128,256]{2,1,0:T(8,128)(2,1)S(1)}, u32[]{:S(2)}, u32[]{:S(2)}) %collective-permute-start.4) | collective-permute-done | bytes 524320 | tf_op jit(solution)/shard_map/ppermute | solution.py:178
  39.3 2.6 %terms.1 = (bf16[16,128,256]{2,1,0:T(8,128)(2,1)S(1)}, bf16[16,128,256]{2,1,0:T(8,128)(2,1)}) custom-call(s32[6,32]{1,0:T(8,128)S(1)} %add_add_fusion.table_ref, bf16[16,128,512]{2,1,0:T(8,128)(2,1)S(1)} %far_lhs.1.far_lhs_ref, bf16[16,128,512]{2,1,0:T(8,128)(2,1)S(1)} %near_lhs.1.near_lhs_ref, ...), custom_call_target="tpu_custom_call" | custom-call | flops 1073741824 | bytes 7340032 | tf_op jit(solution)/shard_map/terms/pallas_call | solution.py:28
  41.9 22.4 %all_to_all.10.parts_ref = bf16[16,128,256]{2,1,0:T(8,128)(2,1)S(1)} all-to-all(bf16[16,128,256]{2,1,0:T(8,128)(2,1)S(1)} %get-tuple-element.24), channel_id=1, replica_groups=mesh['zl'=8,'core'=2,'x'=4,'y'=4,'zh'=2] {'x','y'}, dimensions={0} | all-to-all | bytes 2097152 | tf_op jit(solution)/shard_map/all_to_all | solution.py:208
  64.3 6.0 %all-to-all-start = ((bf16[16,128,256]{2,1,0:T(8,128)(2,1)}), bf16[16,128,256]{2,1,0:T(8,128)(2,1)S(1)}, u32[]{:S(2)}, u32[]{:S(2)}) async-start(bf16[16,128,256]{2,1,0:T(8,128)(2,1)} %get-tuple-element.23), calls=%async_computation | async-start | bytes 2097152 | tf_op jit(solution)/shard_map/all_to_all | solution.py:209
  70.3 0.1 send.1
  70.4 14.1 %collective-permute-start.5 = (bf16[128,256]{1,0:T(8,128)(2,1)S(1)}, bf16[128,256]{1,0:T(8,128)(2,1)S(1)}, u32[]{:S(2)}, u32[]{:S(2)}) collective-permute-start(bf16[128,256]{1,0:T(8,128)(2,1)S(1)} %send.1), channel_id=1, source_target_pairs={{0,1},{1,0},{2,3},{3,2},{4,5},{5,4},{6,7},{7,6},{8,9},{9,8},{10,11... | collective-permute-start | bytes 196616 | tf_op jit(solution)/shard_map/ppermute | solution.py:211
  84.6 0.0 all-to-all-done.parts_ref
  84.6 3.0 %collective-permute-done.5.other_ref = bf16[128,256]{1,0:T(8,128)(2,1)S(1)} collective-permute-done((bf16[128,256]{1,0:T(8,128)(2,1)S(1)}, bf16[128,256]{1,0:T(8,128)(2,1)S(1)}, u32[]{:S(2)}, u32[]{:S(2)}) %collective-permute-start.5) | collective-permute-done | bytes 65568 | tf_op jit(solution)/shard_map/ppermute | solution.py:211
  87.6 0.9 %finish.1 = bf16[128,256]{1,0:T(8,128)(2,1)} custom-call(bf16[16,128,256]{2,1,0:T(8,128)(2,1)S(1)} %all-to-all-done.parts_ref, bf16[128,256]{1,0:T(8,128)(2,1)S(1)} %collective-permute-done.5.other_ref, bf16[256,256]{1,0:T(8,128)(2,1)S(1)} %copy-done, f32[1,256]{1,0:T(1,128)S(1)} %bitcast.7), custom_call_target="tpu_custom_call" | custom-call | flops 16777216 | bytes 2097152 | tf_op jit(solution)/shard_map/finish/pallas_call | solution.py:28
  (9 shorter events, 0.1 us)
Async XLA Ops:
  0.0 15.7 %collective-permute-start = (bf16[1,128,256]{2,1,0:T(8,128)(2,1)}, bf16[1,128,256]{2,1,0:T(8,128)(2,1)S(1)}, u32[]{:S(2)}, u32[]{:S(2)}) collective-permute-start(bf16[1,128,256]{2,1,0:T(8,128)(2,1)} %bitcast.8), channel_id=1, source_target_pairs={{0,256},{64,320},{128,384},{192,448},{256,0},{320,64},{384,128},{4... | collective-permute-start | bytes 196616 | tf_op jit(solution)/shard_map/ppermute | solution.py:175
  15.7 10.7 %collective-permute-start.2 = (bf16[1,128,256]{2,1,0:T(8,128)(2,1)S(1)}, bf16[1,128,256]{2,1,0:T(8,128)(2,1)S(1)}, u32[]{:S(2)}, u32[]{:S(2)}) collective-permute-start(bf16[1,128,256]{2,1,0:T(8,128)(2,1)S(1)} %collective-permute-done), channel_id=1, source_target_pairs={{0,128},{64,192},{128,0},{192,64},{256,384},{320,448},{384,256},{4... | collective-permute-start | bytes 196616 | tf_op jit(solution)/shard_map/ppermute | solution.py:175
  18.1 0.8 copy-start.2
  19.0 7.5 %collective-permute-start.1 = (bf16[1,128,256]{2,1,0:T(8,128)(2,1)S(1)}, bf16[1,128,256]{2,1,0:T(8,128)(2,1)S(1)}, u32[]{:S(2)}, u32[]{:S(2)}) collective-permute-start(bf16[1,128,256]{2,1,0:T(8,128)(2,1)S(1)} %own.1), channel_id=1, source_target_pairs={{0,128},{64,192},{128,0},{192,64},{256,384},{320,448},{384,256},{4... | collective-permute-start | bytes 196616 | tf_op jit(solution)/shard_map/ppermute | solution.py:175
  26.5 9.0 %collective-permute-start.3 = (bf16[4,128,256]{2,1,0:T(8,128)(2,1)S(1)}, bf16[4,128,256]{2,1,0:T(8,128)(2,1)S(1)}, u32[]{:S(2)}, u32[]{:S(2)}) collective-permute-start(bf16[4,128,256]{2,1,0:T(8,128)(2,1)S(1)} %pad_maximum_fusion), channel_id=1, source_target_pairs={{0,64},{64,0},{128,192},{192,128},{256,320},{320,256},{384,448},{4... | collective-permute-start | bytes 786440 | tf_op jit(solution)/shard_map/ppermute | solution.py:175
  35.5 3.8 %collective-permute-start.4 = (bf16[8,128,256]{2,1,0:T(8,128)(2,1)S(1)}, bf16[8,128,256]{2,1,0:T(8,128)(2,1)S(1)}, u32[]{:S(2)}, u32[]{:S(2)}) collective-permute-start(bf16[8,128,256]{2,1,0:T(8,128)(2,1)S(1)} %constant_dynamic-update-slice_fusion.held_ref), channel_id=1, source_target_pairs={{0,32},{32,0},{1,33},{33,1},{2,34},{34,2},{3,35},{35,3},{4,36},{36... | collective-permute-start | bytes 1572872 | tf_op jit(solution)/shard_map/ppermute | solution.py:178
  64.3 23.2 %copy-start = (bf16[256,256]{1,0:T(8,128)(2,1)S(1)}, bf16[256,256]{1,0:T(8,128)(2,1)}, u32[]{:S(2)}) copy-start(bf16[256,256]{1,0:T(8,128)(2,1)} %weight_ref.1) | copy-start | bytes 393220
  64.3 23.2 %copy-start.1 = (f32[256]{0:T(256)S(1)}, f32[256]{0:T(256)}, u32[]{:S(2)}) copy-start(f32[256]{0:T(256)} %param.11) | copy-start | bytes 3076
  64.3 20.3 %all-to-all-start = ((bf16[16,128,256]{2,1,0:T(8,128)(2,1)}), bf16[16,128,256]{2,1,0:T(8,128)(2,1)S(1)}, u32[]{:S(2)}, u32[]{:S(2)}) async-start(bf16[16,128,256]{2,1,0:T(8,128)(2,1)} %get-tuple-element.23), calls=%async_computation | async-start | bytes 2097152 | tf_op jit(solution)/shard_map/all_to_all | solution.py:209
  70.4 17.1 %collective-permute-start.5 = (bf16[128,256]{1,0:T(8,128)(2,1)S(1)}, bf16[128,256]{1,0:T(8,128)(2,1)S(1)}, u32[]{:S(2)}, u32[]{:S(2)}) collective-permute-start(bf16[128,256]{1,0:T(8,128)(2,1)S(1)} %send.1), channel_id=1, source_target_pairs={{0,1},{1,0},{2,3},{3,2},{4,5},{5,4},{6,7},{7,6},{8,9},{9,8},{10,11... | collective-permute-start | bytes 196616 | tf_op jit(solution)/shard_map/ppermute | solution.py:211

commit v12 on v9

--- a/solution.py
+++ b/solution.py
@@ -94,7 +94,7 @@
 
 def far_kernel(table_ref, lhs_ref, *refs):
     held, across, stripe_ref, out_ref, made, sem = refs
-    for i, d in enumerate((0, 4, 2, 6, 1, 5, 3, 7)):
+    for i, d in enumerate((0, 1, 4, 2, 6, 5, 3, 7)):
         stripe_ref[CORE * d] = held[i]
         stripe_ref[CORE * d + 1] = across[i]
     group = X * Y // sem.shape[0]
@@ -201,12 +201,13 @@
         return lax.ppermute(value, "core", [(0, 1), (1, 0)])
 
     p4, p2 = hop(features[None], 4), hop(own, 2)
-    p4, table = lax.optimization_barrier((p4, table))
-    p6 = hop(p4, 2)
+    p4, table, mine = lax.optimization_barrier((p4, table, own))
+    p6, p1 = hop(p4, 2), hop(mine, 1)
+    three = jnp.concatenate([p4, p2, p6], axis=0)
+    three, table = lax.optimization_barrier((three, table))
     far_lhs = far_lhs_rows(table, blocks)
-    p6, far_lhs = lax.optimization_barrier((p6, far_lhs))
-    even = jnp.concatenate([own, p4, p2, p6], axis=0)
-    held = jnp.concatenate([even, hop(even, 1)], axis=0)
+    odd, far_lhs = lax.optimization_barrier((hop(three, 1), far_lhs))
+    held = jnp.concatenate([own, p1, p4, p2, p6, odd], axis=0)
     across = cross(held)
     half = (X * Y, BS, F)
     one = jax.ShapeDtypeStruct((BS, F), bf16)

time: 85.4 us -> 83.9 us (0.982)
  waiting for transfers between devices: 22.7 us -> 15.7 us
  starting transfers between devices: 49.8 us -> 55.1 us
    ppermute x4 -> x5, waiting for transfers between devices: 7.09 us -> 0.94 us  [hop(): return lax.ppermute(value, 'zl', [(z, z ^ bit) for z in range(ZL)])]
    ppermute x4 -> x5, starting transfers between devices: 20.5 us -> 25.6 us  [hop(): return lax.ppermute(value, 'zl', [(z, z ^ bit) for z in range(ZL)])]
  transfers between devices with their start and end apart: 8 -> 9, of which waited for: 7 -> 7; matrix products, arithmetic and copies ran while one was open for 0% -> 0% of each run, Pallas kernels for 9% -> 10%
where the time goes in v12:
time: 83.9 us; the launch traced here: 83.2 us
  starting transfers between devices  55.1 us (66%)
  waiting for transfers between devices  15.7 us (19%)
  Pallas kernels  11.1 us (13%)
  local copies, waits for them, and re-layouts  0.98 us (1%)
    ppermute x5, starting transfers between devices, hop(): return lax.ppermute(value, 'zl', [(z, z ^ bit) for z in range(ZL)])  25.6 us
    ppermute x1, starting transfers between devices, local(): other = lax.ppermute(send, 'zh', [(0, 1), (1, 0)])  13.8 us
    all_to_all x1, waiting for transfers between devices, local(): far_parts = lax.all_to_all(far_terms, ('x', 'y'), 0, 0)  10.4 us
    all_to_all x1, starting transfers between devices, local(): far_parts = lax.all_to_all(far_terms, ('x', 'y'), 0, 0)  7.49 us
    all_to_all x1, starting transfers between devices, local(): near_parts = lax.all_to_all(near_terms, ('x', 'y'), 0, 0)  6.35 us
    pallas_call x1, Pallas kernels, near_half(): pl.pallas_call(near_kernel, grid_spec=pltpu.PrefetchScalarGridSpec(num_sc...  4.84 us
    pallas_call x4, Pallas kernels, whole(): pl.pallas_call(kernel, in_specs=specs or [VMEM] * len(ins), out_specs=out...  3.19 us
    pallas_call x1, Pallas kernels, far_lhs_rows(): pl.pallas_call(far_lhs_kernel, grid_spec=pltpu.PrefetchScalarGridSpec(num...  3.11 us
  transfers between devices with their start and end apart: 9, of which 7 were waited for; matrix products, arithmetic and copies ran while one was open for 0% of the time, Pallas kernels for 10%

profile of v12, /device:TPU:2, one launch (start us, length us, event | category | flops | bytes accessed | tf_op | source)
XLA Modules:
  0.0 83.2 jit_solution(12668138370364624754)
XLA Ops:
  0.0 9.1 %collective-permute-start = (bf16[1,128,256]{2,1,0:T(8,128)(2,1)}, bf16[1,128,256]{2,1,0:T(8,128)(2,1)S(1)}, u32[]{:S(2)}, u32[]{:S(2)}) collective-permute-start(bf16[1,128,256]{2,1,0:T(8,128)(2,1)} %bitcast.8), channel_id=1, source_target_pairs={{0,256},{64,320},{128,384},{192,448},{256,0},{320,64},{384,128},{4... | collective-permute-start | bytes 196616 | tf_op jit(solution)/shard_map/ppermute | solution.py:198
  9.1 0.8 %copy-done.2 = bf16[128,256]{1,0:T(8,128)(2,1)S(1)} copy-done((bf16[128,256]{1,0:T(8,128)(2,1)S(1)}, bf16[128,256]{1,0:T(8,128)(2,1)}, u32[]{:S(2)}) %copy-start.2) | copy-done | bytes 65560
  10.0 5.3 %collective-permute-start.1 = (bf16[1,128,256]{2,1,0:T(8,128)(2,1)S(1)}, bf16[1,128,256]{2,1,0:T(8,128)(2,1)S(1)}, u32[]{:S(2)}, u32[]{:S(2)}) collective-permute-start(bf16[1,128,256]{2,1,0:T(8,128)(2,1)S(1)} %own.1), channel_id=1, source_target_pairs={{0,128},{64,192},{128,0},{192,64},{256,384},{320,448},{384,256},{4... | collective-permute-start | bytes 196616 | tf_op jit(solution)/shard_map/ppermute | solution.py:198
  15.3 0.1 pad.5.clone
  15.4 0.1 add_add_fusion.table_ref
  15.4 0.3 collective-permute-done
  15.7 2.4 %collective-permute-start.2 = (bf16[1,128,256]{2,1,0:T(8,128)(2,1)S(1)}, bf16[1,128,256]{2,1,0:T(8,128)(2,1)S(1)}, u32[]{:S(2)}, u32[]{:S(2)}) collective-permute-start(bf16[1,128,256]{2,1,0:T(8,128)(2,1)S(1)} %collective-permute-done), channel_id=1, source_target_pairs={{0,128},{64,192},{128,0},{192,64},{256,384},{320,448},{384,256},{4... | collective-permute-start | bytes 196616 | tf_op jit(solution)/shard_map/ppermute | solution.py:198
  18.1 4.5 %collective-permute-start.4 = (bf16[1,128,256]{2,1,0:T(8,128)(2,1)S(1)}, bf16[1,128,256]{2,1,0:T(8,128)(2,1)S(1)}, u32[]{:S(2)}, u32[]{:S(2)}) collective-permute-start(bf16[1,128,256]{2,1,0:T(8,128)(2,1)S(1)} %own.1), channel_id=1, source_target_pairs={{0,64},{64,0},{128,192},{192,128},{256,320},{320,256},{384,448},{4... | collective-permute-start | bytes 196616 | tf_op jit(solution)/shard_map/ppermute | solution.py:198
  22.6 0.2 collective-permute-done.2
  22.9 4.3 %collective-permute-start.3 = (bf16[3,128,256]{2,1,0:T(8,128)(2,1)S(1)}, bf16[3,128,256]{2,1,0:T(8,128)(2,1)S(1)}, u32[]{:S(2)}, u32[]{:S(2)}) collective-permute-start(bf16[3,128,256]{2,1,0:T(8,128)(2,1)S(1)} %pad_maximum_fusion), channel_id=1, source_target_pairs={{0,64},{64,0},{128,192},{192,128},{256,320},{320,256},{384,448},{4... | collective-permute-start | bytes 589832 | tf_op jit(solution)/shard_map/ppermute | solution.py:198
  27.3 3.1 %far_lhs.1.lhs_ref = bf16[16,128,512]{2,1,0:T(8,128)(2,1)S(1)} custom-call(s32[6,32]{1,0:T(8,128)S(1)} %add_add_fusion.table_ref, bf16[16,2,4,128,128]{4,3,2,1,0:T(8,128)(2,1)} %bitcast.10), custom_call_target="tpu_custom_call" | custom-call | bytes 4194304 | tf_op jit(solution)/shard_map/far_lhs/pallas_call | solution.py:73
  30.4 0.4 collective-permute-done.3
  30.9 1.9 %collective-permute-start.5 = (bf16[8,128,256]{2,1,0:T(8,128)(2,1)S(1)}, bf16[8,128,256]{2,1,0:T(8,128)(2,1)S(1)}, u32[]{:S(2)}, u32[]{:S(2)}) collective-permute-start(bf16[8,128,256]{2,1,0:T(8,128)(2,1)S(1)} %constant_dynamic-update-slice_fusion.refs_0_), channel_id=1, source_target_pairs={{0,32},{32,0},{1,33},{33,1},{2,34},{34,2},{3,35},{35,3},{4,36},{36... | collective-permute-start | bytes 1572872 | tf_op jit(solution)/shard_map/ppermute | solution.py:201
  32.8 1.9 %collective-permute-done.5.refs_1_ = bf16[8,128,256]{2,1,0:T(8,128)(2,1)S(1)} collective-permute-done((bf16[8,128,256]{2,1,0:T(8,128)(2,1)S(1)}, bf16[8,128,256]{2,1,0:T(8,128)(2,1)S(1)}, u32[]{:S(2)}, u32[]{:S(2)}) %collective-permute-start.5) | collective-permute-done | bytes 524320 | tf_op jit(solution)/shard_map/ppermute | solution.py:201
  34.7 2.1 %far_terms.1 = (bf16[16,128,256]{2,1,0:T(8,128)(2,1)S(1)}, bf16[16,128,256]{2,1,0:T(8,128)(2,1)}) custom-call(s32[6,32]{1,0:T(8,128)S(1)} %add_add_fusion.table_ref, bf16[16,128,512]{2,1,0:T(8,128)(2,1)S(1)} %far_lhs.1.lhs_ref, bf16[8,128,256]{2,1,0:T(8,128)(2,1)S(1)} %constant_dynamic-update-slice_fusion.refs_0_, ...), custom_call_target="tpu_custom_call" | custom-call | flops 536870912 | bytes 4194304 | tf_op jit(solution)/shard_map/far_terms/pallas_call | solution.py:28
  36.8 7.5 %all-to-all-start.1 = ((bf16[16,128,256]{2,1,0:T(8,128)(2,1)}), bf16[16,128,256]{2,1,0:T(8,128)(2,1)S(1)}, u32[]{:S(2)}, u32[]{:S(2)}) async-start(bf16[16,128,256]{2,1,0:T(8,128)(2,1)} %get-tuple-element.22), calls=%async_computation.1 | async-start | bytes 2097152 | tf_op jit(solution)/shard_map/all_to_all | solution.py:226
  44.3 4.8 %near_terms.1 = bf16[16,128,256]{2,1,0:T(8,128)(2,1)} custom-call(s32[6,32]{1,0:T(8,128)S(1)} %add_add_fusion.table_ref, bf16[16,2,4,128,128]{4,3,2,1,0:T(8,128)(2,1)} %bitcast.11, bf16[16,128,256]{2,1,0:T(8,128)(2,1)S(1)} %get-tuple-element.21.stripe_ref), custom_call_target="tpu_custom_call" | custom-call | flops 536870912 | bytes 4194304 | tf_op jit(solution)/shard_map/near_terms/pallas_call | solution.py:127
  49.2 10.4 %all-to-all-done.1.parts_ref = bf16[16,128,256]{2,1,0:T(8,128)(2,1)S(1)} async-done(((bf16[16,128,256]{2,1,0:T(8,128)(2,1)}), bf16[16,128,256]{2,1,0:T(8,128)(2,1)S(1)}, u32[]{:S(2)}, u32[]{:S(2)}) %all-to-all-start.1) | async-done | bytes 1048608 | tf_op jit(solution)/shard_map/all_to_all | solution.py:226
  59.6 6.4 %all-to-all-start = ((bf16[16,128,256]{2,1,0:T(8,128)(2,1)}), bf16[16,128,256]{2,1,0:T(8,128)(2,1)S(1)}, u32[]{:S(2)}, u32[]{:S(2)}) async-start(bf16[16,128,256]{2,1,0:T(8,128)(2,1)} %near_terms.1), calls=%async_computation | async-start | bytes 2097152 | tf_op jit(solution)/shard_map/all_to_all | solution.py:227
  66.0 0.1 send.1
  66.1 13.8 %collective-permute-start.6 = (bf16[128,256]{1,0:T(8,128)(2,1)S(1)}, bf16[128,256]{1,0:T(8,128)(2,1)S(1)}, u32[]{:S(2)}, u32[]{:S(2)}) collective-permute-start(bf16[128,256]{1,0:T(8,128)(2,1)S(1)} %send.1), channel_id=1, source_target_pairs={{0,1},{1,0},{2,3},{3,2},{4,5},{5,4},{6,7},{7,6},{8,9},{9,8},{10,11... | collective-permute-start | bytes 196616 | tf_op jit(solution)/shard_map/ppermute | solution.py:229
  79.9 0.1 all-to-all-done.parts_ref
  80.0 2.4 %collective-permute-done.6.other_ref = bf16[128,256]{1,0:T(8,128)(2,1)S(1)} collective-permute-done((bf16[128,256]{1,0:T(8,128)(2,1)S(1)}, bf16[128,256]{1,0:T(8,128)(2,1)S(1)}, u32[]{:S(2)}, u32[]{:S(2)}) %collective-permute-start.6) | collective-permute-done | bytes 65568 | tf_op jit(solution)/shard_map/ppermute | solution.py:229
  82.3 0.9 %finish.1 = bf16[128,256]{1,0:T(8,128)(2,1)} custom-call(bf16[16,128,256]{2,1,0:T(8,128)(2,1)S(1)} %all-to-all-done.parts_ref, bf16[128,256]{1,0:T(8,128)(2,1)S(1)} %collective-permute-done.6.other_ref, bf16[256,256]{1,0:T(8,128)(2,1)S(1)} %copy-done, f32[1,256]{1,0:T(1,128)S(1)} %bitcast.7), custom_call_target="tpu_custom_call" | custom-call | flops 16777216 | bytes 2097152 | tf_op jit(solution)/shard_map/finish/pallas_call | solution.py:28
  (20 shorter events, 0.1 us)
Async XLA Ops:
  0.0 15.7 %collective-permute-start = (bf16[1,128,256]{2,1,0:T(8,128)(2,1)}, bf16[1,128,256]{2,1,0:T(8,128)(2,1)S(1)}, u32[]{:S(2)}, u32[]{:S(2)}) collective-permute-start(bf16[1,128,256]{2,1,0:T(8,128)(2,1)} %bitcast.8), channel_id=1, source_target_pairs={{0,256},{64,320},{128,384},{192,448},{256,0},{320,64},{384,128},{4... | collective-permute-start | bytes 196616 | tf_op jit(solution)/shard_map/ppermute | solution.py:198
  9.1 0.9 %copy-start.2 = (bf16[128,256]{1,0:T(8,128)(2,1)S(1)}, bf16[128,256]{1,0:T(8,128)(2,1)}, u32[]{:S(2)}) copy-start(bf16[128,256]{1,0:T(8,128)(2,1)} %param.6) | copy-start | bytes 196612
  9.9 5.4 %copy-start.3 = (s32[32,4]{0,1:T(4,128)S(1)}, s32[32,4]{0,1:T(4,128)}, u32[]{:S(2)}) copy-start(s32[32,4]{0,1:T(4,128)} %param.8) | copy-start | bytes 1540
  9.9 5.4 %copy-start.4 = (s32[32,1]{0,1:T(1,128)S(1)}, s32[32,1]{0,1:T(1,128)}, u32[]{:S(2)}) copy-start(s32[32,1]{0,1:T(1,128)} %param.9) | copy-start | bytes 388
  10.0 12.7 %collective-permute-start.1 = (bf16[1,128,256]{2,1,0:T(8,128)(2,1)S(1)}, bf16[1,128,256]{2,1,0:T(8,128)(2,1)S(1)}, u32[]{:S(2)}, u32[]{:S(2)}) collective-permute-start(bf16[1,128,256]{2,1,0:T(8,128)(2,1)S(1)} %own.1), channel_id=1, source_target_pairs={{0,128},{64,192},{128,0},{192,64},{256,384},{320,448},{384,256},{4... | collective-permute-start | bytes 196616 | tf_op jit(solution)/shard_map/ppermute | solution.py:198
  15.7 7.2 %collective-permute-start.2 = (bf16[1,128,256]{2,1,0:T(8,128)(2,1)S(1)}, bf16[1,128,256]{2,1,0:T(8,128)(2,1)S(1)}, u32[]{:S(2)}, u32[]{:S(2)}) collective-permute-start(bf16[1,128,256]{2,1,0:T(8,128)(2,1)S(1)} %collective-permute-done), channel_id=1, source_target_pairs={{0,128},{64,192},{128,0},{192,64},{256,384},{320,448},{384,256},{4... | collective-permute-start | bytes 196616 | tf_op jit(solution)/shard_map/ppermute | solution.py:198
  18.1 9.1 %collective-permute-start.4 = (bf16[1,128,256]{2,1,0:T(8,128)(2,1)S(1)}, bf16[1,128,256]{2,1,0:T(8,128)(2,1)S(1)}, u32[]{:S(2)}, u32[]{:S(2)}) collective-permute-start(bf16[1,128,256]{2,1,0:T(8,128)(2,1)S(1)} %own.1), channel_id=1, source_target_pairs={{0,64},{64,0},{128,192},{192,128},{256,320},{320,256},{384,448},{4... | collective-permute-start | bytes 196616 | tf_op jit(solution)/shard_map/ppermute | solution.py:198
  22.9 8.0 %collective-permute-start.3 = (bf16[3,128,256]{2,1,0:T(8,128)(2,1)S(1)}, bf16[3,128,256]{2,1,0:T(8,128)(2,1)S(1)}, u32[]{:S(2)}, u32[]{:S(2)}) collective-permute-start(bf16[3,128,256]{2,1,0:T(8,128)(2,1)S(1)} %pad_maximum_fusion), channel_id=1, source_target_pairs={{0,64},{64,0},{128,192},{192,128},{256,320},{320,256},{384,448},{4... | collective-permute-start | bytes 589832 | tf_op jit(solution)/shard_map/ppermute | solution.py:198
  30.9 3.8 %collective-permute-start.5 = (bf16[8,128,256]{2,1,0:T(8,128)(2,1)S(1)}, bf16[8,128,256]{2,1,0:T(8,128)(2,1)S(1)}, u32[]{:S(2)}, u32[]{:S(2)}) collective-permute-start(bf16[8,128,256]{2,1,0:T(8,128)(2,1)S(1)} %constant_dynamic-update-slice_fusion.refs_0_), channel_id=1, source_target_pairs={{0,32},{32,0},{1,33},{33,1},{2,34},{34,2},{3,35},{35,3},{4,36},{36... | collective-permute-start | bytes 1572872 | tf_op jit(solution)/shard_map/ppermute | solution.py:201
  36.8 22.8 %all-to-all-start.1 = ((bf16[16,128,256]{2,1,0:T(8,128)(2,1)}), bf16[16,128,256]{2,1,0:T(8,128)(2,1)S(1)}, u32[]{:S(2)}, u32[]{:S(2)}) async-start(bf16[16,128,256]{2,1,0:T(8,128)(2,1)} %get-tuple-element.22), calls=%async_computation.1 | async-start | bytes 2097152 | tf_op jit(solution)/shard_map/all_to_all | solution.py:226
  44.3 38.0 %copy-start = (bf16[256,256]{1,0:T(8,128)(2,1)S(1)}, bf16[256,256]{1,0:T(8,128)(2,1)}, u32[]{:S(2)}) copy-start(bf16[256,256]{1,0:T(8,128)(2,1)} %weight_ref.1) | copy-start | bytes 393220
  44.3 38.0 %copy-start.1 = (f32[256]{0:T(256)S(1)}, f32[256]{0:T(256)}, u32[]{:S(2)}) copy-start(f32[256]{0:T(256)} %param.11) | copy-start | bytes 3076
  59.6 20.3 %all-to-all-start = ((bf16[16,128,256]{2,1,0:T(8,128)(2,1)}), bf16[16,128,256]{2,1,0:T(8,128)(2,1)S(1)}, u32[]{:S(2)}, u32[]{:S(2)}) async-start(bf16[16,128,256]{2,1,0:T(8,128)(2,1)} %near_terms.1), calls=%async_computation | async-start | bytes 2097152 | tf_op jit(solution)/shard_map/all_to_all | solution.py:227
  66.1 16.2 %collective-permute-start.6 = (bf16[128,256]{1,0:T(8,128)(2,1)S(1)}, bf16[128,256]{1,0:T(8,128)(2,1)S(1)}, u32[]{:S(2)}, u32[]{:S(2)}) collective-permute-start(bf16[128,256]{1,0:T(8,128)(2,1)S(1)} %send.1), channel_id=1, source_target_pairs={{0,1},{1,0},{2,3},{3,2},{4,5},{5,4},{6,7},{7,6},{8,9},{9,8},{10,11... | collective-permute-start | bytes 196616 | tf_op jit(solution)/shard_map/ppermute | solution.py:229

commit v13 on v12

--- a/solution.py
+++ b/solution.py
@@ -94,7 +94,7 @@
 
 def far_kernel(table_ref, lhs_ref, *refs):
     held, across, stripe_ref, out_ref, made, sem = refs
-    for i, d in enumerate((0, 1, 4, 2, 6, 5, 3, 7)):
+    for i, d in enumerate((0, 1, 4, 2, 6, 3, 5, 7)):
         stripe_ref[CORE * d] = held[i]
         stripe_ref[CORE * d + 1] = across[i]
     group = X * Y // sem.shape[0]
@@ -202,12 +202,12 @@
 
     p4, p2 = hop(features[None], 4), hop(own, 2)
     p4, table, mine = lax.optimization_barrier((p4, table, own))
-    p6, p1 = hop(p4, 2), hop(mine, 1)
-    three = jnp.concatenate([p4, p2, p6], axis=0)
-    three, table = lax.optimization_barrier((three, table))
+    p6, p1, p3 = hop(p4, 2), hop(mine, 1), hop(p2, 1)
+    two = jnp.concatenate([p4, p6], axis=0)
+    two, table = lax.optimization_barrier((two, table))
     far_lhs = far_lhs_rows(table, blocks)
-    odd, far_lhs = lax.optimization_barrier((hop(three, 1), far_lhs))
-    held = jnp.concatenate([own, p1, p4, p2, p6, odd], axis=0)
+    odd, far_lhs = lax.optimization_barrier((hop(two, 1), far_lhs))
+    held = jnp.concatenate([own, p1, p4, p2, p6, p3, odd], axis=0)
     across = cross(held)
     half = (X * Y, BS, F)
     one = jax.ShapeDtypeStruct((BS, F), bf16)

time: 83.9 us -> 84.8 us (1.011)
    ppermute x5 -> x6, starting transfers between devices: 25.6 us -> 27.1 us  [hop(): return lax.ppermute(value, 'zl', [(z, z ^ bit) for z in range(ZL)])]
    all_to_all x1, waiting for transfers between devices: 0.08 us -> 1.04 us  [local(): near_parts = lax.all_to_all(near_terms, ('x', 'y'), 0, 0)]
    ppermute x1, starting transfers between devices: 13.8 us -> 12.8 us  [local(): other = lax.ppermute(send, 'zh', [(0, 1), (1, 0)])]
  transfers between devices with their start and end apart: 9 -> 10, of which waited for: 7 -> 5; matrix products, arithmetic and copies ran while one was open for 0% -> 0% of each run, Pallas kernels for 10% -> 9%
where the time goes in v13:
time: 84.8 us; the launch traced here: 84.1 us
  starting transfers between devices  55.7 us (66%)
  waiting for transfers between devices  16 us (19%)
  Pallas kernels  11.1 us (13%)
  local copies, waits for them, and re-layouts  0.99 us (1%)
    ppermute x6, starting transfers between devices, hop(): return lax.ppermute(value, 'zl', [(z, z ^ bit) for z in range(ZL)])  27.1 us
    ppermute x1, starting transfers between devices, local(): other = lax.ppermute(send, 'zh', [(0, 1), (1, 0)])  12.8 us
    all_to_all x1, waiting for transfers between devices, local(): far_parts = lax.all_to_all(far_terms, ('x', 'y'), 0, 0)  10.5 us
    all_to_all x1, starting transfers between devices, local(): far_parts = lax.all_to_all(far_terms, ('x', 'y'), 0, 0)  7.49 us
    all_to_all x1, starting transfers between devices, local(): near_parts = lax.all_to_all(near_terms, ('x', 'y'), 0, 0)  6.35 us
    pallas_call x1, Pallas kernels, near_half(): pl.pallas_call(near_kernel, grid_spec=pltpu.PrefetchScalarGridSpec(num_sc...  4.83 us
    pallas_call x4, Pallas kernels, whole(): pl.pallas_call(kernel, in_specs=specs or [VMEM] * len(ins), out_specs=out...  3.2 us
    pallas_call x1, Pallas kernels, far_lhs_rows(): pl.pallas_call(far_lhs_kernel, grid_spec=pltpu.PrefetchScalarGridSpec(num...  3.11 us
  transfers between devices with their start and end apart: 10, of which 5 were waited for; matrix products, arithmetic and copies ran while one was open for 0% of the time, Pallas kernels for 9%

profile of v13, /device:TPU:2, one launch (start us, length us, event | category | flops | bytes accessed | tf_op | source)
XLA Modules:
  0.0 84.1 jit_solution(12698923802492520824)
XLA Ops:
  0.0 9.1 %collective-permute-start = (bf16[1,128,256]{2,1,0:T(8,128)(2,1)}, bf16[1,128,256]{2,1,0:T(8,128)(2,1)S(1)}, u32[]{:S(2)}, u32[]{:S(2)}) collective-permute-start(bf16[1,128,256]{2,1,0:T(8,128)(2,1)} %bitcast.8), channel_id=1, source_target_pairs={{0,256},{64,320},{128,384},{192,448},{256,0},{320,64},{384,128},{4... | collective-permute-start | bytes 196616 | tf_op jit(solution)/shard_map/ppermute | solution.py:198
  9.1 0.8 copy-done.2
  10.0 5.3 %collective-permute-start.4 = (bf16[1,128,256]{2,1,0:T(8,128)(2,1)S(1)}, bf16[1,128,256]{2,1,0:T(8,128)(2,1)S(1)}, u32[]{:S(2)}, u32[]{:S(2)}) collective-permute-start(bf16[1,128,256]{2,1,0:T(8,128)(2,1)S(1)} %own.1), channel_id=1, source_target_pairs={{0,128},{64,192},{128,0},{192,64},{256,384},{320,448},{384,256},{4... | collective-permute-start | bytes 196616 | tf_op jit(solution)/shard_map/ppermute | solution.py:198
  15.3 0.1 pad.4.clone
  15.4 0.1 add_add_fusion.table_ref
  15.4 0.3 collective-permute-done
  15.7 2.4 %collective-permute-start.1 = (bf16[1,128,256]{2,1,0:T(8,128)(2,1)S(1)}, bf16[1,128,256]{2,1,0:T(8,128)(2,1)S(1)}, u32[]{:S(2)}, u32[]{:S(2)}) collective-permute-start(bf16[1,128,256]{2,1,0:T(8,128)(2,1)S(1)} %collective-permute-done), channel_id=1, source_target_pairs={{0,128},{64,192},{128,0},{192,64},{256,384},{320,448},{384,256},{4... | collective-permute-start | bytes 196616 | tf_op jit(solution)/shard_map/ppermute | solution.py:198
  18.1 4.5 %collective-permute-start.3 = (bf16[1,128,256]{2,1,0:T(8,128)(2,1)S(1)}, bf16[1,128,256]{2,1,0:T(8,128)(2,1)S(1)}, u32[]{:S(2)}, u32[]{:S(2)}) collective-permute-start(bf16[1,128,256]{2,1,0:T(8,128)(2,1)S(1)} %own.1), channel_id=1, source_target_pairs={{0,64},{64,0},{128,192},{192,128},{256,320},{320,256},{384,448},{4... | collective-permute-start | bytes 196616 | tf_op jit(solution)/shard_map/ppermute | solution.py:198
  22.6 1.9 %collective-permute-start.5 = (bf16[1,128,256]{2,1,0:T(8,128)(2,1)S(1)}, bf16[1,128,256]{2,1,0:T(8,128)(2,1)S(1)}, u32[]{:S(2)}, u32[]{:S(2)}) collective-permute-start(bf16[1,128,256]{2,1,0:T(8,128)(2,1)S(1)} %collective-permute-done.4), channel_id=1, source_target_pairs={{0,64},{64,0},{128,192},{192,128},{256,320},{320,256},{384,448},{4... | collective-permute-start | bytes 196616 | tf_op jit(solution)/shard_map/ppermute | solution.py:198
  24.6 3.9 %collective-permute-start.2 = (bf16[2,128,256]{2,1,0:T(8,128)(2,1)S(1)}, bf16[2,128,256]{2,1,0:T(8,128)(2,1)S(1)}, u32[]{:S(2)}, u32[]{:S(2)}) collective-permute-start(bf16[2,128,256]{2,1,0:T(8,128)(2,1)S(1)} %pad_maximum_fusion), channel_id=1, source_target_pairs={{0,64},{64,0},{128,192},{192,128},{256,320},{320,256},{384,448},{4... | collective-permute-start | bytes 393224 | tf_op jit(solution)/shard_map/ppermute | solution.py:198
  28.6 3.1 %far_lhs.1.lhs_ref = bf16[16,128,512]{2,1,0:T(8,128)(2,1)S(1)} custom-call(s32[6,32]{1,0:T(8,128)S(1)} %add_add_fusion.table_ref, bf16[16,2,4,128,128]{4,3,2,1,0:T(8,128)(2,1)} %bitcast.10), custom_call_target="tpu_custom_call" | custom-call | bytes 4194304 | tf_op jit(solution)/shard_map/far_lhs/pallas_call | solution.py:73
  31.8 1.9 %collective-permute-start.6 = (bf16[8,128,256]{2,1,0:T(8,128)(2,1)S(1)}, bf16[8,128,256]{2,1,0:T(8,128)(2,1)S(1)}, u32[]{:S(2)}, u32[]{:S(2)}) collective-permute-start(bf16[8,128,256]{2,1,0:T(8,128)(2,1)S(1)} %constant_dynamic-update-slice_fusion.refs_0_), channel_id=1, source_target_pairs={{0,32},{32,0},{1,33},{33,1},{2,34},{34,2},{3,35},{35,3},{4,36},{36... | collective-permute-start | bytes 1572872 | tf_op jit(solution)/shard_map/ppermute | solution.py:201
  33.7 1.9 %collective-permute-done.6.refs_1_ = bf16[8,128,256]{2,1,0:T(8,128)(2,1)S(1)} collective-permute-done((bf16[8,128,256]{2,1,0:T(8,128)(2,1)S(1)}, bf16[8,128,256]{2,1,0:T(8,128)(2,1)S(1)}, u32[]{:S(2)}, u32[]{:S(2)}) %collective-permute-start.6) | collective-permute-done | bytes 524320 | tf_op jit(solution)/shard_map/ppermute | solution.py:201
  35.6 2.1 %far_terms.1 = (bf16[16,128,256]{2,1,0:T(8,128)(2,1)S(1)}, bf16[16,128,256]{2,1,0:T(8,128)(2,1)}) custom-call(s32[6,32]{1,0:T(8,128)S(1)} %add_add_fusion.table_ref, bf16[16,128,512]{2,1,0:T(8,128)(2,1)S(1)} %far_lhs.1.lhs_ref, bf16[8,128,256]{2,1,0:T(8,128)(2,1)S(1)} %constant_dynamic-update-slice_fusion.refs_0_, ...), custom_call_target="tpu_custom_call" | custom-call | flops 536870912 | bytes 4194304 | tf_op jit(solution)/shard_map/far_terms/pallas_call | solution.py:28
  37.7 7.5 %all-to-all-start.1 = ((bf16[16,128,256]{2,1,0:T(8,128)(2,1)}), bf16[16,128,256]{2,1,0:T(8,128)(2,1)S(1)}, u32[]{:S(2)}, u32[]{:S(2)}) async-start(bf16[16,128,256]{2,1,0:T(8,128)(2,1)} %get-tuple-element.22), calls=%async_computation.1 | async-start | bytes 2097152 | tf_op jit(solution)/shard_map/all_to_all | solution.py:226
  45.2 0.0 copy-start.1
  45.2 4.8 %near_terms.1 = bf16[16,128,256]{2,1,0:T(8,128)(2,1)} custom-call(s32[6,32]{1,0:T(8,128)S(1)} %add_add_fusion.table_ref, bf16[16,2,4,128,128]{4,3,2,1,0:T(8,128)(2,1)} %bitcast.11, bf16[16,128,256]{2,1,0:T(8,128)(2,1)S(1)} %get-tuple-element.21.stripe_ref), custom_call_target="tpu_custom_call" | custom-call | flops 536870912 | bytes 4194304 | tf_op jit(solution)/shard_map/near_terms/pallas_call | solution.py:127
  50.1 10.5 %all-to-all-done.1.parts_ref = bf16[16,128,256]{2,1,0:T(8,128)(2,1)S(1)} async-done(((bf16[16,128,256]{2,1,0:T(8,128)(2,1)}), bf16[16,128,256]{2,1,0:T(8,128)(2,1)S(1)}, u32[]{:S(2)}, u32[]{:S(2)}) %all-to-all-start.1) | async-done | bytes 1048608 | tf_op jit(solution)/shard_map/all_to_all | solution.py:226
  60.5 6.3 %all-to-all-start = ((bf16[16,128,256]{2,1,0:T(8,128)(2,1)}), bf16[16,128,256]{2,1,0:T(8,128)(2,1)S(1)}, u32[]{:S(2)}, u32[]{:S(2)}) async-start(bf16[16,128,256]{2,1,0:T(8,128)(2,1)} %near_terms.1), calls=%async_computation | async-start | bytes 2097152 | tf_op jit(solution)/shard_map/all_to_all | solution.py:227
  66.9 0.1 send.1
  67.0 12.8 %collective-permute-start.7 = (bf16[128,256]{1,0:T(8,128)(2,1)S(1)}, bf16[128,256]{1,0:T(8,128)(2,1)S(1)}, u32[]{:S(2)}, u32[]{:S(2)}) collective-permute-start(bf16[128,256]{1,0:T(8,128)(2,1)S(1)} %send.1), channel_id=1, source_target_pairs={{0,1},{1,0},{2,3},{3,2},{4,5},{5,4},{6,7},{7,6},{8,9},{9,8},{10,11... | collective-permute-start | bytes 196616 | tf_op jit(solution)/shard_map/ppermute | solution.py:229
  79.8 1.0 %all-to-all-done.parts_ref = bf16[16,128,256]{2,1,0:T(8,128)(2,1)S(1)} async-done(((bf16[16,128,256]{2,1,0:T(8,128)(2,1)}), bf16[16,128,256]{2,1,0:T(8,128)(2,1)S(1)}, u32[]{:S(2)}, u32[]{:S(2)}) %all-to-all-start) | async-done | bytes 1048608 | tf_op jit(solution)/shard_map/all_to_all | solution.py:227
  80.9 2.3 %collective-permute-done.7.other_ref = bf16[128,256]{1,0:T(8,128)(2,1)S(1)} collective-permute-done((bf16[128,256]{1,0:T(8,128)(2,1)S(1)}, bf16[128,256]{1,0:T(8,128)(2,1)S(1)}, u32[]{:S(2)}, u32[]{:S(2)}) %collective-permute-start.7) | collective-permute-done | bytes 65568 | tf_op jit(solution)/shard_map/ppermute | solution.py:229
  83.2 0.9 %finish.1 = bf16[128,256]{1,0:T(8,128)(2,1)} custom-call(bf16[16,128,256]{2,1,0:T(8,128)(2,1)S(1)} %all-to-all-done.parts_ref, bf16[128,256]{1,0:T(8,128)(2,1)S(1)} %collective-permute-done.7.other_ref, bf16[256,256]{1,0:T(8,128)(2,1)S(1)} %copy-done, f32[1,256]{1,0:T(1,128)S(1)} %bitcast.7), custom_call_target="tpu_custom_call" | custom-call | flops 16777216 | bytes 2097152 | tf_op jit(solution)/shard_map/finish/pallas_call | solution.py:28
  (23 shorter events, 0.1 us)
Async XLA Ops:
  0.0 15.7 %collective-permute-start = (bf16[1,128,256]{2,1,0:T(8,128)(2,1)}, bf16[1,128,256]{2,1,0:T(8,128)(2,1)S(1)}, u32[]{:S(2)}, u32[]{:S(2)}) collective-permute-start(bf16[1,128,256]{2,1,0:T(8,128)(2,1)} %bitcast.8), channel_id=1, source_target_pairs={{0,256},{64,320},{128,384},{192,448},{256,0},{320,64},{384,128},{4... | collective-permute-start | bytes 196616 | tf_op jit(solution)/shard_map/ppermute | solution.py:198
  9.1 0.9 %copy-start.2 = (bf16[128,256]{1,0:T(8,128)(2,1)S(1)}, bf16[128,256]{1,0:T(8,128)(2,1)}, u32[]{:S(2)}) copy-start(bf16[128,256]{1,0:T(8,128)(2,1)} %param.6) | copy-start | bytes 196612
  9.9 5.4 %copy-start.3 = (s32[32,4]{0,1:T(4,128)S(1)}, s32[32,4]{0,1:T(4,128)}, u32[]{:S(2)}) copy-start(s32[32,4]{0,1:T(4,128)} %param.8) | copy-start | bytes 1540
  9.9 5.4 %copy-start.4 = (s32[32,1]{0,1:T(1,128)S(1)}, s32[32,1]{0,1:T(1,128)}, u32[]{:S(2)}) copy-start(s32[32,1]{0,1:T(1,128)} %param.9) | copy-start | bytes 388
  10.0 12.7 %collective-permute-start.4 = (bf16[1,128,256]{2,1,0:T(8,128)(2,1)S(1)}, bf16[1,128,256]{2,1,0:T(8,128)(2,1)S(1)}, u32[]{:S(2)}, u32[]{:S(2)}) collective-permute-start(bf16[1,128,256]{2,1,0:T(8,128)(2,1)S(1)} %own.1), channel_id=1, source_target_pairs={{0,128},{64,192},{128,0},{192,64},{256,384},{320,448},{384,256},{4... | collective-permute-start | bytes 196616 | tf_op jit(solution)/shard_map/ppermute | solution.py:198
  15.7 8.9 %collective-permute-start.1 = (bf16[1,128,256]{2,1,0:T(8,128)(2,1)S(1)}, bf16[1,128,256]{2,1,0:T(8,128)(2,1)S(1)}, u32[]{:S(2)}, u32[]{:S(2)}) collective-permute-start(bf16[1,128,256]{2,1,0:T(8,128)(2,1)S(1)} %collective-permute-done), channel_id=1, source_target_pairs={{0,128},{64,192},{128,0},{192,64},{256,384},{320,448},{384,256},{4... | collective-permute-start | bytes 196616 | tf_op jit(solution)/shard_map/ppermute | solution.py:198
  18.1 10.4 %collective-permute-start.3 = (bf16[1,128,256]{2,1,0:T(8,128)(2,1)S(1)}, bf16[1,128,256]{2,1,0:T(8,128)(2,1)S(1)}, u32[]{:S(2)}, u32[]{:S(2)}) collective-permute-start(bf16[1,128,256]{2,1,0:T(8,128)(2,1)S(1)} %own.1), channel_id=1, source_target_pairs={{0,64},{64,0},{128,192},{192,128},{256,320},{320,256},{384,448},{4... | collective-permute-start | bytes 196616 | tf_op jit(solution)/shard_map/ppermute | solution.py:198
  22.6 9.1 %collective-permute-start.5 = (bf16[1,128,256]{2,1,0:T(8,128)(2,1)S(1)}, bf16[1,128,256]{2,1,0:T(8,128)(2,1)S(1)}, u32[]{:S(2)}, u32[]{:S(2)}) collective-permute-start(bf16[1,128,256]{2,1,0:T(8,128)(2,1)S(1)} %collective-permute-done.4), channel_id=1, source_target_pairs={{0,64},{64,0},{128,192},{192,128},{256,320},{320,256},{384,448},{4... | collective-permute-start | bytes 196616 | tf_op jit(solution)/shard_map/ppermute | solution.py:198
  24.6 7.1 %collective-permute-start.2 = (bf16[2,128,256]{2,1,0:T(8,128)(2,1)S(1)}, bf16[2,128,256]{2,1,0:T(8,128)(2,1)S(1)}, u32[]{:S(2)}, u32[]{:S(2)}) collective-permute-start(bf16[2,128,256]{2,1,0:T(8,128)(2,1)S(1)} %pad_maximum_fusion), channel_id=1, source_target_pairs={{0,64},{64,0},{128,192},{192,128},{256,320},{320,256},{384,448},{4... | collective-permute-start | bytes 393224 | tf_op jit(solution)/shard_map/ppermute | solution.py:198
  31.8 3.8 %collective-permute-start.6 = (bf16[8,128,256]{2,1,0:T(8,128)(2,1)S(1)}, bf16[8,128,256]{2,1,0:T(8,128)(2,1)S(1)}, u32[]{:S(2)}, u32[]{:S(2)}) collective-permute-start(bf16[8,128,256]{2,1,0:T(8,128)(2,1)S(1)} %constant_dynamic-update-slice_fusion.refs_0_), channel_id=1, source_target_pairs={{0,32},{32,0},{1,33},{33,1},{2,34},{34,2},{3,35},{35,3},{4,36},{36... | collective-permute-start | bytes 1572872 | tf_op jit(solution)/shard_map/ppermute | solution.py:201
  37.7 22.8 %all-to-all-start.1 = ((bf16[16,128,256]{2,1,0:T(8,128)(2,1)}), bf16[16,128,256]{2,1,0:T(8,128)(2,1)S(1)}, u32[]{:S(2)}, u32[]{:S(2)}) async-start(bf16[16,128,256]{2,1,0:T(8,128)(2,1)} %get-tuple-element.22), calls=%async_computation.1 | async-start | bytes 2097152 | tf_op jit(solution)/shard_map/all_to_all | solution.py:226
  45.2 38.0 %copy-start = (bf16[256,256]{1,0:T(8,128)(2,1)S(1)}, bf16[256,256]{1,0:T(8,128)(2,1)}, u32[]{:S(2)}) copy-start(bf16[256,256]{1,0:T(8,128)(2,1)} %weight_ref.1) | copy-start | bytes 393220
  45.2 38.0 %copy-start.1 = (f32[256]{0:T(256)S(1)}, f32[256]{0:T(256)}, u32[]{:S(2)}) copy-start(f32[256]{0:T(256)} %param.11) | copy-start | bytes 3076
  60.5 20.4 %all-to-all-start = ((bf16[16,128,256]{2,1,0:T(8,128)(2,1)}), bf16[16,128,256]{2,1,0:T(8,128)(2,1)S(1)}, u32[]{:S(2)}, u32[]{:S(2)}) async-start(bf16[16,128,256]{2,1,0:T(8,128)(2,1)} %near_terms.1), calls=%async_computation | async-start | bytes 2097152 | tf_op jit(solution)/shard_map/all_to_all | solution.py:227
  67.0 16.2 %collective-permute-start.7 = (bf16[128,256]{1,0:T(8,128)(2,1)S(1)}, bf16[128,256]{1,0:T(8,128)(2,1)S(1)}, u32[]{:S(2)}, u32[]{:S(2)}) collective-permute-start(bf16[128,256]{1,0:T(8,128)(2,1)S(1)} %send.1), channel_id=1, source_target_pairs={{0,1},{1,0},{2,3},{3,2},{4,5},{5,4},{6,7},{7,6},{8,9},{9,8},{10,11... | collective-permute-start | bytes 196616 | tf_op jit(solution)/shard_map/ppermute | solution.py:229

commit v14 on v12

--- a/solution.py
+++ b/solution.py
@@ -160,16 +160,19 @@
     out_ref[...] = total([parts_ref[k] for k in range(X * Y)]).astype(jnp.bfloat16)
 
 
-def finish_kernel(parts_ref, other_ref, weight_ref, bias_ref, out_ref):
-    summed = total([parts_ref[k] for k in range(X * Y)]) + other_ref[...].astype(
-        jnp.float32
-    )
-    hidden = jnp.dot(
-        summed.astype(jnp.bfloat16),
-        weight_ref[...],
-        preferred_element_type=jnp.float32,
-    )
-    out_ref[...] = jnp.maximum(hidden + bias_ref[...], 0.0).astype(jnp.bfloat16)
+def near_hidden_kernel(parts_ref, weight_ref, bias_ref, out_ref):
+    summed = total([parts_ref[k] for k in range(X * Y)]).astype(jnp.bfloat16)
+    out_ref[...] = (
+        jnp.dot(summed, weight_ref[...], preferred_element_type=jnp.float32)
+        + bias_ref[...]
+    )
+
+
+def finish_kernel(other_ref, hidden_ref, weight_ref, out_ref):
+    hidden = hidden_ref[...] + jnp.dot(
+        other_ref[...], weight_ref[...], preferred_element_type=jnp.float32
+    )
+    out_ref[...] = jnp.maximum(hidden, 0.0).astype(jnp.bfloat16)
 
 
 def shard_table(block_col, row_count):
@@ -227,12 +230,15 @@
     near_parts = lax.all_to_all(near_terms, ("x", "y"), 0, 0)
     send = whole(send_kernel, [far_parts], one, "send", (0, 1 << 20))
     other = lax.ppermute(send, "zh", [(0, 1), (1, 0)])
+    hidden = whole(
+        near_hidden_kernel,
+        [near_parts, weight, out_bias[None]],
+        jax.ShapeDtypeStruct((BS, F), jnp.float32),
+        "near_hidden",
+        (2 * BS * F * F, 2 << 20),
+    )
     return whole(
-        finish_kernel,
-        [near_parts, other, weight, out_bias[None]],
-        one,
-        "finish",
-        (2 * BS * F * F, 2 << 20),
+        finish_kernel, [other, hidden, weight], one, "finish", (2 * BS * F * F, 1 << 19)
     )
 
 

time: 83.9 us -> 83.7 us (level)
    pallas_call x4 -> x5, Pallas kernels: 3.19 us -> 3.35 us  [whole(): pl.pallas_call(kernel, in_specs=specs or [VMEM] * len(ins), out_specs=out...]
where the time goes in v14:
time: 83.7 us; the launch traced here: 83.1 us
  starting transfers between devices  55.1 us (66%)
  waiting for transfers between devices  15.4 us (18%)
  Pallas kernels  11.3 us (14%)
  local copies, waits for them, and re-layouts  0.98 us (1%)
    ppermute x5, starting transfers between devices, hop(): return lax.ppermute(value, 'zl', [(z, z ^ bit) for z in range(ZL)])  25.6 us
    ppermute x1, starting transfers between devices, local(): other = lax.ppermute(send, 'zh', [(0, 1), (1, 0)])  13.8 us
    all_to_all x1, waiting for transfers between devices, local(): far_parts = lax.all_to_all(far_terms, ('x', 'y'), 0, 0)  10.4 us
    all_to_all x1, starting transfers between devices, local(): far_parts = lax.all_to_all(far_terms, ('x', 'y'), 0, 0)  7.49 us
    all_to_all x1, starting transfers between devices, local(): near_parts = lax.all_to_all(near_terms, ('x', 'y'), 0, 0)  6.35 us
    pallas_call x1, Pallas kernels, near_half(): pl.pallas_call(near_kernel, grid_spec=pltpu.PrefetchScalarGridSpec(num_sc...  4.84 us
    pallas_call x5, Pallas kernels, whole(): pl.pallas_call(kernel, in_specs=specs or [VMEM] * len(ins), out_specs=out...  3.35 us
    pallas_call x1, Pallas kernels, far_lhs_rows(): pl.pallas_call(far_lhs_kernel, grid_spec=pltpu.PrefetchScalarGridSpec(num...  3.11 us
  transfers between devices with their start and end apart: 9, of which 7 were waited for; matrix products, arithmetic and copies ran while one was open for 0% of the time, Pallas kernels for 10%

profile of v14, /device:TPU:2, one launch (start us, length us, event | category | flops | bytes accessed | tf_op | source)
XLA Modules:
  0.0 83.1 jit_solution(7700450827752577984)
XLA Ops:
  0.0 9.1 %collective-permute-start = (bf16[1,128,256]{2,1,0:T(8,128)(2,1)}, bf16[1,128,256]{2,1,0:T(8,128)(2,1)S(1)}, u32[]{:S(2)}, u32[]{:S(2)}) collective-permute-start(bf16[1,128,256]{2,1,0:T(8,128)(2,1)} %bitcast.8), channel_id=1, source_target_pairs={{0,256},{64,320},{128,384},{192,448},{256,0},{320,64},{384,128},{4... | collective-permute-start | bytes 196616 | tf_op jit(solution)/shard_map/ppermute | solution.py:201
  9.1 0.8 %copy-done.2 = bf16[128,256]{1,0:T(8,128)(2,1)S(1)} copy-done((bf16[128,256]{1,0:T(8,128)(2,1)S(1)}, bf16[128,256]{1,0:T(8,128)(2,1)}, u32[]{:S(2)}) %copy-start.2) | copy-done | bytes 65560
  10.0 5.3 %collective-permute-start.1 = (bf16[1,128,256]{2,1,0:T(8,128)(2,1)S(1)}, bf16[1,128,256]{2,1,0:T(8,128)(2,1)S(1)}, u32[]{:S(2)}, u32[]{:S(2)}) collective-permute-start(bf16[1,128,256]{2,1,0:T(8,128)(2,1)S(1)} %own.1), channel_id=1, source_target_pairs={{0,128},{64,192},{128,0},{192,64},{256,384},{320,448},{384,256},{4... | collective-permute-start | bytes 196616 | tf_op jit(solution)/shard_map/ppermute | solution.py:201
  15.3 0.1 pad.5.clone
  15.4 0.3 collective-permute-done
  15.7 2.4 %collective-permute-start.2 = (bf16[1,128,256]{2,1,0:T(8,128)(2,1)S(1)}, bf16[1,128,256]{2,1,0:T(8,128)(2,1)S(1)}, u32[]{:S(2)}, u32[]{:S(2)}) collective-permute-start(bf16[1,128,256]{2,1,0:T(8,128)(2,1)S(1)} %collective-permute-done), channel_id=1, source_target_pairs={{0,128},{64,192},{128,0},{192,64},{256,384},{320,448},{384,256},{4... | collective-permute-start | bytes 196616 | tf_op jit(solution)/shard_map/ppermute | solution.py:201
  18.1 4.5 %collective-permute-start.4 = (bf16[1,128,256]{2,1,0:T(8,128)(2,1)S(1)}, bf16[1,128,256]{2,1,0:T(8,128)(2,1)S(1)}, u32[]{:S(2)}, u32[]{:S(2)}) collective-permute-start(bf16[1,128,256]{2,1,0:T(8,128)(2,1)S(1)} %own.1), channel_id=1, source_target_pairs={{0,64},{64,0},{128,192},{192,128},{256,320},{320,256},{384,448},{4... | collective-permute-start | bytes 196616 | tf_op jit(solution)/shard_map/ppermute | solution.py:201
  22.6 0.2 collective-permute-done.2
  22.9 4.3 %collective-permute-start.3 = (bf16[3,128,256]{2,1,0:T(8,128)(2,1)S(1)}, bf16[3,128,256]{2,1,0:T(8,128)(2,1)S(1)}, u32[]{:S(2)}, u32[]{:S(2)}) collective-permute-start(bf16[3,128,256]{2,1,0:T(8,128)(2,1)S(1)} %pad_maximum_fusion), channel_id=1, source_target_pairs={{0,64},{64,0},{128,192},{192,128},{256,320},{320,256},{384,448},{4... | collective-permute-start | bytes 589832 | tf_op jit(solution)/shard_map/ppermute | solution.py:201
  27.3 3.1 %far_lhs.1.lhs_ref = bf16[16,128,512]{2,1,0:T(8,128)(2,1)S(1)} custom-call(s32[6,32]{1,0:T(8,128)S(1)} %add_add_fusion.table_ref, bf16[16,2,4,128,128]{4,3,2,1,0:T(8,128)(2,1)} %bitcast.10), custom_call_target="tpu_custom_call" | custom-call | bytes 4194304 | tf_op jit(solution)/shard_map/far_lhs/pallas_call | solution.py:73
  30.4 0.4 collective-permute-done.3
  30.9 1.9 %collective-permute-start.5 = (bf16[8,128,256]{2,1,0:T(8,128)(2,1)S(1)}, bf16[8,128,256]{2,1,0:T(8,128)(2,1)S(1)}, u32[]{:S(2)}, u32[]{:S(2)}) collective-permute-start(bf16[8,128,256]{2,1,0:T(8,128)(2,1)S(1)} %constant_dynamic-update-slice_fusion.refs_0_), channel_id=1, source_target_pairs={{0,32},{32,0},{1,33},{33,1},{2,34},{34,2},{3,35},{35,3},{4,36},{36... | collective-permute-start | bytes 1572872 | tf_op jit(solution)/shard_map/ppermute | solution.py:204
  32.8 1.9 %collective-permute-done.5.refs_1_ = bf16[8,128,256]{2,1,0:T(8,128)(2,1)S(1)} collective-permute-done((bf16[8,128,256]{2,1,0:T(8,128)(2,1)S(1)}, bf16[8,128,256]{2,1,0:T(8,128)(2,1)S(1)}, u32[]{:S(2)}, u32[]{:S(2)}) %collective-permute-start.5) | collective-permute-done | bytes 524320 | tf_op jit(solution)/shard_map/ppermute | solution.py:204
  34.7 2.1 %far_terms.1 = (bf16[16,128,256]{2,1,0:T(8,128)(2,1)S(1)}, bf16[16,128,256]{2,1,0:T(8,128)(2,1)}) custom-call(s32[6,32]{1,0:T(8,128)S(1)} %add_add_fusion.table_ref, bf16[16,128,512]{2,1,0:T(8,128)(2,1)S(1)} %far_lhs.1.lhs_ref, bf16[8,128,256]{2,1,0:T(8,128)(2,1)S(1)} %constant_dynamic-update-slice_fusion.refs_0_, ...), custom_call_target="tpu_custom_call" | custom-call | flops 536870912 | bytes 4194304 | tf_op jit(solution)/shard_map/far_terms/pallas_call | solution.py:28
  36.8 7.5 %all-to-all-start = ((bf16[16,128,256]{2,1,0:T(8,128)(2,1)}), bf16[16,128,256]{2,1,0:T(8,128)(2,1)S(1)}, u32[]{:S(2)}, u32[]{:S(2)}) async-start(bf16[16,128,256]{2,1,0:T(8,128)(2,1)} %get-tuple-element.21), calls=%async_computation | async-start | bytes 2097152 | tf_op jit(solution)/shard_map/all_to_all | solution.py:229
  44.3 4.8 %near_terms.1 = bf16[16,128,256]{2,1,0:T(8,128)(2,1)} custom-call(s32[6,32]{1,0:T(8,128)S(1)} %add_add_fusion.table_ref, bf16[16,2,4,128,128]{4,3,2,1,0:T(8,128)(2,1)} %bitcast.11, bf16[16,128,256]{2,1,0:T(8,128)(2,1)S(1)} %get-tuple-element.22.stripe_ref), custom_call_target="tpu_custom_call" | custom-call | flops 536870912 | bytes 4194304 | tf_op jit(solution)/shard_map/near_terms/pallas_call | solution.py:127
  49.2 10.4 %all-to-all-done.parts_ref = bf16[16,128,256]{2,1,0:T(8,128)(2,1)S(1)} async-done(((bf16[16,128,256]{2,1,0:T(8,128)(2,1)}), bf16[16,128,256]{2,1,0:T(8,128)(2,1)S(1)}, u32[]{:S(2)}, u32[]{:S(2)}) %all-to-all-start) | async-done | bytes 1048608 | tf_op jit(solution)/shard_map/all_to_all | solution.py:229
  59.6 6.4 %all-to-all-start.1 = ((bf16[16,128,256]{2,1,0:T(8,128)(2,1)}), bf16[16,128,256]{2,1,0:T(8,128)(2,1)S(1)}, u32[]{:S(2)}, u32[]{:S(2)}) async-start(bf16[16,128,256]{2,1,0:T(8,128)(2,1)} %near_terms.1), calls=%async_computation.1 | async-start | bytes 2097152 | tf_op jit(solution)/shard_map/all_to_all | solution.py:230
  66.0 0.1 send.1
  66.1 13.8 %collective-permute-start.6 = (bf16[128,256]{1,0:T(8,128)(2,1)S(1)}, bf16[128,256]{1,0:T(8,128)(2,1)S(1)}, u32[]{:S(2)}, u32[]{:S(2)}) collective-permute-start(bf16[128,256]{1,0:T(8,128)(2,1)S(1)} %send.1), channel_id=1, source_target_pairs={{0,1},{1,0},{2,3},{3,2},{4,5},{5,4},{6,7},{7,6},{8,9},{9,8},{10,11... | collective-permute-start | bytes 196616 | tf_op jit(solution)/shard_map/ppermute | solution.py:232
  79.9 0.1 all-to-all-done.1.parts_ref
  80.0 0.3 near_hidden.1.hidden_ref
  80.2 2.1 %collective-permute-done.6.other_ref = bf16[128,256]{1,0:T(8,128)(2,1)S(1)} collective-permute-done((bf16[128,256]{1,0:T(8,128)(2,1)S(1)}, bf16[128,256]{1,0:T(8,128)(2,1)S(1)}, u32[]{:S(2)}, u32[]{:S(2)}) %collective-permute-start.6) | collective-permute-done | bytes 65568 | tf_op jit(solution)/shard_map/ppermute | solution.py:232
  82.3 0.8 finish.1
  (21 shorter events, 0.2 us)
Async XLA Ops:
  0.0 15.7 %collective-permute-start = (bf16[1,128,256]{2,1,0:T(8,128)(2,1)}, bf16[1,128,256]{2,1,0:T(8,128)(2,1)S(1)}, u32[]{:S(2)}, u32[]{:S(2)}) collective-permute-start(bf16[1,128,256]{2,1,0:T(8,128)(2,1)} %bitcast.8), channel_id=1, source_target_pairs={{0,256},{64,320},{128,384},{192,448},{256,0},{320,64},{384,128},{4... | collective-permute-start | bytes 196616 | tf_op jit(solution)/shard_map/ppermute | solution.py:201
  9.1 0.9 %copy-start.2 = (bf16[128,256]{1,0:T(8,128)(2,1)S(1)}, bf16[128,256]{1,0:T(8,128)(2,1)}, u32[]{:S(2)}) copy-start(bf16[128,256]{1,0:T(8,128)(2,1)} %param.6) | copy-start | bytes 196612
  9.9 5.4 %copy-start.3 = (s32[32,4]{0,1:T(4,128)S(1)}, s32[32,4]{0,1:T(4,128)}, u32[]{:S(2)}) copy-start(s32[32,4]{0,1:T(4,128)} %param.8) | copy-start | bytes 1540
  9.9 5.4 %copy-start.4 = (s32[32,1]{0,1:T(1,128)S(1)}, s32[32,1]{0,1:T(1,128)}, u32[]{:S(2)}) copy-start(s32[32,1]{0,1:T(1,128)} %param.9) | copy-start | bytes 388
  10.0 12.7 %collective-permute-start.1 = (bf16[1,128,256]{2,1,0:T(8,128)(2,1)S(1)}, bf16[1,128,256]{2,1,0:T(8,128)(2,1)S(1)}, u32[]{:S(2)}, u32[]{:S(2)}) collective-permute-start(bf16[1,128,256]{2,1,0:T(8,128)(2,1)S(1)} %own.1), channel_id=1, source_target_pairs={{0,128},{64,192},{128,0},{192,64},{256,384},{320,448},{384,256},{4... | collective-permute-start | bytes 196616 | tf_op jit(solution)/shard_map/ppermute | solution.py:201
  15.7 7.2 %collective-permute-start.2 = (bf16[1,128,256]{2,1,0:T(8,128)(2,1)S(1)}, bf16[1,128,256]{2,1,0:T(8,128)(2,1)S(1)}, u32[]{:S(2)}, u32[]{:S(2)}) collective-permute-start(bf16[1,128,256]{2,1,0:T(8,128)(2,1)S(1)} %collective-permute-done), channel_id=1, source_target_pairs={{0,128},{64,192},{128,0},{192,64},{256,384},{320,448},{384,256},{4... | collective-permute-start | bytes 196616 | tf_op jit(solution)/shard_map/ppermute | solution.py:201
  18.1 9.1 %collective-permute-start.4 = (bf16[1,128,256]{2,1,0:T(8,128)(2,1)S(1)}, bf16[1,128,256]{2,1,0:T(8,128)(2,1)S(1)}, u32[]{:S(2)}, u32[]{:S(2)}) collective-permute-start(bf16[1,128,256]{2,1,0:T(8,128)(2,1)S(1)} %own.1), channel_id=1, source_target_pairs={{0,64},{64,0},{128,192},{192,128},{256,320},{320,256},{384,448},{4... | collective-permute-start | bytes 196616 | tf_op jit(solution)/shard_map/ppermute | solution.py:201
  22.9 8.0 %collective-permute-start.3 = (bf16[3,128,256]{2,1,0:T(8,128)(2,1)S(1)}, bf16[3,128,256]{2,1,0:T(8,128)(2,1)S(1)}, u32[]{:S(2)}, u32[]{:S(2)}) collective-permute-start(bf16[3,128,256]{2,1,0:T(8,128)(2,1)S(1)} %pad_maximum_fusion), channel_id=1, source_target_pairs={{0,64},{64,0},{128,192},{192,128},{256,320},{320,256},{384,448},{4... | collective-permute-start | bytes 589832 | tf_op jit(solution)/shard_map/ppermute | solution.py:201
  30.9 3.8 %collective-permute-start.5 = (bf16[8,128,256]{2,1,0:T(8,128)(2,1)S(1)}, bf16[8,128,256]{2,1,0:T(8,128)(2,1)S(1)}, u32[]{:S(2)}, u32[]{:S(2)}) collective-permute-start(bf16[8,128,256]{2,1,0:T(8,128)(2,1)S(1)} %constant_dynamic-update-slice_fusion.refs_0_), channel_id=1, source_target_pairs={{0,32},{32,0},{1,33},{33,1},{2,34},{34,2},{3,35},{35,3},{4,36},{36... | collective-permute-start | bytes 1572872 | tf_op jit(solution)/shard_map/ppermute | solution.py:204
  36.8 22.8 %all-to-all-start = ((bf16[16,128,256]{2,1,0:T(8,128)(2,1)}), bf16[16,128,256]{2,1,0:T(8,128)(2,1)S(1)}, u32[]{:S(2)}, u32[]{:S(2)}) async-start(bf16[16,128,256]{2,1,0:T(8,128)(2,1)} %get-tuple-element.21), calls=%async_computation | async-start | bytes 2097152 | tf_op jit(solution)/shard_map/all_to_all | solution.py:229
  44.3 35.6 %copy-start = (bf16[256,256]{1,0:T(8,128)(2,1)S(1)}, bf16[256,256]{1,0:T(8,128)(2,1)}, u32[]{:S(2)}) copy-start(bf16[256,256]{1,0:T(8,128)(2,1)} %weight_ref.3) | copy-start | bytes 393220
  44.3 35.6 %copy-start.1 = (f32[256]{0:T(256)S(1)}, f32[256]{0:T(256)}, u32[]{:S(2)}) copy-start(f32[256]{0:T(256)} %param.11) | copy-start | bytes 3076
  59.6 20.3 %all-to-all-start.1 = ((bf16[16,128,256]{2,1,0:T(8,128)(2,1)}), bf16[16,128,256]{2,1,0:T(8,128)(2,1)S(1)}, u32[]{:S(2)}, u32[]{:S(2)}) async-start(bf16[16,128,256]{2,1,0:T(8,128)(2,1)} %near_terms.1), calls=%async_computation.1 | async-start | bytes 2097152 | tf_op jit(solution)/shard_map/all_to_all | solution.py:230
  66.1 16.2 %collective-permute-start.6 = (bf16[128,256]{1,0:T(8,128)(2,1)S(1)}, bf16[128,256]{1,0:T(8,128)(2,1)S(1)}, u32[]{:S(2)}, u32[]{:S(2)}) collective-permute-start(bf16[128,256]{1,0:T(8,128)(2,1)S(1)} %send.1), channel_id=1, source_target_pairs={{0,1},{1,0},{2,3},{3,2},{4,5},{5,4},{6,7},{7,6},{8,9},{9,8},{10,11... | collective-permute-start | bytes 196616 | tf_op jit(solution)/shard_map/ppermute | solution.py:232
